TPU v7x, 512 devices: a whole 4x8x8 slice. The times are simulated.
512 devices in a mesh: layer: 32 (over y, x), dp: 16 (over z, core).
Axes of the slice: x: 4, y: 8, z: 8, core: 2. Of those that a mesh axis runs over, the one named last changes fastest.
Arguments:
- states: bfloat16 [64, 16, 128, 1024], P('layer', 'dp'), may hold values from -6 to 6
- filters: bfloat16 [64, 128, 1152], P('layer'), may hold values from -0.1875 to 0.1875
- guess_adjoint: bfloat16 [64, 16, 128, 1024], P('layer', 'dp'), may hold values from -4 to 4
- terminal: bfloat16 [16, 128, 1024], P('dp'), may hold values from -6 to 6
Outputs:
- adjoint: bfloat16 [64, 16, 128, 1024], P('layer', 'dp')
- filter_grad: float32 [64, 128, 1152], P('layer', 'dp')
All inputs are finite; a program needn't handle non-finite values.
Results may differ from a plain program's by a relative error of at most 0.0057.
Values may be sent and summed in bfloat16 or wider, within the bound.
No kernel may reach another device: no remote copies, remote signals or barrier semaphores. Data moves between devices by JAX's collectives and lax.ppermute only.
A program may use at most 64 MiB of HBM per device.

v0:
```python
import math

import jax
import jax.numpy as jnp
from jax import lax
from jax.sharding import PartitionSpec as P

step_size = 0.0625


def shifted(shard, axis, by):
    devices = lax.axis_size(axis)
    pairs = [(i, i + by) for i in range(devices) if 0 <= i + by < devices]
    return lax.ppermute(shard, axis, pairs)


def shifted_stack(in_field):
    images, channels, pixels = in_field.shape
    grid_side = math.isqrt(pixels)
    grid_field = in_field.reshape(images, channels, grid_side, grid_side)
    padded = jnp.pad(grid_field, ((0, 0), (0, 0), (1, 1), (1, 1)))
    pieces = []
    for row_off in (-1, 0, 1):
        for col_off in (-1, 0, 1):
            pieces.append(
                padded[
                    :,
                    :,
                    1 - row_off : 1 - row_off + grid_side,
                    1 - col_off : 1 - col_off + grid_side,
                ]
            )
    return jnp.stack(pieces, axis=1).reshape(images, 9 * channels, pixels)


def adjoint_step(carried, stacked, layer_state, kernel):
    backward = jnp.einsum("ck,bkp->bcp", kernel, stacked, preferred_element_type=jnp.float32)
    slope_term = 1.0 - jnp.tanh(layer_state.astype(jnp.float32)) ** 2
    return (1.0 - step_size) * carried.astype(jnp.float32) + step_size * slope_term * backward


def layer_gradient(layer_state, stacked):
    activation = jnp.tanh(layer_state.astype(jnp.float32)).astype(jnp.bfloat16)
    return step_size * jnp.einsum(
        "bcp,bkp->ck", activation, stacked, preferred_element_type=jnp.float32
    )


def pool_field(in_field):
    images, channels, pixels = in_field.shape
    half_side = math.isqrt(pixels) // 2
    grid_field = in_field.reshape(images, channels, half_side, 2, half_side, 2)
    return jnp.mean(grid_field, axis=(3, 5)).reshape(images, channels, half_side * half_side)


def spread_field(coarse):
    images, channels, cells = coarse.shape
    half_side = math.isqrt(cells)
    grid_field = coarse.reshape(images, channels, half_side, 1, half_side, 1)
    grid_field = jnp.broadcast_to(grid_field, (images, channels, half_side, 2, half_side, 2))
    return grid_field.reshape(images, channels, 4 * cells)


def coarse_matrix(kernel, window_depth):
    channels = kernel.shape[0]
    summed = jnp.sum(kernel.astype(jnp.float32).reshape(channels, 9, channels), axis=1)
    base_matrix = (1.0 - step_size) * jnp.eye(channels, dtype=jnp.float32) + step_size * summed

    def times_base(count_idx, product):
        return jnp.dot(product, base_matrix, precision=lax.Precision.HIGHEST)

    return lax.fori_loop(0, window_depth - 1, times_base, base_matrix)


def apply_matrix(matrix, in_field):
    return jnp.einsum("ij,bjp->bip", matrix, in_field, precision=lax.Precision.HIGHEST)


def fine_sweep(top_adjoint, layer_states, kernels):

    def fine_relax_layer(carried, layer_pair):
        layer_state, kernel = layer_pair
        fresh_adjoint = adjoint_step(carried, shifted_stack(carried), layer_state, kernel).astype(
            jnp.bfloat16
        )
        return (fresh_adjoint, None)

    carried, unused = lax.scan(
        fine_relax_layer, top_adjoint, (layer_states[1:], kernels[1:]), reverse=True
    )
    return carried


def corrected_sweep(top_adjoint, layer_states, kernels, c_point):

    def corrected_relax_layer(carried, layer_pair):
        layer_state, kernel = layer_pair
        stacked = shifted_stack(carried)
        fresh_adjoint = adjoint_step(carried, stacked, layer_state, kernel).astype(jnp.bfloat16)
        return (fresh_adjoint, (fresh_adjoint, layer_gradient(layer_state, stacked)))

    carried, outputs = lax.scan(
        corrected_relax_layer, top_adjoint, (layer_states[1:], kernels[1:]), reverse=True
    )
    fresh_all, gradients = outputs
    first_grad = layer_gradient(layer_states[0], shifted_stack(carried))
    adjoint_block = jnp.concatenate([c_point[None], fresh_all], axis=0)
    grad_block = jnp.concatenate([first_grad[None], gradients], axis=0)
    return (adjoint_block, grad_block)


def per_device(states, filters, guess_adjoint, terminal):
    blocks = lax.axis_size("layer")
    block_index = lax.axis_index("layer")
    window_depth = states.shape[0]
    above_guess = shifted(guess_adjoint[0], "layer", -1)
    top_adjoint = jnp.where(block_index == blocks - 1, terminal, above_guess)
    below_adjoint = fine_sweep(top_adjoint, states, filters)
    residual = adjoint_step(
        below_adjoint, shifted_stack(below_adjoint), states[0], filters[0]
    ) - guess_adjoint[0].astype(jnp.float32)
    coarse_residual = pool_field(residual)
    matrix = coarse_matrix(filters[0], window_depth)

    def chain_turn(turn_count, chain_carry):
        own_error, received = chain_carry
        received = shifted(own_error, "layer", -1)
        return (apply_matrix(matrix, received) + coarse_residual, received)

    own_error, upper_error = lax.fori_loop(
        0, blocks, chain_turn, (coarse_residual, jnp.zeros_like(coarse_residual))
    )
    c_point = (guess_adjoint[0].astype(jnp.float32) + spread_field(own_error)).astype(jnp.bfloat16)
    new_top = (top_adjoint.astype(jnp.float32) + spread_field(upper_error)).astype(jnp.bfloat16)
    adjoint_block, grad_block = corrected_sweep(new_top, states, filters, c_point)
    filter_grad = lax.psum_scatter(grad_block, "dp", scatter_dimension=1, tiled=True)
    return (adjoint_block, filter_grad)


def solution(mesh):
    return jax.shard_map(
        per_device,
        mesh=mesh,
        in_specs=(
            P("layer", "dp", None, None),
            P("layer", None, None),
            P("layer", "dp", None, None),
            P("dp", None, None),
        ),
        out_specs=(P("layer", "dp", None, None), P("layer", "dp", None)),
        check_vma=False,
    )
```

profile of v0, /device:TPU:1, one launch (start us, length us, event | category | flops | bytes accessed | tf_op | source)
XLA Modules:
  0.0 527.7 jit_solution(5351318849520853384)
XLA Ops:
  25.8 274.8 %while.2 = (s32[]{:T(128)}, f32[1,128,256]{1,2,0:T(8,128)S(1)}, f32[1,128,256]{1,2,0:T(8,128)}, f32[128,128]{1,0:T(8,128)S(1)}, f32[1,128,256]{1,2,0:T(8,128)S(1)}, /*index=5*/s32[]{:T(128)}) while((s32[]{:T(128)}, f32[1,128,256]{1,2,0:T(8,128)S(1)}, f32[1,128,256]{1,2,0:T(8,128)}, f32[128,128]{1,0:T(8,128)S(1)}, ...), condition=%wide.region_3.4_spmd, body=%wide.region_2.3_spmd.sunk | while | flops 50364416 | bytes 1507465 | solution.py:130
  27.3 6.4 %collective-permute-done = f32[1,128,256]{1,2,0:T(8,128)S(1)} collective-permute-done((f32[1,128,256]{1,2,0:T(8,128)S(1)}, f32[1,128,256]{1,2,0:T(8,128)S(1)}, u32[]{:S(2)}, u32[]{:S(2)}) %collective-permute-start) | collective-permute-done | bytes 131104 | tf_op jit(solution)/shard_map/while/body/eval_jaxpr/ppermute | solution.py:14
  43.0 6.2 %collective-permute-done = f32[1,128,256]{1,2,0:T(8,128)S(1)} collective-permute-done((f32[1,128,256]{1,2,0:T(8,128)S(1)}, f32[1,128,256]{1,2,0:T(8,128)S(1)}, u32[]{:S(2)}, u32[]{:S(2)}) %collective-permute-start) | collective-permute-done | bytes 131104 | tf_op jit(solution)/shard_map/while/body/eval_jaxpr/ppermute | solution.py:14
  51.1 6.4 %collective-permute-done = f32[1,128,256]{1,2,0:T(8,128)S(1)} collective-permute-done((f32[1,128,256]{1,2,0:T(8,128)S(1)}, f32[1,128,256]{1,2,0:T(8,128)S(1)}, u32[]{:S(2)}, u32[]{:S(2)}) %collective-permute-start) | collective-permute-done | bytes 131104 | tf_op jit(solution)/shard_map/while/body/eval_jaxpr/ppermute | solution.py:14
  59.4 6.5 %collective-permute-done = f32[1,128,256]{1,2,0:T(8,128)S(1)} collective-permute-done((f32[1,128,256]{1,2,0:T(8,128)S(1)}, f32[1,128,256]{1,2,0:T(8,128)S(1)}, u32[]{:S(2)}, u32[]{:S(2)}) %collective-permute-start) | collective-permute-done | bytes 131104 | tf_op jit(solution)/shard_map/while/body/eval_jaxpr/ppermute | solution.py:14
  67.9 6.5 %collective-permute-done = f32[1,128,256]{1,2,0:T(8,128)S(1)} collective-permute-done((f32[1,128,256]{1,2,0:T(8,128)S(1)}, f32[1,128,256]{1,2,0:T(8,128)S(1)}, u32[]{:S(2)}, u32[]{:S(2)}) %collective-permute-start) | collective-permute-done | bytes 131104 | tf_op jit(solution)/shard_map/while/body/eval_jaxpr/ppermute | solution.py:14
  76.4 6.5 %collective-permute-done = f32[1,128,256]{1,2,0:T(8,128)S(1)} collective-permute-done((f32[1,128,256]{1,2,0:T(8,128)S(1)}, f32[1,128,256]{1,2,0:T(8,128)S(1)}, u32[]{:S(2)}, u32[]{:S(2)}) %collective-permute-start) | collective-permute-done | bytes 131104 | tf_op jit(solution)/shard_map/while/body/eval_jaxpr/ppermute | solution.py:14
  84.8 6.8 %collective-permute-done = f32[1,128,256]{1,2,0:T(8,128)S(1)} collective-permute-done((f32[1,128,256]{1,2,0:T(8,128)S(1)}, f32[1,128,256]{1,2,0:T(8,128)S(1)}, u32[]{:S(2)}, u32[]{:S(2)}) %collective-permute-start) | collective-permute-done | bytes 131104 | tf_op jit(solution)/shard_map/while/body/eval_jaxpr/ppermute | solution.py:14
  93.5 8.0 %collective-permute-done = f32[1,128,256]{1,2,0:T(8,128)S(1)} collective-permute-done((f32[1,128,256]{1,2,0:T(8,128)S(1)}, f32[1,128,256]{1,2,0:T(8,128)S(1)}, u32[]{:S(2)}, u32[]{:S(2)}) %collective-permute-start) | collective-permute-done | bytes 131104 | tf_op jit(solution)/shard_map/while/body/eval_jaxpr/ppermute | solution.py:14
  103.4 7.2 %collective-permute-done = f32[1,128,256]{1,2,0:T(8,128)S(1)} collective-permute-done((f32[1,128,256]{1,2,0:T(8,128)S(1)}, f32[1,128,256]{1,2,0:T(8,128)S(1)}, u32[]{:S(2)}, u32[]{:S(2)}) %collective-permute-start) | collective-permute-done | bytes 131104 | tf_op jit(solution)/shard_map/while/body/eval_jaxpr/ppermute | solution.py:14
  120.1 6.2 %collective-permute-done = f32[1,128,256]{1,2,0:T(8,128)S(1)} collective-permute-done((f32[1,128,256]{1,2,0:T(8,128)S(1)}, f32[1,128,256]{1,2,0:T(8,128)S(1)}, u32[]{:S(2)}, u32[]{:S(2)}) %collective-permute-start) | collective-permute-done | bytes 131104 | tf_op jit(solution)/shard_map/while/body/eval_jaxpr/ppermute | solution.py:14
  128.3 6.5 %collective-permute-done = f32[1,128,256]{1,2,0:T(8,128)S(1)} collective-permute-done((f32[1,128,256]{1,2,0:T(8,128)S(1)}, f32[1,128,256]{1,2,0:T(8,128)S(1)}, u32[]{:S(2)}, u32[]{:S(2)}) %collective-permute-start) | collective-permute-done | bytes 131104 | tf_op jit(solution)/shard_map/while/body/eval_jaxpr/ppermute | solution.py:14
  136.7 6.5 %collective-permute-done = f32[1,128,256]{1,2,0:T(8,128)S(1)} collective-permute-done((f32[1,128,256]{1,2,0:T(8,128)S(1)}, f32[1,128,256]{1,2,0:T(8,128)S(1)}, u32[]{:S(2)}, u32[]{:S(2)}) %collective-permute-start) | collective-permute-done | bytes 131104 | tf_op jit(solution)/shard_map/while/body/eval_jaxpr/ppermute | solution.py:14
  145.2 6.5 %collective-permute-done = f32[1,128,256]{1,2,0:T(8,128)S(1)} collective-permute-done((f32[1,128,256]{1,2,0:T(8,128)S(1)}, f32[1,128,256]{1,2,0:T(8,128)S(1)}, u32[]{:S(2)}, u32[]{:S(2)}) %collective-permute-start) | collective-permute-done | bytes 131104 | tf_op jit(solution)/shard_map/while/body/eval_jaxpr/ppermute | solution.py:14
  153.7 6.5 %collective-permute-done = f32[1,128,256]{1,2,0:T(8,128)S(1)} collective-permute-done((f32[1,128,256]{1,2,0:T(8,128)S(1)}, f32[1,128,256]{1,2,0:T(8,128)S(1)}, u32[]{:S(2)}, u32[]{:S(2)}) %collective-permute-start) | collective-permute-done | bytes 131104 | tf_op jit(solution)/shard_map/while/body/eval_jaxpr/ppermute | solution.py:14
  162.1 7.9 %collective-permute-done = f32[1,128,256]{1,2,0:T(8,128)S(1)} collective-permute-done((f32[1,128,256]{1,2,0:T(8,128)S(1)}, f32[1,128,256]{1,2,0:T(8,128)S(1)}, u32[]{:S(2)}, u32[]{:S(2)}) %collective-permute-start) | collective-permute-done | bytes 131104 | tf_op jit(solution)/shard_map/while/body/eval_jaxpr/ppermute | solution.py:14
  172.0 8.5 %collective-permute-done = f32[1,128,256]{1,2,0:T(8,128)S(1)} collective-permute-done((f32[1,128,256]{1,2,0:T(8,128)S(1)}, f32[1,128,256]{1,2,0:T(8,128)S(1)}, u32[]{:S(2)}, u32[]{:S(2)}) %collective-permute-start) | collective-permute-done | bytes 131104 | tf_op jit(solution)/shard_map/while/body/eval_jaxpr/ppermute | solution.py:14
  182.4 6.2 %collective-permute-done = f32[1,128,256]{1,2,0:T(8,128)S(1)} collective-permute-done((f32[1,128,256]{1,2,0:T(8,128)S(1)}, f32[1,128,256]{1,2,0:T(8,128)S(1)}, u32[]{:S(2)}, u32[]{:S(2)}) %collective-permute-start) | collective-permute-done | bytes 131104 | tf_op jit(solution)/shard_map/while/body/eval_jaxpr/ppermute | solution.py:14
  190.6 6.0 %collective-permute-done = f32[1,128,256]{1,2,0:T(8,128)S(1)} collective-permute-done((f32[1,128,256]{1,2,0:T(8,128)S(1)}, f32[1,128,256]{1,2,0:T(8,128)S(1)}, u32[]{:S(2)}, u32[]{:S(2)}) %collective-permute-start) | collective-permute-done | bytes 131104 | tf_op jit(solution)/shard_map/while/body/eval_jaxpr/ppermute | solution.py:14
  198.5 6.0 %collective-permute-done = f32[1,128,256]{1,2,0:T(8,128)S(1)} collective-permute-done((f32[1,128,256]{1,2,0:T(8,128)S(1)}, f32[1,128,256]{1,2,0:T(8,128)S(1)}, u32[]{:S(2)}, u32[]{:S(2)}) %collective-permute-start) | collective-permute-done | bytes 131104 | tf_op jit(solution)/shard_map/while/body/eval_jaxpr/ppermute | solution.py:14
  206.4 6.5 %collective-permute-done = f32[1,128,256]{1,2,0:T(8,128)S(1)} collective-permute-done((f32[1,128,256]{1,2,0:T(8,128)S(1)}, f32[1,128,256]{1,2,0:T(8,128)S(1)}, u32[]{:S(2)}, u32[]{:S(2)}) %collective-permute-start) | collective-permute-done | bytes 131104 | tf_op jit(solution)/shard_map/while/body/eval_jaxpr/ppermute | solution.py:14
  214.9 6.5 %collective-permute-done = f32[1,128,256]{1,2,0:T(8,128)S(1)} collective-permute-done((f32[1,128,256]{1,2,0:T(8,128)S(1)}, f32[1,128,256]{1,2,0:T(8,128)S(1)}, u32[]{:S(2)}, u32[]{:S(2)}) %collective-permute-start) | collective-permute-done | bytes 131104 | tf_op jit(solution)/shard_map/while/body/eval_jaxpr/ppermute | solution.py:14
  223.4 6.5 %collective-permute-done = f32[1,128,256]{1,2,0:T(8,128)S(1)} collective-permute-done((f32[1,128,256]{1,2,0:T(8,128)S(1)}, f32[1,128,256]{1,2,0:T(8,128)S(1)}, u32[]{:S(2)}, u32[]{:S(2)}) %collective-permute-start) | collective-permute-done | bytes 131104 | tf_op jit(solution)/shard_map/while/body/eval_jaxpr/ppermute | solution.py:14
  231.8 6.9 %collective-permute-done = f32[1,128,256]{1,2,0:T(8,128)S(1)} collective-permute-done((f32[1,128,256]{1,2,0:T(8,128)S(1)}, f32[1,128,256]{1,2,0:T(8,128)S(1)}, u32[]{:S(2)}, u32[]{:S(2)}) %collective-permute-start) | collective-permute-done | bytes 131104 | tf_op jit(solution)/shard_map/while/body/eval_jaxpr/ppermute | solution.py:14
  240.7 8.3 %collective-permute-done = f32[1,128,256]{1,2,0:T(8,128)S(1)} collective-permute-done((f32[1,128,256]{1,2,0:T(8,128)S(1)}, f32[1,128,256]{1,2,0:T(8,128)S(1)}, u32[]{:S(2)}, u32[]{:S(2)}) %collective-permute-start) | collective-permute-done | bytes 131104 | tf_op jit(solution)/shard_map/while/body/eval_jaxpr/ppermute | solution.py:14
  251.0 7.3 %collective-permute-done = f32[1,128,256]{1,2,0:T(8,128)S(1)} collective-permute-done((f32[1,128,256]{1,2,0:T(8,128)S(1)}, f32[1,128,256]{1,2,0:T(8,128)S(1)}, u32[]{:S(2)}, u32[]{:S(2)}) %collective-permute-start) | collective-permute-done | bytes 131104 | tf_op jit(solution)/shard_map/while/body/eval_jaxpr/ppermute | solution.py:14
  260.2 6.7 %collective-permute-done = f32[1,128,256]{1,2,0:T(8,128)S(1)} collective-permute-done((f32[1,128,256]{1,2,0:T(8,128)S(1)}, f32[1,128,256]{1,2,0:T(8,128)S(1)}, u32[]{:S(2)}, u32[]{:S(2)}) %collective-permute-start) | collective-permute-done | bytes 131104 | tf_op jit(solution)/shard_map/while/body/eval_jaxpr/ppermute | solution.py:14
  268.8 5.7 %collective-permute-done = f32[1,128,256]{1,2,0:T(8,128)S(1)} collective-permute-done((f32[1,128,256]{1,2,0:T(8,128)S(1)}, f32[1,128,256]{1,2,0:T(8,128)S(1)}, u32[]{:S(2)}, u32[]{:S(2)}) %collective-permute-start) | collective-permute-done | bytes 131104 | tf_op jit(solution)/shard_map/while/body/eval_jaxpr/ppermute | solution.py:14
  276.5 6.5 %collective-permute-done = f32[1,128,256]{1,2,0:T(8,128)S(1)} collective-permute-done((f32[1,128,256]{1,2,0:T(8,128)S(1)}, f32[1,128,256]{1,2,0:T(8,128)S(1)}, u32[]{:S(2)}, u32[]{:S(2)}) %collective-permute-start) | collective-permute-done | bytes 131104 | tf_op jit(solution)/shard_map/while/body/eval_jaxpr/ppermute | solution.py:14
  285.0 6.5 %collective-permute-done = f32[1,128,256]{1,2,0:T(8,128)S(1)} collective-permute-done((f32[1,128,256]{1,2,0:T(8,128)S(1)}, f32[1,128,256]{1,2,0:T(8,128)S(1)}, u32[]{:S(2)}, u32[]{:S(2)}) %collective-permute-start) | collective-permute-done | bytes 131104 | tf_op jit(solution)/shard_map/while/body/eval_jaxpr/ppermute | solution.py:14
  293.4 6.5 %collective-permute-done = f32[1,128,256]{1,2,0:T(8,128)S(1)} collective-permute-done((f32[1,128,256]{1,2,0:T(8,128)S(1)}, f32[1,128,256]{1,2,0:T(8,128)S(1)}, u32[]{:S(2)}, u32[]{:S(2)}) %collective-permute-start) | collective-permute-done | bytes 131104 | tf_op jit(solution)/shard_map/while/body/eval_jaxpr/ppermute | solution.py:14
  317.8 201.4 %all-reduce.7.cloned.1.call-done = f32[2,128,1152]{2,0,1:T(2,128)} async-done(((f32[2,128,1152]{2,0,1:T(2,128)}), f32[2,128,1152]{2,0,1:T(2,128)}) %all-reduce.7.cloned.1.call-update) | async-done | bytes 1179664
  (210 shorter events, 109.0 us)
Async XLA Ops:
  7.2 512.1 %all-reduce.7.cloned.1.call-start = ((), (), s32[]{:S(2)}) async-start(), calls=%async_computation | async-start | bytes 2359296
  8.4 7.7 %collective-permute-start.1 = (bf16[1,128,1024]{1,2,0:T(8,128)(2,1)S(1)}, bf16[1,128,1024]{1,2,0:T(8,128)(2,1)S(1)}, u32[]{:S(2)}, u32[]{:S(2)}) collective-permute-start(bf16[1,128,1024]{1,2,0:T(8,128)(2,1)S(1)} %bitcast.322), channel_id=1, source_target_pairs={{16,0},{32,16},{48,32},{64,48},{80,64},{96,80},{112,96},{128,112},... | collective-permute-start | bytes 786440 | tf_op jit(solution)/shard_map/ppermute | solution.py:14
  26.0 7.7 %collective-permute-start = (f32[1,128,256]{1,2,0:T(8,128)S(1)}, f32[1,128,256]{1,2,0:T(8,128)S(1)}, u32[]{:S(2)}, u32[]{:S(2)}) collective-permute-start(f32[1,128,256]{1,2,0:T(8,128)S(1)} %get-tuple-element.126), channel_id=1, source_target_pairs={{16,0},{32,16},{48,32},{64,48},{80,64},{96,80},{112,96},{128,112},... | collective-permute-start | bytes 393224 | tf_op jit(solution)/shard_map/while/body/eval_jaxpr/ppermute | solution.py:14
  41.7 7.4 %collective-permute-start = (f32[1,128,256]{1,2,0:T(8,128)S(1)}, f32[1,128,256]{1,2,0:T(8,128)S(1)}, u32[]{:S(2)}, u32[]{:S(2)}) collective-permute-start(f32[1,128,256]{1,2,0:T(8,128)S(1)} %get-tuple-element.126), channel_id=1, source_target_pairs={{16,0},{32,16},{48,32},{64,48},{80,64},{96,80},{112,96},{128,112},... | collective-permute-start | bytes 393224 | tf_op jit(solution)/shard_map/while/body/eval_jaxpr/ppermute | solution.py:14
  49.8 7.7 %collective-permute-start = (f32[1,128,256]{1,2,0:T(8,128)S(1)}, f32[1,128,256]{1,2,0:T(8,128)S(1)}, u32[]{:S(2)}, u32[]{:S(2)}) collective-permute-start(f32[1,128,256]{1,2,0:T(8,128)S(1)} %get-tuple-element.126), channel_id=1, source_target_pairs={{16,0},{32,16},{48,32},{64,48},{80,64},{96,80},{112,96},{128,112},... | collective-permute-start | bytes 393224 | tf_op jit(solution)/shard_map/while/body/eval_jaxpr/ppermute | solution.py:14
  58.1 7.8 %collective-permute-start = (f32[1,128,256]{1,2,0:T(8,128)S(1)}, f32[1,128,256]{1,2,0:T(8,128)S(1)}, u32[]{:S(2)}, u32[]{:S(2)}) collective-permute-start(f32[1,128,256]{1,2,0:T(8,128)S(1)} %get-tuple-element.126), channel_id=1, source_target_pairs={{16,0},{32,16},{48,32},{64,48},{80,64},{96,80},{112,96},{128,112},... | collective-permute-start | bytes 393224 | tf_op jit(solution)/shard_map/while/body/eval_jaxpr/ppermute | solution.py:14
  66.6 7.8 %collective-permute-start = (f32[1,128,256]{1,2,0:T(8,128)S(1)}, f32[1,128,256]{1,2,0:T(8,128)S(1)}, u32[]{:S(2)}, u32[]{:S(2)}) collective-permute-start(f32[1,128,256]{1,2,0:T(8,128)S(1)} %get-tuple-element.126), channel_id=1, source_target_pairs={{16,0},{32,16},{48,32},{64,48},{80,64},{96,80},{112,96},{128,112},... | collective-permute-start | bytes 393224 | tf_op jit(solution)/shard_map/while/body/eval_jaxpr/ppermute | solution.py:14
  75.1 7.8 %collective-permute-start = (f32[1,128,256]{1,2,0:T(8,128)S(1)}, f32[1,128,256]{1,2,0:T(8,128)S(1)}, u32[]{:S(2)}, u32[]{:S(2)}) collective-permute-start(f32[1,128,256]{1,2,0:T(8,128)S(1)} %get-tuple-element.126), channel_id=1, source_target_pairs={{16,0},{32,16},{48,32},{64,48},{80,64},{96,80},{112,96},{128,112},... | collective-permute-start | bytes 393224 | tf_op jit(solution)/shard_map/while/body/eval_jaxpr/ppermute | solution.py:14
  83.5 8.0 %collective-permute-start = (f32[1,128,256]{1,2,0:T(8,128)S(1)}, f32[1,128,256]{1,2,0:T(8,128)S(1)}, u32[]{:S(2)}, u32[]{:S(2)}) collective-permute-start(f32[1,128,256]{1,2,0:T(8,128)S(1)} %get-tuple-element.126), channel_id=1, source_target_pairs={{16,0},{32,16},{48,32},{64,48},{80,64},{96,80},{112,96},{128,112},... | collective-permute-start | bytes 393224 | tf_op jit(solution)/shard_map/while/body/eval_jaxpr/ppermute | solution.py:14
  92.2 9.3 %collective-permute-start = (f32[1,128,256]{1,2,0:T(8,128)S(1)}, f32[1,128,256]{1,2,0:T(8,128)S(1)}, u32[]{:S(2)}, u32[]{:S(2)}) collective-permute-start(f32[1,128,256]{1,2,0:T(8,128)S(1)} %get-tuple-element.126), channel_id=1, source_target_pairs={{16,0},{32,16},{48,32},{64,48},{80,64},{96,80},{112,96},{128,112},... | collective-permute-start | bytes 393224 | tf_op jit(solution)/shard_map/while/body/eval_jaxpr/ppermute | solution.py:14
  102.2 8.5 %collective-permute-start = (f32[1,128,256]{1,2,0:T(8,128)S(1)}, f32[1,128,256]{1,2,0:T(8,128)S(1)}, u32[]{:S(2)}, u32[]{:S(2)}) collective-permute-start(f32[1,128,256]{1,2,0:T(8,128)S(1)} %get-tuple-element.126), channel_id=1, source_target_pairs={{16,0},{32,16},{48,32},{64,48},{80,64},{96,80},{112,96},{128,112},... | collective-permute-start | bytes 393224 | tf_op jit(solution)/shard_map/while/body/eval_jaxpr/ppermute | solution.py:14
  118.8 7.5 %collective-permute-start = (f32[1,128,256]{1,2,0:T(8,128)S(1)}, f32[1,128,256]{1,2,0:T(8,128)S(1)}, u32[]{:S(2)}, u32[]{:S(2)}) collective-permute-start(f32[1,128,256]{1,2,0:T(8,128)S(1)} %get-tuple-element.126), channel_id=1, source_target_pairs={{16,0},{32,16},{48,32},{64,48},{80,64},{96,80},{112,96},{128,112},... | collective-permute-start | bytes 393224 | tf_op jit(solution)/shard_map/while/body/eval_jaxpr/ppermute | solution.py:14
  127.0 7.8 %collective-permute-start = (f32[1,128,256]{1,2,0:T(8,128)S(1)}, f32[1,128,256]{1,2,0:T(8,128)S(1)}, u32[]{:S(2)}, u32[]{:S(2)}) collective-permute-start(f32[1,128,256]{1,2,0:T(8,128)S(1)} %get-tuple-element.126), channel_id=1, source_target_pairs={{16,0},{32,16},{48,32},{64,48},{80,64},{96,80},{112,96},{128,112},... | collective-permute-start | bytes 393224 | tf_op jit(solution)/shard_map/while/body/eval_jaxpr/ppermute | solution.py:14
  135.5 7.8 %collective-permute-start = (f32[1,128,256]{1,2,0:T(8,128)S(1)}, f32[1,128,256]{1,2,0:T(8,128)S(1)}, u32[]{:S(2)}, u32[]{:S(2)}) collective-permute-start(f32[1,128,256]{1,2,0:T(8,128)S(1)} %get-tuple-element.126), channel_id=1, source_target_pairs={{16,0},{32,16},{48,32},{64,48},{80,64},{96,80},{112,96},{128,112},... | collective-permute-start | bytes 393224 | tf_op jit(solution)/shard_map/while/body/eval_jaxpr/ppermute | solution.py:14
  143.9 7.8 %collective-permute-start = (f32[1,128,256]{1,2,0:T(8,128)S(1)}, f32[1,128,256]{1,2,0:T(8,128)S(1)}, u32[]{:S(2)}, u32[]{:S(2)}) collective-permute-start(f32[1,128,256]{1,2,0:T(8,128)S(1)} %get-tuple-element.126), channel_id=1, source_target_pairs={{16,0},{32,16},{48,32},{64,48},{80,64},{96,80},{112,96},{128,112},... | collective-permute-start | bytes 393224 | tf_op jit(solution)/shard_map/while/body/eval_jaxpr/ppermute | solution.py:14
  152.4 7.8 %collective-permute-start = (f32[1,128,256]{1,2,0:T(8,128)S(1)}, f32[1,128,256]{1,2,0:T(8,128)S(1)}, u32[]{:S(2)}, u32[]{:S(2)}) collective-permute-start(f32[1,128,256]{1,2,0:T(8,128)S(1)} %get-tuple-element.126), channel_id=1, source_target_pairs={{16,0},{32,16},{48,32},{64,48},{80,64},{96,80},{112,96},{128,112},... | collective-permute-start | bytes 393224 | tf_op jit(solution)/shard_map/while/body/eval_jaxpr/ppermute | solution.py:14
  160.8 9.2 %collective-permute-start = (f32[1,128,256]{1,2,0:T(8,128)S(1)}, f32[1,128,256]{1,2,0:T(8,128)S(1)}, u32[]{:S(2)}, u32[]{:S(2)}) collective-permute-start(f32[1,128,256]{1,2,0:T(8,128)S(1)} %get-tuple-element.126), channel_id=1, source_target_pairs={{16,0},{32,16},{48,32},{64,48},{80,64},{96,80},{112,96},{128,112},... | collective-permute-start | bytes 393224 | tf_op jit(solution)/shard_map/while/body/eval_jaxpr/ppermute | solution.py:14
  170.7 9.8 %collective-permute-start = (f32[1,128,256]{1,2,0:T(8,128)S(1)}, f32[1,128,256]{1,2,0:T(8,128)S(1)}, u32[]{:S(2)}, u32[]{:S(2)}) collective-permute-start(f32[1,128,256]{1,2,0:T(8,128)S(1)} %get-tuple-element.126), channel_id=1, source_target_pairs={{16,0},{32,16},{48,32},{64,48},{80,64},{96,80},{112,96},{128,112},... | collective-permute-start | bytes 393224 | tf_op jit(solution)/shard_map/while/body/eval_jaxpr/ppermute | solution.py:14
  181.1 7.5 %collective-permute-start = (f32[1,128,256]{1,2,0:T(8,128)S(1)}, f32[1,128,256]{1,2,0:T(8,128)S(1)}, u32[]{:S(2)}, u32[]{:S(2)}) collective-permute-start(f32[1,128,256]{1,2,0:T(8,128)S(1)} %get-tuple-element.126), channel_id=1, source_target_pairs={{16,0},{32,16},{48,32},{64,48},{80,64},{96,80},{112,96},{128,112},... | collective-permute-start | bytes 393224 | tf_op jit(solution)/shard_map/while/body/eval_jaxpr/ppermute | solution.py:14
  189.3 7.2 %collective-permute-start = (f32[1,128,256]{1,2,0:T(8,128)S(1)}, f32[1,128,256]{1,2,0:T(8,128)S(1)}, u32[]{:S(2)}, u32[]{:S(2)}) collective-permute-start(f32[1,128,256]{1,2,0:T(8,128)S(1)} %get-tuple-element.126), channel_id=1, source_target_pairs={{16,0},{32,16},{48,32},{64,48},{80,64},{96,80},{112,96},{128,112},... | collective-permute-start | bytes 393224 | tf_op jit(solution)/shard_map/while/body/eval_jaxpr/ppermute | solution.py:14
  197.2 7.3 %collective-permute-start = (f32[1,128,256]{1,2,0:T(8,128)S(1)}, f32[1,128,256]{1,2,0:T(8,128)S(1)}, u32[]{:S(2)}, u32[]{:S(2)}) collective-permute-start(f32[1,128,256]{1,2,0:T(8,128)S(1)} %get-tuple-element.126), channel_id=1, source_target_pairs={{16,0},{32,16},{48,32},{64,48},{80,64},{96,80},{112,96},{128,112},... | collective-permute-start | bytes 393224 | tf_op jit(solution)/shard_map/while/body/eval_jaxpr/ppermute | solution.py:14
  205.1 7.8 %collective-permute-start = (f32[1,128,256]{1,2,0:T(8,128)S(1)}, f32[1,128,256]{1,2,0:T(8,128)S(1)}, u32[]{:S(2)}, u32[]{:S(2)}) collective-permute-start(f32[1,128,256]{1,2,0:T(8,128)S(1)} %get-tuple-element.126), channel_id=1, source_target_pairs={{16,0},{32,16},{48,32},{64,48},{80,64},{96,80},{112,96},{128,112},... | collective-permute-start | bytes 393224 | tf_op jit(solution)/shard_map/while/body/eval_jaxpr/ppermute | solution.py:14
  213.6 7.8 %collective-permute-start = (f32[1,128,256]{1,2,0:T(8,128)S(1)}, f32[1,128,256]{1,2,0:T(8,128)S(1)}, u32[]{:S(2)}, u32[]{:S(2)}) collective-permute-start(f32[1,128,256]{1,2,0:T(8,128)S(1)} %get-tuple-element.126), channel_id=1, source_target_pairs={{16,0},{32,16},{48,32},{64,48},{80,64},{96,80},{112,96},{128,112},... | collective-permute-start | bytes 393224 | tf_op jit(solution)/shard_map/while/body/eval_jaxpr/ppermute | solution.py:14
  222.1 7.8 %collective-permute-start = (f32[1,128,256]{1,2,0:T(8,128)S(1)}, f32[1,128,256]{1,2,0:T(8,128)S(1)}, u32[]{:S(2)}, u32[]{:S(2)}) collective-permute-start(f32[1,128,256]{1,2,0:T(8,128)S(1)} %get-tuple-element.126), channel_id=1, source_target_pairs={{16,0},{32,16},{48,32},{64,48},{80,64},{96,80},{112,96},{128,112},... | collective-permute-start | bytes 393224 | tf_op jit(solution)/shard_map/while/body/eval_jaxpr/ppermute | solution.py:14
  230.5 8.2 %collective-permute-start = (f32[1,128,256]{1,2,0:T(8,128)S(1)}, f32[1,128,256]{1,2,0:T(8,128)S(1)}, u32[]{:S(2)}, u32[]{:S(2)}) collective-permute-start(f32[1,128,256]{1,2,0:T(8,128)S(1)} %get-tuple-element.126), channel_id=1, source_target_pairs={{16,0},{32,16},{48,32},{64,48},{80,64},{96,80},{112,96},{128,112},... | collective-permute-start | bytes 393224 | tf_op jit(solution)/shard_map/while/body/eval_jaxpr/ppermute | solution.py:14
  239.4 9.6 %collective-permute-start = (f32[1,128,256]{1,2,0:T(8,128)S(1)}, f32[1,128,256]{1,2,0:T(8,128)S(1)}, u32[]{:S(2)}, u32[]{:S(2)}) collective-permute-start(f32[1,128,256]{1,2,0:T(8,128)S(1)} %get-tuple-element.126), channel_id=1, source_target_pairs={{16,0},{32,16},{48,32},{64,48},{80,64},{96,80},{112,96},{128,112},... | collective-permute-start | bytes 393224 | tf_op jit(solution)/shard_map/while/body/eval_jaxpr/ppermute | solution.py:14
  249.7 8.6 %collective-permute-start = (f32[1,128,256]{1,2,0:T(8,128)S(1)}, f32[1,128,256]{1,2,0:T(8,128)S(1)}, u32[]{:S(2)}, u32[]{:S(2)}) collective-permute-start(f32[1,128,256]{1,2,0:T(8,128)S(1)} %get-tuple-element.126), channel_id=1, source_target_pairs={{16,0},{32,16},{48,32},{64,48},{80,64},{96,80},{112,96},{128,112},... | collective-permute-start | bytes 393224 | tf_op jit(solution)/shard_map/while/body/eval_jaxpr/ppermute | solution.py:14
  258.9 8.0 %collective-permute-start = (f32[1,128,256]{1,2,0:T(8,128)S(1)}, f32[1,128,256]{1,2,0:T(8,128)S(1)}, u32[]{:S(2)}, u32[]{:S(2)}) collective-permute-start(f32[1,128,256]{1,2,0:T(8,128)S(1)} %get-tuple-element.126), channel_id=1, source_target_pairs={{16,0},{32,16},{48,32},{64,48},{80,64},{96,80},{112,96},{128,112},... | collective-permute-start | bytes 393224 | tf_op jit(solution)/shard_map/while/body/eval_jaxpr/ppermute | solution.py:14
  267.6 7.0 %collective-permute-start = (f32[1,128,256]{1,2,0:T(8,128)S(1)}, f32[1,128,256]{1,2,0:T(8,128)S(1)}, u32[]{:S(2)}, u32[]{:S(2)}) collective-permute-start(f32[1,128,256]{1,2,0:T(8,128)S(1)} %get-tuple-element.126), channel_id=1, source_target_pairs={{16,0},{32,16},{48,32},{64,48},{80,64},{96,80},{112,96},{128,112},... | collective-permute-start | bytes 393224 | tf_op jit(solution)/shard_map/while/body/eval_jaxpr/ppermute | solution.py:14
  275.2 7.8 %collective-permute-start = (f32[1,128,256]{1,2,0:T(8,128)S(1)}, f32[1,128,256]{1,2,0:T(8,128)S(1)}, u32[]{:S(2)}, u32[]{:S(2)}) collective-permute-start(f32[1,128,256]{1,2,0:T(8,128)S(1)} %get-tuple-element.126), channel_id=1, source_target_pairs={{16,0},{32,16},{48,32},{64,48},{80,64},{96,80},{112,96},{128,112},... | collective-permute-start | bytes 393224 | tf_op jit(solution)/shard_map/while/body/eval_jaxpr/ppermute | solution.py:14
  283.7 7.8 %collective-permute-start = (f32[1,128,256]{1,2,0:T(8,128)S(1)}, f32[1,128,256]{1,2,0:T(8,128)S(1)}, u32[]{:S(2)}, u32[]{:S(2)}) collective-permute-start(f32[1,128,256]{1,2,0:T(8,128)S(1)} %get-tuple-element.126), channel_id=1, source_target_pairs={{16,0},{32,16},{48,32},{64,48},{80,64},{96,80},{112,96},{128,112},... | collective-permute-start | bytes 393224 | tf_op jit(solution)/shard_map/while/body/eval_jaxpr/ppermute | solution.py:14
  292.1 7.8 %collective-permute-start = (f32[1,128,256]{1,2,0:T(8,128)S(1)}, f32[1,128,256]{1,2,0:T(8,128)S(1)}, u32[]{:S(2)}, u32[]{:S(2)}) collective-permute-start(f32[1,128,256]{1,2,0:T(8,128)S(1)} %get-tuple-element.126), channel_id=1, source_target_pairs={{16,0},{32,16},{48,32},{64,48},{80,64},{96,80},{112,96},{128,112},... | collective-permute-start | bytes 393224 | tf_op jit(solution)/shard_map/while/body/eval_jaxpr/ppermute | solution.py:14
  (37 other events, 45.0 us)
Sparse Core Ops, SparseCore 0:
  314.7 204.5 all-reduce.6
where the time goes:
time: 529 us; the launch traced here: 528 us
  waiting for transfers between devices  418 us (79%)
  starting transfers between devices  42.3 us (8%)
  local copies, waits for them, and re-layouts  36.7 us (7%)
  between operations  15.1 us (3%)
  matrix products  14.1 us (3%)
    ppermute x33, waiting for transfers between devices, shifted(): return lax.ppermute(shard, axis, pairs)  217 us
    unnamed x2, waiting for transfers between devices  201 us
    ppermute x33, starting transfers between devices, shifted(): return lax.ppermute(shard, axis, pairs)  42.3 us
    another operation x8, local copies, waits for them, and re-layouts, shifted_stack(): return jnp.stack(pieces, axis=1).reshape(images, 9 * channels, pixels)  12.4 us
    while x64, local copies, waits for them, and re-layouts  11.9 us
  transfers between devices with their start and end apart: 34, of which 34 were waited for; matrix products, arithmetic and copies ran while one was open for 1% of the time, Pallas kernels for 0%

commit v1 on v0

v1 whole, which is shorter than its diff:
```python
import functools

import jax
import jax.numpy as jnp
from jax import lax
from jax.experimental import pallas as pl
from jax.experimental.pallas import tpu as pltpu
from jax.sharding import PartitionSpec as P

STEP = 0.0625
KEEP = 1.0 - STEP
SIDE, PIX, CH, TAPS = 32, 1024, 128, 9
HALF = SIDE // 2
CELLS = HALF * HALF
XS, YS, ZS = 4, 8, 8
BF, F32 = jnp.bfloat16, jnp.float32
EXACT = lax.Precision.HIGHEST
VMEM = pl.BlockSpec(memory_space=pltpu.VMEM)


def dot(a, b, precision=None):
    return jnp.dot(a, b, preferred_element_type=F32, precision=precision)


def split(a):
    high = a.astype(BF)
    return high, (a - high.astype(F32)).astype(BF)


def write_stack(field, stack_ref):
    lane = lax.broadcasted_iota(jnp.int32, (1, PIX), 1)
    col = lane & (SIDE - 1)
    first, last = (col != 0).astype(BF), (col != SIDE - 1).astype(BF)
    top, bottom = (lane >= SIDE).astype(BF), (lane < PIX - SIDE).astype(BF)
    columns = (
        pltpu.roll(field, PIX - 1, 1) * last,
        field,
        pltpu.roll(field, 1, 1) * first,
    )
    for c, moved in enumerate(columns):
        rows = (
            pltpu.roll(moved, PIX - SIDE, 1) * bottom,
            moved,
            pltpu.roll(moved, SIDE, 1) * top,
        )
        for a, piece in enumerate(rows):
            t = 3 * a + c
            stack_ref[t * CH : (t + 1) * CH, :] = piece


def pool_matrix():
    pixel = lax.broadcasted_iota(jnp.int32, (PIX, CELLS), 0)
    cell = lax.broadcasted_iota(jnp.int32, (PIX, CELLS), 1)
    square = ((pixel >> 6) << 4) + ((pixel & (SIDE - 1)) >> 1)
    return square == cell


def spread_matrix():
    cell = lax.broadcasted_iota(jnp.int32, (CELLS, PIX), 0)
    pixel = lax.broadcasted_iota(jnp.int32, (CELLS, PIX), 1)
    square = ((pixel >> 6) << 4) + ((pixel & (SIDE - 1)) >> 1)
    return (square == cell).astype(F32).astype(BF)


def prep_kernel(states_ref, filters_ref, act_ref, slope_ref, matrix_ref):
    total = filters_ref[:, 0:CH].astype(F32)
    for t in range(1, TAPS):
        total += filters_ref[:, t * CH : (t + 1) * CH].astype(F32)
    row = lax.broadcasted_iota(jnp.int32, (CH, CH), 0)
    col = lax.broadcasted_iota(jnp.int32, (CH, CH), 1)
    base = jnp.where(row == col, KEEP, 0.0) + STEP * total
    matrix = dot(base, base, EXACT)
    for j in range(XS):
        matrix_ref[j] = matrix
    for l in range(2):
        act = jnp.tanh(states_ref[l].astype(F32))
        act_ref[l] = act.astype(BF)
        slope_ref[l] = STEP * (1.0 - act * act)


def fine_kernel(above_ref, terminal_ref, guess_ref, slope_ref, filters_ref, top_ref, coarse_ref, stack_ref):
    last = lax.axis_index("layer") == XS * YS - 1
    top = jnp.where(last, terminal_ref[...].astype(F32), above_ref[...].astype(F32))
    top_ref[...] = top.astype(BF)
    write_stack(top.astype(BF), stack_ref)
    below = (KEEP * top + slope_ref[1] * dot(filters_ref[1], stack_ref[...])).astype(BF)
    write_stack(below, stack_ref)
    residual = KEEP * below.astype(F32) + slope_ref[0] * dot(filters_ref[0], stack_ref[...])
    residual -= guess_ref[...].astype(F32)
    high, low = split(residual)
    pool = jnp.where(pool_matrix(), 0.25, 0.0).astype(BF)
    coarse = (dot(high, pool) + dot(low, pool)).astype(BF)
    for j in range(XS):
        coarse_ref[j] = coarse


def group_kernel(matrix_ref, part_ref, reach_ref, group_ref, row_scr, reach_scr):
    m0, m1, m2, m3 = (matrix_ref[j] for j in range(XS))
    p01, p12, p23 = dot(m0, m1, EXACT), dot(m1, m2, EXACT), dot(m2, m3, EXACT)
    p012, p123, group = dot(p01, m2, EXACT), dot(p12, m3, EXACT), dot(p01, p23, EXACT)
    for j in range(YS):
        group_ref[j] = group
    row = lax.broadcasted_iota(jnp.int32, (CH, CH), 0)
    col = lax.broadcasted_iota(jnp.int32, (CH, CH), 1)
    one = jnp.where(row == col, 1.0, 0.0)
    nil = jnp.zeros((CH, CH), F32)
    table = (
        (one, m0, p01, p012),
        (nil, one, m1, p12),
        (nil, nil, one, m2),
        (nil, nil, nil, one),
        (nil, nil, nil, nil),
    )
    for s in range(5):
        for j in range(4):
            row_scr[s, :, j * CH : (j + 1) * CH] = table[s][j]
    for s, reach in enumerate((group, p123, p23, m3, one)):
        reach_scr[s] = reach
    x = lax.axis_index("layer") % XS
    for i, s in enumerate((0, x, x + 1)):
        high, low = split(row_scr[s])
        part_ref[i * CH : (i + 1) * CH, : XS * CH] = high
        part_ref[i * CH : (i + 1) * CH, XS * CH :] = low
    reach_ref[:CH] = reach_scr[x]
    reach_ref[CH:] = reach_scr[x + 1]


def local_kernel(part_ref, coarse_ref, value_ref, local_ref):
    coarse = coarse_ref[...].reshape(XS * CH, CELLS)
    part = dot(part_ref[:, : XS * CH], coarse) + dot(part_ref[:, XS * CH :], coarse)
    value = part[:CH].astype(BF)
    for j in range(YS):
        value_ref[j] = value
    local_ref[...] = part[CH:]


def reach_kernel(group_ref, reach_ref, far_ref):
    y = lax.axis_index("layer") // XS
    reach = reach_ref[...]
    nil = jnp.zeros_like(reach)
    for j in range(YS):
        ahead = j > y
        high, low = split(jnp.where(ahead, reach, nil))
        far_ref[:, j * CH : (j + 1) * CH] = high
        far_ref[:, (YS + j) * CH : (YS + j + 1) * CH] = low
        if j < YS - 1:
            reach = jnp.where(ahead, dot(reach, group_ref[j], EXACT), reach)


def correct_kernel(
    far_ref, value_ref, local_ref, top_ref, guess_ref, slope_ref, act_ref, filters_ref,
    adjoint_ref, keep_ref, send_ref, stack_ref, grad_scr,
):
    value = value_ref[...].reshape(YS * CH, CELLS)
    error = local_ref[...] + dot(far_ref[:, : YS * CH], value) + dot(far_ref[:, YS * CH :], value)
    high, low = split(error)
    spread = spread_matrix()
    wide = dot(high, spread) + dot(low, spread)
    adjoint_ref[0] = (guess_ref[...].astype(F32) + wide[:CH]).astype(BF)
    top = (top_ref[...].astype(F32) + wide[CH:]).astype(BF)
    nt = (((1,), (1,)), ((), ()))

    def gradient(l):
        grad = STEP * lax.dot_general(act_ref[l], stack_ref[...], nt, preferred_element_type=F32)
        grad_scr[:, :, l] = grad.reshape(ZS, 2, 8, TAPS * CH)

    write_stack(top, stack_ref)
    below = KEEP * top.astype(F32) + slope_ref[1] * dot(filters_ref[1], stack_ref[...])
    gradient(1)
    below = below.astype(BF)
    adjoint_ref[1] = below
    write_stack(below, stack_ref)
    gradient(0)
    core = lax.axis_index("dp") % 2
    keep_ref[...] = grad_scr[:, core]
    send_ref[...] = grad_scr[:, 1 - core].astype(BF)


def join_kernel(keep_ref, came_ref, sum_ref):
    sum_ref[...] = (keep_ref[...] + came_ref[...].astype(F32)).astype(BF)


def total_kernel(came_ref, grad_ref):
    total = came_ref[0].astype(F32)
    for z in range(1, ZS):
        total += came_ref[z].astype(F32)
    grad_ref[...] = total


def call(body, outs, scratch=(), flops=10**6, name=None):
    outs = [jax.ShapeDtypeStruct(s, d) for s, d in outs]
    single = len(outs) == 1
    return pl.pallas_call(
        body,
        out_shape=outs[0] if single else outs,
        scratch_shapes=[pltpu.VMEM(s, d) for s, d in scratch],
        name=name,
        compiler_params=pltpu.CompilerParams(vmem_limit_bytes=48 << 20),
        cost_estimate=pl.CostEstimate(flops=flops, bytes_accessed=1 << 20, transcendentals=0),
    )


STACK = ((TAPS * CH, PIX), BF)
prep = call(prep_kernel, [((2, CH, PIX), BF), ((2, CH, PIX), F32), ((XS, CH, CH), F32)])
fine = call(fine_kernel, [((CH, PIX), BF), ((XS, CH, CELLS), BF)], [STACK], 10**9)
group_of = call(
    group_kernel,
    [((3 * CH, 2 * XS * CH), BF), ((2 * CH, CH), F32), ((YS, CH, CH), F32)],
    [((5, CH, XS * CH), F32), ((5, CH, CH), F32)],
)
local_of = call(local_kernel, [((YS, CH, CELLS), BF), ((2 * CH, CELLS), F32)])
reach_of = call(reach_kernel, [((2 * CH, 2 * YS * CH), BF)])
correct = call(
    correct_kernel,
    [((2, CH, PIX), BF), ((ZS, 2, 8, TAPS * CH), F32), ((ZS, 2, 8, TAPS * CH), BF)],
    [STACK, ((ZS, 2, 2, 8, TAPS * CH), F32)],
    2 * 10**9,
)
join = call(join_kernel, [((ZS, 2, 8, TAPS * CH), BF)])
total_of = call(total_kernel, [((2, 8, TAPS * CH), F32)])


def per_device(states, filters, guess, terminal):
    states, guess, terminal = states[:, 0], guess[:, 0], terminal[0]
    x_groups = [[y * XS + x for x in range(XS)] for y in range(YS)]
    y_groups = [[y * XS + x for y in range(YS)] for x in range(XS)]
    z_groups = [[z * 2 + c for z in range(ZS)] for c in range(2)]

    def exchange(a, axis, groups):
        return lax.all_to_all(a, axis, 0, 0, axis_index_groups=groups)

    above = lax.ppermute(guess[0], "layer", [(i + 1, i) for i in range(XS * YS - 1)])
    act, slope, matrix = prep(states, filters[0])
    matrices = exchange(matrix, "layer", x_groups)
    top, coarse = fine(above, terminal, guess[0], slope, filters)
    coarses = exchange(coarse, "layer", x_groups)
    part, reach, group = group_of(matrices)
    groups = exchange(group, "layer", y_groups)
    value, local = local_of(part, coarses)
    values = exchange(value, "layer", y_groups)
    far = reach_of(groups, reach)
    adjoint, keep, send = correct(far, values, local, top, guess[0], slope, act, filters)
    came = lax.ppermute(send, "dp", [(i ^ 1, i) for i in range(2 * ZS)])
    shares = exchange(join(keep, came), "dp", z_groups)
    return adjoint[:, None], total_of(shares)


def solution(mesh):
    return jax.shard_map(
        per_device,
        mesh=mesh,
        in_specs=(
            P("layer", "dp", None, None),
            P("layer", None, None),
            P("layer", "dp", None, None),
            P("dp", None, None),
        ),
        out_specs=(P("layer", "dp", None, None), P("layer", "dp", None)),
        check_vma=False,
    )
```

time: 529 us -> 103 us (0.19)
  waiting for transfers between devices: 418 us -> 31 us
  local copies, waits for them, and re-layouts: 36.7 us -> 5.96 us
  blocking collectives: 0 us -> 22 us
  between operations: 15.1 us -> 0.72 us
  matrix products: 14.1 us -> 0 us
  Pallas kernels: 0 us -> 13.3 us
  starting transfers between devices: 42.3 us -> 29.7 us
    ppermute x33 -> x2, waiting for transfers between devices: 217 us -> 1.19 us  [the longest x1 1.19 us: per_device(): came = lax.ppermute(send, 'dp', [(i ^ 1, i) for i in range(2 * ZS)])]
    unnamed x2 -> x0, waiting for transfers between devices: 201 us -> none
    ppermute x33 -> x2, starting transfers between devices: 42.3 us -> 8.6 us  [the longest x1 7.31 us: per_device(): came = lax.ppermute(send, 'dp', [(i ^ 1, i) for i in range(2 * ZS)])]
    all_to_all x0 -> x4, waiting for transfers between devices: none -> 29.8 us  [exchange(): return lax.all_to_all(a, axis, 0, 0, axis_index_groups=groups)]
    all_to_all x0 -> x1, blocking collectives: none -> 22 us  [exchange(): return lax.all_to_all(a, axis, 0, 0, axis_index_groups=groups)]
    all_to_all x0 -> x4, starting transfers between devices: none -> 21.1 us  [exchange(): return lax.all_to_all(a, axis, 0, 0, axis_index_groups=groups)]
    dot_general x38 -> x0, matrix products: 14.1 us -> none  [the longest x32 8.83 us: apply_matrix(): jnp.einsum('ij,bjp->bip', matrix, in_field, precision=lax.Precision.HIGHEST)]
    pallas_call x0 -> x8, Pallas kernels: none -> 13.3 us  [the longest x1 3.79 us: per_device(): correct(far, values, local, top, guess[0], slope, act, filters)]
  transfers between devices with their start and end apart: 34 -> 6, of which waited for: 34 -> 5; matrix products, arithmetic and copies ran while one was open for 1% -> 1% of each run, Pallas kernels for 0% -> 9%
where the time goes in v1:
time: 103 us
  waiting for transfers between devices  31 us (30%)
  starting transfers between devices  29.7 us (29%)
  blocking collectives  22 us (21%)
  Pallas kernels  13.3 us (13%)
  local copies, waits for them, and re-layouts  5.96 us (6%)
    all_to_all x4, waiting for transfers between devices, exchange(): return lax.all_to_all(a, axis, 0, 0, axis_index_groups=groups)  29.8 us
    all_to_all x1, blocking collectives, exchange(): return lax.all_to_all(a, axis, 0, 0, axis_index_groups=groups)  22 us
    all_to_all x4, starting transfers between devices, exchange(): return lax.all_to_all(a, axis, 0, 0, axis_index_groups=groups)  21.1 us
    ppermute x1, starting transfers between devices, per_device(): came = lax.ppermute(send, 'dp', [(i ^ 1, i) for i in range(2 * ZS)])  7.31 us
    unnamed x18, local copies, waits for them, and re-layouts  3.94 us
    pallas_call x1, Pallas kernels, per_device(): correct(far, values, local, top, guess[0], slope, act, filters)  3.79 us
    pallas_call x1, Pallas kernels, per_device(): top, coarse = fine(above, terminal, guess[0], slope, filters)  2.96 us
    pallas_call x1, Pallas kernels, per_device(): far = reach_of(groups, reach)  2.14 us
  transfers between devices with their start and end apart: 6, of which 5 were waited for; matrix products, arithmetic and copies ran while one was open for 1% of the time, Pallas kernels for 9%

profile of v1, /device:TPU:1, one launch (start us, length us, event | category | flops | bytes accessed | tf_op | source)
XLA Modules:
  0.0 102.7 jit_solution(11277343267226694078)
XLA Ops:
  0.6 0.0 copy-start
  0.6 1.0 slice_bitcast_fusion.1.guess_ref
  1.7 1.3 %collective-permute-start = (bf16[128,1024]{1,0:T(8,128)(2,1)S(1)}, bf16[128,1024]{1,0:T(8,128)(2,1)S(1)}, u32[]{:S(2)}, u32[]{:S(2)}) collective-permute-start(bf16[128,1024]{1,0:T(8,128)(2,1)S(1)} %slice_bitcast_fusion.1.guess_ref), channel_id=1, source_target_pairs={{16,0},{32,16},{48,32},{64,48},{80,64},{96,80},{112,96},{128,112},... | collective-permute-start | bytes 786440 | tf_op jit(solution)/shard_map/ppermute | solution.py:232
  3.0 1.0 slice_bitcast_fusion.filters_ref
  4.0 0.0 copy-done
  4.0 0.0 copy-start.1
  4.0 1.0 shard_map.59
  4.9 5.9 %all-to-all-start = ((f32[4,128,128]{2,1,0:T(8,128)}), f32[4,128,128]{2,1,0:T(8,128)S(1)}, u32[]{:S(2)}, u32[]{:S(2)}) async-start(f32[4,128,128]{2,1,0:T(8,128)} %get-tuple-element.15), calls=%async_computation | async-start | bytes 524288 | tf_op jit(solution)/shard_map/all_to_all | solution.py:230
  10.8 0.0 collective-permute-done.above_ref
  10.8 0.0 copy-done.1
  10.8 0.0 copy-done.6
  10.8 3.0 %shard_map.62 = (bf16[128,1024]{1,0:T(8,128)(2,1)S(1)}, bf16[4,128,256]{2,1,0:T(8,128)(2,1)}) custom-call(bf16[128,1024]{1,0:T(8,128)(2,1)S(1)} %collective-permute-done.above_ref, bf16[128,1024]{1,0:T(8,128)(2,1)S(1)} %bitcast.10, bf16[128,1024]{1,0:T(8,128)(2,1)S(1)} %slice_bitcast_fusion.1.guess_ref, f32[2,128,1024]{2,1,0:T(8,128)S(1)} %get-tuple-element.19.slope_ref, ...), custom_call_target="tpu_custom_call" | custom-call | flops 1000000000 | bytes 1048576 | tf_op jit(solution)/shard_map/pallas_call | solution.py:235
  13.8 0.7 copy-done.7
  14.5 1.8 %all-to-all-done.matrix_ref = f32[4,128,128]{2,1,0:T(8,128)S(1)} async-done(((f32[4,128,128]{2,1,0:T(8,128)}), f32[4,128,128]{2,1,0:T(8,128)S(1)}, u32[]{:S(2)}, u32[]{:S(2)}) %all-to-all-start) | async-done | bytes 262176 | tf_op jit(solution)/shard_map/all_to_all | solution.py:230
  16.3 4.8 %all-to-all-start.2 = ((bf16[4,128,256]{2,1,0:T(8,128)(2,1)}), bf16[4,128,256]{2,1,0:T(8,128)(2,1)S(1)}, u32[]{:S(2)}, u32[]{:S(2)}) async-start(bf16[4,128,256]{2,1,0:T(8,128)(2,1)} %get-tuple-element.20), calls=%async_computation.2 | async-start | bytes 524288 | tf_op jit(solution)/shard_map/all_to_all | solution.py:230
  21.1 1.6 %shard_map.60 = (bf16[384,1024]{1,0:T(8,128)(2,1)S(1)}, f32[256,128]{1,0:T(8,128)S(1)}, f32[8,128,128]{2,1,0:T(8,128)}) custom-call(f32[4,128,128]{2,1,0:T(8,128)S(1)} %all-to-all-done.matrix_ref), custom_call_target="tpu_custom_call" | custom-call | flops 1000000 | bytes 1048576 | tf_op jit(solution)/shard_map/pallas_call | solution.py:237
  22.7 4.0 %all-to-all-done.2.coarse_ref = bf16[4,128,256]{2,1,0:T(8,128)(2,1)S(1)} async-done(((bf16[4,128,256]{2,1,0:T(8,128)(2,1)}), bf16[4,128,256]{2,1,0:T(8,128)(2,1)S(1)}, u32[]{:S(2)}, u32[]{:S(2)}) %all-to-all-start.2) | async-done | bytes 262176 | tf_op jit(solution)/shard_map/all_to_all | solution.py:230
  26.6 7.0 %all-to-all-start.1 = ((f32[8,128,128]{2,1,0:T(8,128)}), f32[8,128,128]{2,1,0:T(8,128)S(1)}, u32[]{:S(2)}, u32[]{:S(2)}) async-start(f32[8,128,128]{2,1,0:T(8,128)} %get-tuple-element.16), calls=%async_computation.1 | async-start | bytes 1048576 | tf_op jit(solution)/shard_map/all_to_all | solution.py:230
  33.7 1.1 %shard_map.63 = (bf16[8,128,256]{2,1,0:T(8,128)(2,1)}, f32[256,256]{1,0:T(8,128)S(1)}) custom-call(bf16[384,1024]{1,0:T(8,128)(2,1)S(1)} %get-tuple-element.18.part_ref, bf16[4,128,256]{2,1,0:T(8,128)(2,1)S(1)} %all-to-all-done.2.coarse_ref), custom_call_target="tpu_custom_call" | custom-call | flops 1000000 | bytes 1048576 | tf_op jit(solution)/shard_map/pallas_call | solution.py:239
  34.8 13.2 %all-to-all-done.1.group_ref = f32[8,128,128]{2,1,0:T(8,128)S(1)} async-done(((f32[8,128,128]{2,1,0:T(8,128)}), f32[8,128,128]{2,1,0:T(8,128)S(1)}, u32[]{:S(2)}, u32[]{:S(2)}) %all-to-all-start.1) | async-done | bytes 524320 | tf_op jit(solution)/shard_map/all_to_all | solution.py:230
  48.0 3.5 %all-to-all-start.3 = ((bf16[8,128,256]{2,1,0:T(8,128)(2,1)}), bf16[8,128,256]{2,1,0:T(8,128)(2,1)S(1)}, u32[]{:S(2)}, u32[]{:S(2)}) async-start(bf16[8,128,256]{2,1,0:T(8,128)(2,1)} %get-tuple-element.21), calls=%async_computation.3 | async-start | bytes 1048576 | tf_op jit(solution)/shard_map/all_to_all | solution.py:230
  51.5 2.1 %shard_map.61.far_ref = bf16[256,2048]{1,0:T(8,128)(2,1)S(1)} custom-call(f32[8,128,128]{2,1,0:T(8,128)S(1)} %all-to-all-done.1.group_ref, f32[256,128]{1,0:T(8,128)S(1)} %get-tuple-element.17.reach_ref), custom_call_target="tpu_custom_call" | custom-call | flops 1000000 | bytes 1048576 | tf_op jit(solution)/shard_map/pallas_call | solution.py:241
  53.6 10.8 %all-to-all-done.3.value_ref = bf16[8,128,256]{2,1,0:T(8,128)(2,1)S(1)} async-done(((bf16[8,128,256]{2,1,0:T(8,128)(2,1)}), bf16[8,128,256]{2,1,0:T(8,128)(2,1)S(1)}, u32[]{:S(2)}, u32[]{:S(2)}) %all-to-all-start.3) | async-done | bytes 524320 | tf_op jit(solution)/shard_map/all_to_all | solution.py:230
  64.5 1.2 %copy-done.3 = f32[2,128,1024]{2,1,0:T(8,128)S(1)} copy-done((f32[2,128,1024]{2,1,0:T(8,128)S(1)}, f32[2,128,1024]{2,1,0:T(8,128)}, u32[]{:S(2)}) %copy-start.3) | copy-done | bytes 1048600
  65.7 1.0 %copy-done.5 = bf16[2,128,1024]{2,1,0:T(8,128)(2,1)S(1)} copy-done((bf16[2,128,1024]{2,1,0:T(8,128)(2,1)S(1)}, bf16[2,128,1024]{2,1,0:T(8,128)(2,1)}, u32[]{:S(2)}) %copy-start.5) | copy-done | bytes 524312
  66.7 0.9 copy-done.8
  67.7 3.8 %shard_map.64 = (bf16[2,128,1024]{2,1,0:T(8,128)(2,1)}, f32[8,2,8,1152]{3,2,1,0:T(8,128)S(1)}, bf16[8,2,8,1152]{3,2,1,0:T(8,128)(2,1)S(1)}) custom-call(bf16[256,2048]{1,0:T(8,128)(2,1)S(1)} %shard_map.61.far_ref, bf16[8,128,256]{2,1,0:T(8,128)(2,1)S(1)} %all-to-all-done.3.value_ref, f32[256,256]{1,0:T(8,128)S(1)} %get-tuple-element.22.local_ref, ...), custom_call_target="tpu_custom_call" | custom-call | flops 2000000000 | bytes 1048576 | tf_op jit(solution)/shard_map/pallas_call | solution.py:242
  71.5 7.3 %collective-permute-start.1 = (bf16[8,2,8,1152]{3,2,1,0:T(8,128)(2,1)S(1)}, bf16[8,2,8,1152]{3,2,1,0:T(8,128)(2,1)S(1)}, u32[]{:S(2)}, u32[]{:S(2)}) collective-permute-start(bf16[8,2,8,1152]{3,2,1,0:T(8,128)(2,1)S(1)} %get-tuple-element.27), channel_id=1, source_target_pairs={{1,0},{0,1},{3,2},{2,3},{5,4},{4,5},{7,6},{6,7},{9,8},{8,9},{11,10... | collective-permute-start | bytes 884744 | tf_op jit(solution)/shard_map/ppermute | solution.py:243
  78.8 1.2 %collective-permute-done.1.came_ref = bf16[8,2,8,1152]{3,2,1,0:T(8,128)(2,1)S(1)} collective-permute-done((bf16[8,2,8,1152]{3,2,1,0:T(8,128)(2,1)S(1)}, bf16[8,2,8,1152]{3,2,1,0:T(8,128)(2,1)S(1)}, u32[]{:S(2)}, u32[]{:S(2)}) %collective-permute-start.1) | collective-permute-done | bytes 294944 | tf_op jit(solution)/shard_map/ppermute | solution.py:243
  80.0 0.1 shard_map.65
  80.0 22.0 %all_to_all.25.came_ref = bf16[8,2,8,1152]{3,2,1,0:T(8,128)(2,1)S(1)} all-to-all(bf16[8,2,8,1152]{3,2,1,0:T(8,128)(2,1)S(1)} %shard_map.65), channel_id=1, replica_groups={{0,2,4,6,8,10,12,14},{1,3,5,7,9,11,13,15},{16,18,20,22,24,26,28,30},{17..., dimensions={0} | all-to-all | bytes 589824 | tf_op jit(solution)/shard_map/all_to_all | solution.py:230
  102.0 0.7 shard_map.66
  (9 shorter events, 0.0 us)
Async XLA Ops:
  0.6 3.3 %copy-start = (bf16[2,1,128,1024]{3,2,1,0:T(8,128)(2,1)S(1)}, bf16[2,1,128,1024]{3,2,1,0:T(8,128)(2,1)}, u32[]{:S(2)}) copy-start(bf16[2,1,128,1024]{3,2,1,0:T(8,128)(2,1)} %param.4) | copy-start | bytes 1572868
  1.7 9.1 %collective-permute-start = (bf16[128,1024]{1,0:T(8,128)(2,1)S(1)}, bf16[128,1024]{1,0:T(8,128)(2,1)S(1)}, u32[]{:S(2)}, u32[]{:S(2)}) collective-permute-start(bf16[128,1024]{1,0:T(8,128)(2,1)S(1)} %slice_bitcast_fusion.1.guess_ref), channel_id=1, source_target_pairs={{16,0},{32,16},{48,32},{64,48},{80,64},{96,80},{112,96},{128,112},... | collective-permute-start | bytes 786440 | tf_op jit(solution)/shard_map/ppermute | solution.py:232
  4.0 6.8 %copy-start.1 = (bf16[2,128,1152]{2,1,0:T(8,128)(2,1)S(1)}, bf16[2,128,1152]{2,1,0:T(8,128)(2,1)}, u32[]{:S(2)}) copy-start(bf16[2,128,1152]{2,1,0:T(8,128)(2,1)} %filters_ref.3) | copy-start | bytes 1769476
  4.9 8.9 %copy-start.2 = (f32[2,128,1024]{2,1,0:T(8,128)}, f32[2,128,1024]{2,1,0:T(8,128)S(1)}, u32[]{:S(2)}) copy-start(f32[2,128,1024]{2,1,0:T(8,128)S(1)} %get-tuple-element.19.slope_ref) | copy-start | bytes 3145732
  4.9 8.9 %copy-start.4 = (bf16[2,128,1024]{2,1,0:T(8,128)(2,1)}, bf16[2,128,1024]{2,1,0:T(8,128)(2,1)S(1)}, u32[]{:S(2)}) copy-start(bf16[2,128,1024]{2,1,0:T(8,128)(2,1)S(1)} %get-tuple-element.24.act_ref) | copy-start | bytes 1572868
  4.9 5.9 %copy-start.6 = (bf16[1,128,1024]{2,1,0:T(8,128)(2,1)S(1)}, bf16[1,128,1024]{2,1,0:T(8,128)(2,1)}, u32[]{:S(2)}) copy-start(bf16[1,128,1024]{2,1,0:T(8,128)(2,1)} %param.7) | copy-start | bytes 786436
  4.9 11.4 %all-to-all-start = ((f32[4,128,128]{2,1,0:T(8,128)}), f32[4,128,128]{2,1,0:T(8,128)S(1)}, u32[]{:S(2)}, u32[]{:S(2)}) async-start(f32[4,128,128]{2,1,0:T(8,128)} %get-tuple-element.15), calls=%async_computation | async-start | bytes 524288 | tf_op jit(solution)/shard_map/all_to_all | solution.py:230
  13.8 0.7 copy-start.7
  16.3 10.3 %all-to-all-start.2 = ((bf16[4,128,256]{2,1,0:T(8,128)(2,1)}), bf16[4,128,256]{2,1,0:T(8,128)(2,1)S(1)}, u32[]{:S(2)}, u32[]{:S(2)}) async-start(bf16[4,128,256]{2,1,0:T(8,128)(2,1)} %get-tuple-element.20), calls=%async_computation.2 | async-start | bytes 524288 | tf_op jit(solution)/shard_map/all_to_all | solution.py:230
  26.6 21.3 %all-to-all-start.1 = ((f32[8,128,128]{2,1,0:T(8,128)}), f32[8,128,128]{2,1,0:T(8,128)S(1)}, u32[]{:S(2)}, u32[]{:S(2)}) async-start(f32[8,128,128]{2,1,0:T(8,128)} %get-tuple-element.16), calls=%async_computation.1 | async-start | bytes 1048576 | tf_op jit(solution)/shard_map/all_to_all | solution.py:230
  48.0 16.5 %all-to-all-start.3 = ((bf16[8,128,256]{2,1,0:T(8,128)(2,1)}), bf16[8,128,256]{2,1,0:T(8,128)(2,1)S(1)}, u32[]{:S(2)}, u32[]{:S(2)}) async-start(bf16[8,128,256]{2,1,0:T(8,128)(2,1)} %get-tuple-element.21), calls=%async_computation.3 | async-start | bytes 1048576 | tf_op jit(solution)/shard_map/all_to_all | solution.py:230
  64.5 1.2 %copy-start.3 = (f32[2,128,1024]{2,1,0:T(8,128)S(1)}, f32[2,128,1024]{2,1,0:T(8,128)}, u32[]{:S(2)}) copy-start(f32[2,128,1024]{2,1,0:T(8,128)} %copy-done.2) | copy-start | bytes 3145732
  65.7 1.0 %copy-start.5 = (bf16[2,128,1024]{2,1,0:T(8,128)(2,1)S(1)}, bf16[2,128,1024]{2,1,0:T(8,128)(2,1)}, u32[]{:S(2)}) copy-start(bf16[2,128,1024]{2,1,0:T(8,128)(2,1)} %copy-done.4) | copy-start | bytes 1572868
  66.7 0.9 copy-start.8
  71.5 8.5 %collective-permute-start.1 = (bf16[8,2,8,1152]{3,2,1,0:T(8,128)(2,1)S(1)}, bf16[8,2,8,1152]{3,2,1,0:T(8,128)(2,1)S(1)}, u32[]{:S(2)}, u32[]{:S(2)}) collective-permute-start(bf16[8,2,8,1152]{3,2,1,0:T(8,128)(2,1)S(1)} %get-tuple-element.27), channel_id=1, source_target_pairs={{1,0},{0,1},{3,2},{2,3},{5,4},{4,5},{7,6},{6,7},{9,8},{8,9},{11,10... | collective-permute-start | bytes 884744 | tf_op jit(solution)/shard_map/ppermute | solution.py:243

commit v2 on v1

v2 whole, which is shorter than its diff:
```python
import functools

import jax
import jax.numpy as jnp
from jax import lax
from jax.experimental import pallas as pl
from jax.experimental.pallas import tpu as pltpu
from jax.sharding import PartitionSpec as P

STEP = 0.0625
KEEP = 1.0 - STEP
SIDE, PIX, CH, TAPS = 32, 1024, 128, 9
HALF = SIDE // 2
CELLS = HALF * HALF
XS, YS, ZS = 4, 8, 8
BF, F32 = jnp.bfloat16, jnp.float32
EXACT = lax.Precision.HIGHEST
VMEM = pl.BlockSpec(memory_space=pltpu.VMEM)


def dot(a, b, precision=None):
    return jnp.dot(a, b, preferred_element_type=F32, precision=precision)


def split(a):
    high = a.astype(BF)
    return high, (a - high.astype(F32)).astype(BF)


def write_stack(field, stack_ref):
    lane = lax.broadcasted_iota(jnp.int32, (1, PIX), 1)
    col = lane & (SIDE - 1)
    first, last = (col != 0).astype(BF), (col != SIDE - 1).astype(BF)
    top, bottom = (lane >= SIDE).astype(BF), (lane < PIX - SIDE).astype(BF)
    columns = (
        pltpu.roll(field, PIX - 1, 1) * last,
        field,
        pltpu.roll(field, 1, 1) * first,
    )
    for c, moved in enumerate(columns):
        rows = (
            pltpu.roll(moved, PIX - SIDE, 1) * bottom,
            moved,
            pltpu.roll(moved, SIDE, 1) * top,
        )
        for a, piece in enumerate(rows):
            t = 3 * a + c
            stack_ref[t * CH : (t + 1) * CH, :] = piece


def pool_matrix():
    pixel = lax.broadcasted_iota(jnp.int32, (PIX, CELLS), 0)
    cell = lax.broadcasted_iota(jnp.int32, (PIX, CELLS), 1)
    square = ((pixel >> 6) << 4) + ((pixel & (SIDE - 1)) >> 1)
    return square == cell


def spread_matrix():
    cell = lax.broadcasted_iota(jnp.int32, (CELLS, PIX), 0)
    pixel = lax.broadcasted_iota(jnp.int32, (CELLS, PIX), 1)
    square = ((pixel >> 6) << 4) + ((pixel & (SIDE - 1)) >> 1)
    return (square == cell).astype(F32).astype(BF)


def times(high, low, right):
    right_high, right_low = split(right)
    return dot(high, right_high) + dot(high, right_low) + dot(low, right_high)


def tanh_of(state):
    return jnp.tanh(state.astype(F32))


def slope_of(act):
    return STEP * (1.0 - act * act)


def prep_kernel(filters_ref, matrix_ref):
    total = filters_ref[0, :, 0:CH].astype(F32)
    for t in range(1, TAPS):
        total += filters_ref[0, :, t * CH : (t + 1) * CH].astype(F32)
    row = lax.broadcasted_iota(jnp.int32, (CH, CH), 0)
    col = lax.broadcasted_iota(jnp.int32, (CH, CH), 1)
    base = jnp.where(row == col, KEEP, 0.0) + STEP * total
    high, low = split(dot(base, base, EXACT))
    matrix_ref[:, :CH] = high
    matrix_ref[:, CH:] = low


def fine_kernel(
    above_ref, terminal_ref, guess_ref, states_ref, filters_ref, matrix_ref, top_ref, pack_ref, stack_ref
):
    last = lax.axis_index("layer") == XS * YS - 1
    top = jnp.where(last, terminal_ref[...].astype(F32), above_ref[...].astype(F32))
    top_ref[...] = top.astype(BF)
    write_stack(top.astype(BF), stack_ref)
    below = KEEP * top + slope_of(tanh_of(states_ref[1])) * dot(filters_ref[1], stack_ref[...])
    below = below.astype(BF)
    write_stack(below, stack_ref)
    moved = slope_of(tanh_of(states_ref[0])) * dot(filters_ref[0], stack_ref[...])
    residual = KEEP * below.astype(F32) + moved - guess_ref[...].astype(F32)
    high, low = split(residual)
    pool = jnp.where(pool_matrix(), 0.25, 0.0).astype(BF)
    coarse = (dot(high, pool) + dot(low, pool)).astype(BF)
    matrix = matrix_ref[...]
    for j in range(XS):
        pack_ref[j, :, :CELLS] = coarse
        pack_ref[j, :, CELLS:] = matrix


def group_kernel(packs_ref, pack_ref):
    value = packs_ref[XS - 1, :, :CELLS].astype(F32)
    highs = [packs_ref[j, :, CELLS : CELLS + CH] for j in range(XS)]
    lows = [packs_ref[j, :, CELLS + CH :] for j in range(XS)]
    for j in range(XS - 2, -1, -1):
        value = times(highs[j], lows[j], value) + packs_ref[j, :, :CELLS].astype(F32)
    full = [highs[j].astype(F32) + lows[j].astype(F32) for j in range(XS)]
    group = dot(dot(full[0], full[1], EXACT), dot(full[2], full[3], EXACT), EXACT)
    value = value.astype(BF)
    high, low = split(group)
    for j in range(YS):
        pack_ref[j, :, :CELLS] = value
        pack_ref[j, :, CELLS : CELLS + CH] = high
        pack_ref[j, :, CELLS + CH :] = low


def correct_kernel(
    groups_ref, packs_hbm, top_hbm, guess_hbm, states_hbm, filters_hbm,
    adjoint_ref, keep_ref, send_ref,
    packs_ref, top_ref, guess_ref, states_ref, filters_ref, stack_ref, grad_scr, sems,
):
    copies = [
        pltpu.make_async_copy(source, target, sems.at[i])
        for i, (source, target) in enumerate((
            (packs_hbm, packs_ref),
            (top_hbm, top_ref),
            (guess_hbm.at[0], guess_ref),
            (filters_hbm.at[1], filters_ref),
            (states_hbm, states_ref),
        ))
    ]
    for copy in copies:
        copy.start()
    layer = lax.axis_index("layer")
    x, y = layer % XS, layer // XS
    upper = jnp.zeros((CH, CELLS), F32)
    for j in range(YS - 1, 0, -1):
        moved = times(groups_ref[j, :, CELLS : CELLS + CH], groups_ref[j, :, CELLS + CH :], upper)
        upper = jnp.where(j > y, moved + groups_ref[j, :, :CELLS].astype(F32), upper)
    copies[0].wait()
    own = upper
    for j in range(XS - 1, -1, -1):
        moved = times(packs_ref[j, :, CELLS : CELLS + CH], packs_ref[j, :, CELLS + CH :], upper)
        moved += packs_ref[j, :, :CELLS].astype(F32)
        own = jnp.where(x == j, moved, own)
        upper = jnp.where(j > x, moved, upper)
    spread = spread_matrix()

    def widen(error):
        high, low = split(error)
        return dot(high, spread) + dot(low, spread)

    nt = (((1,), (1,)), ((), ()))

    def gradient(l, act):
        grad = STEP * lax.dot_general(act.astype(BF), stack_ref[...], nt, preferred_element_type=F32)
        grad_scr[:, :, l] = grad.reshape(ZS, 2, 8, TAPS * CH)

    copies[1].wait()
    top = (top_ref[...].astype(F32) + widen(upper)).astype(BF)
    write_stack(top, stack_ref)
    copies[2].wait()
    copies[3].wait()
    copies[4].wait()
    act = tanh_of(states_ref[1])
    below = (KEEP * top.astype(F32) + slope_of(act) * dot(filters_ref[...], stack_ref[...])).astype(BF)
    gradient(1, act)
    adjoint_ref[0] = (guess_ref[...].astype(F32) + widen(own)).astype(BF)
    adjoint_ref[1] = below
    write_stack(below, stack_ref)
    gradient(0, tanh_of(states_ref[0]))
    core = lax.axis_index("dp") % 2
    keep_ref[...] = grad_scr[:, core].reshape(ZS, 16, TAPS * CH)
    send_ref[...] = grad_scr[:, 1 - core].reshape(ZS, 16, TAPS * CH).astype(BF)


def join_kernel(keep_ref, came_ref, sum_ref):
    sum_ref[...] = (keep_ref[...] + came_ref[...].astype(F32)).astype(BF)


def total_kernel(came_ref, grad_ref):
    total = came_ref[0].astype(F32)
    for z in range(1, ZS):
        total += came_ref[z].astype(F32)
    grad_ref[...] = total.reshape(2, 8, TAPS * CH)


def call(body, outs, scratch=(), flops=10**6, vmem=6, in_specs=None):
    outs = [jax.ShapeDtypeStruct(s, d) for s, d in outs]
    extra = {} if in_specs is None else {"in_specs": in_specs}
    return pl.pallas_call(
        body,
        out_shape=outs[0] if len(outs) == 1 else outs,
        scratch_shapes=list(scratch),
        compiler_params=pltpu.CompilerParams(vmem_limit_bytes=vmem << 20),
        cost_estimate=pl.CostEstimate(flops=flops, bytes_accessed=1 << 20, transcendentals=0),
        **extra,
    )


WIDTH = CELLS + 2 * CH
FIELD = (CH, PIX)
STACK = pltpu.VMEM((TAPS * CH, PIX), BF)
SHARE = (ZS, 16, TAPS * CH)
ANY = pl.BlockSpec(memory_space=pl.ANY)
prep = call(prep_kernel, [((CH, 2 * CH), BF)])
fine = call(fine_kernel, [(FIELD, BF), ((XS, CH, WIDTH), BF)], [STACK], 10**9, 16)
group_of = call(group_kernel, [((YS, CH, WIDTH), BF)])
correct = call(
    correct_kernel,
    [((2,) + FIELD, BF), (SHARE, F32), (SHARE, BF)],
    [
        pltpu.VMEM((XS, CH, WIDTH), BF),
        pltpu.VMEM(FIELD, BF),
        pltpu.VMEM(FIELD, BF),
        pltpu.VMEM((2,) + FIELD, BF),
        pltpu.VMEM((CH, TAPS * CH), BF),
        STACK,
        pltpu.VMEM((ZS, 2, 2, 8, TAPS * CH), F32),
        pltpu.SemaphoreType.DMA((5,)),
    ],
    2 * 10**9,
    24,
    [VMEM] + [ANY] * 5,
)
join = call(join_kernel, [(SHARE, BF)])
total_of = call(total_kernel, [((2, 8, TAPS * CH), F32)])


def per_device(states, filters, guess, terminal):
    states, guess, terminal = states[:, 0], guess[:, 0], terminal[0]
    x_groups = [[y * XS + x for x in range(XS)] for y in range(YS)]
    y_groups = [[y * XS + x for y in range(YS)] for x in range(XS)]
    z_groups = [[z * 2 + c for z in range(ZS)] for c in range(2)]

    def exchange(a, axis, groups):
        return lax.all_to_all(a, axis, 0, 0, axis_index_groups=groups)

    above = lax.ppermute(guess[0], "layer", [(i + 1, i) for i in range(XS * YS - 1)])
    matrix = prep(filters)
    top, pack = fine(above, terminal, guess[0], states, filters, matrix)
    packs = exchange(pack, "layer", x_groups)
    groups = exchange(group_of(packs), "layer", y_groups)
    adjoint, keep, send = correct(groups, packs, top, guess, states, filters)
    came = lax.ppermute(send, "dp", [(i ^ 1, i) for i in range(2 * ZS)])
    shares = exchange(join(keep, came), "dp", z_groups)
    return adjoint[:, None], total_of(shares)


def solution(mesh):
    return jax.shard_map(
        per_device,
        mesh=mesh,
        in_specs=(
            P("layer", "dp", None, None),
            P("layer", None, None),
            P("layer", "dp", None, None),
            P("dp", None, None),
        ),
        out_specs=(P("layer", "dp", None, None), P("layer", "dp", None)),
        check_vma=False,
    )
```

time: 103 us -> 98 us (0.951)
  blocking collectives: 22 us -> 69.9 us
  waiting for transfers between devices: 31 us -> 6.26 us
  starting transfers between devices: 29.7 us -> 7.43 us
  local copies, waits for them, and re-layouts: 5.96 us -> 3.05 us
  Pallas kernels: 13.3 us -> 10.4 us
    all_to_all x1 -> x3, blocking collectives: 22 us -> 69.9 us  [exchange(): return lax.all_to_all(a, axis, 0, 0, axis_index_groups=groups)]
    all_to_all x4 -> x0, waiting for transfers between devices: 29.8 us -> none  [exchange(): return lax.all_to_all(a, axis, 0, 0, axis_index_groups=groups)]
    all_to_all x4 -> x0, starting transfers between devices: 21.1 us -> none  [exchange(): return lax.all_to_all(a, axis, 0, 0, axis_index_groups=groups)]
    ppermute x1, waiting for transfers between devices: 0.01 us -> 5.07 us  [per_device(): lax.ppermute(guess[0], 'layer', [(i + 1, i) for i in range(XS * YS - 1)])]
    pallas_call x6 -> x4, Pallas kernels: 12.5 us -> 9.64 us  [the longest x1 6 us: per_device(): adjoint, keep, send = correct(groups, packs, top, guess, states, filters)]
    unnamed x18 -> x10, local copies, waits for them, and re-layouts: 3.94 us -> 2.02 us
    ppermute x1, starting transfers between devices: 7.31 us -> 6.13 us  [per_device(): came = lax.ppermute(send, 'dp', [(i ^ 1, i) for i in range(2 * ZS)])]
  transfers between devices with their start and end apart: 6 -> 2, of which waited for: 5 -> 2; matrix products, arithmetic and copies ran while one was open for 1% -> 0% of each run, Pallas kernels for 9% -> 0%
where the time goes in v2:
time: 98 us; the launch traced here: 97.7 us
  blocking collectives  69.9 us (71%)
  Pallas kernels  10.4 us (11%)
  starting transfers between devices  7.43 us (8%)
  waiting for transfers between devices  6.26 us (6%)
  local copies, waits for them, and re-layouts  3.05 us (3%)
    all_to_all x3, blocking collectives, exchange(): return lax.all_to_all(a, axis, 0, 0, axis_index_groups=groups)  69.9 us
    ppermute x1, starting transfers between devices, per_device(): came = lax.ppermute(send, 'dp', [(i ^ 1, i) for i in range(2 * ZS)])  6.13 us
    pallas_call x1, Pallas kernels, per_device(): adjoint, keep, send = correct(groups, packs, top, guess, states, filters)  6 us
    ppermute x1, waiting for transfers between devices, per_device(): lax.ppermute(guess[0], 'layer', [(i + 1, i) for i in range(XS * YS - 1)])  5.07 us
    pallas_call x1, Pallas kernels, per_device(): top, pack = fine(above, terminal, guess[0], states, filters, matrix)  2.32 us
    unnamed x10, local copies, waits for them, and re-layouts  2.02 us
  transfers between devices with their start and end apart: 2, of which 2 were waited for; matrix products, arithmetic and copies ran while one was open for 0% of the time, Pallas kernels for 0%

profile of v2, /device:TPU:1, one launch (start us, length us, event | category | flops | bytes accessed | tf_op | source)
XLA Modules:
  0.0 97.7 jit_solution(3838314615113485953)
XLA Ops:
  0.6 0.0 copy-start.3
  0.6 1.0 %slice_bitcast_fusion.guess_ref = bf16[128,1024]{1,0:T(8,128)(2,1)S(1)} fusion(bf16[2,1,128,1024]{3,2,1,0:T(8,128)(2,1)} %param.6), kind=kLoop, calls=%fused_computation | loop fusion | bytes 524288 | tf_op jit(solution)/shard_map/squeeze | solution.py:249
  1.7 1.3 %collective-permute-start = (bf16[128,1024]{1,0:T(8,128)(2,1)S(1)}, bf16[128,1024]{1,0:T(8,128)(2,1)S(1)}, u32[]{:S(2)}, u32[]{:S(2)}) collective-permute-start(bf16[128,1024]{1,0:T(8,128)(2,1)S(1)} %slice_bitcast_fusion.guess_ref), channel_id=1, source_target_pairs={{16,0},{32,16},{48,32},{64,48},{80,64},{96,80},{112,96},{128,112},... | collective-permute-start | bytes 786440 | tf_op jit(solution)/shard_map/ppermute | solution.py:249
  3.0 0.0 copy-start
  3.0 1.1 %copy-done = bf16[2,128,1152]{2,1,0:T(8,128)(2,1)S(1)} copy-done((bf16[2,128,1152]{2,1,0:T(8,128)(2,1)S(1)}, bf16[2,128,1152]{2,1,0:T(8,128)(2,1)}, u32[]{:S(2)}) %copy-start) | copy-done | bytes 589848
  4.0 0.0 copy-start.1
  4.0 0.2 shard_map.59.matrix_ref
  4.3 5.1 %collective-permute-done.above_ref = bf16[128,1024]{1,0:T(8,128)(2,1)S(1)} collective-permute-done((bf16[128,1024]{1,0:T(8,128)(2,1)S(1)}, bf16[128,1024]{1,0:T(8,128)(2,1)S(1)}, u32[]{:S(2)}, u32[]{:S(2)}) %collective-permute-start) | collective-permute-done | bytes 262176 | tf_op jit(solution)/shard_map/ppermute | solution.py:249
  9.4 0.0 copy-done.3
  9.4 0.0 copy-done.1
  9.4 0.0 copy-start.4
  9.4 0.9 copy-done.4
  10.3 2.3 %shard_map.60 = (bf16[128,1024]{1,0:T(8,128)(2,1)S(1)}, bf16[4,128,512]{2,1,0:T(8,128)(2,1)S(1)}) custom-call(bf16[128,1024]{1,0:T(8,128)(2,1)S(1)} %collective-permute-done.above_ref, bf16[128,1024]{1,0:T(8,128)(2,1)S(1)} %bitcast.11, bf16[128,1024]{1,0:T(8,128)(2,1)S(1)} %slice_bitcast_fusion.guess_ref, bf16[2,128,1024]{2,1,0:T(8,128)(2,1)S(1)} %bitcast.9, ...), custom_call_target="tpu_custom_call" | custom-call | flops 1000000000 | bytes 1048576 | tf_op jit(solution)/shard_map/pallas_call | solution.py:251
  12.6 15.5 %all_to_all.15.packs_ref.packs_hbm = bf16[4,128,512]{2,1,0:T(8,128)(2,1)S(1)} all-to-all(bf16[4,128,512]{2,1,0:T(8,128)(2,1)S(1)} %get-tuple-element.7), channel_id=1, replica_groups={{0,16,32,48},{64,80,96,112},{128,144,160,176},{192,208,224,240},{256,27..., dimensions={0} | all-to-all | bytes 1048576 | tf_op jit(solution)/shard_map/all_to_all | solution.py:247
  28.1 1.1 %shard_map.61 = bf16[8,128,512]{2,1,0:T(8,128)(2,1)S(1)} custom-call(bf16[4,128,512]{2,1,0:T(8,128)(2,1)S(1)} %all_to_all.15.packs_ref.packs_hbm), custom_call_target="tpu_custom_call" | custom-call | flops 1000000 | bytes 1048576 | tf_op jit(solution)/shard_map/pallas_call | solution.py:253
  29.2 0.0 copy-start.2
  29.2 32.4 %all_to_all.16.groups_ref = bf16[8,128,512]{2,1,0:T(8,128)(2,1)S(1)} all-to-all(bf16[8,128,512]{2,1,0:T(8,128)(2,1)S(1)} %shard_map.61), channel_id=1, replica_groups={{0,64,128,192,256,320,384,448},{16,80,144,208,272,336,400,464},{32,96,1..., dimensions={0} | all-to-all | bytes 2097152 | tf_op jit(solution)/shard_map/all_to_all | solution.py:247
  61.6 0.0 copy-done.2
  61.6 6.0 %shard_map.62 = (bf16[2,128,1024]{2,1,0:T(8,128)(2,1)}, f32[8,16,1152]{2,1,0:T(8,128)S(1)}, bf16[8,16,1152]{2,1,0:T(8,128)(2,1)S(1)}) custom-call(bf16[8,128,512]{2,1,0:T(8,128)(2,1)S(1)} %all_to_all.16.groups_ref, bf16[4,128,512]{2,1,0:T(8,128)(2,1)S(1)} %all_to_all.15.packs_ref.packs_hbm, bf16[128,1024]{1,0:T(8,128)(2,1)S(1)} %get-tuple-element.8.top_hbm, ...), custom_call_target="tpu_custom_call" | custom-call | flops 2000000000 | bytes 1048576 | tf_op jit(solution)/shard_map/pallas_call | solution.py:254
  67.6 6.1 %collective-permute-start.1 = (bf16[8,16,1152]{2,1,0:T(8,128)(2,1)S(1)}, bf16[8,16,1152]{2,1,0:T(8,128)(2,1)S(1)}, u32[]{:S(2)}, u32[]{:S(2)}) collective-permute-start(bf16[8,16,1152]{2,1,0:T(8,128)(2,1)S(1)} %get-tuple-element.11), channel_id=1, source_target_pairs={{1,0},{0,1},{3,2},{2,3},{5,4},{4,5},{7,6},{6,7},{9,8},{8,9},{11,10... | collective-permute-start | bytes 884744 | tf_op jit(solution)/shard_map/ppermute | solution.py:255
  73.7 1.2 %collective-permute-done.1.came_ref = bf16[8,16,1152]{2,1,0:T(8,128)(2,1)S(1)} collective-permute-done((bf16[8,16,1152]{2,1,0:T(8,128)(2,1)S(1)}, bf16[8,16,1152]{2,1,0:T(8,128)(2,1)S(1)}, u32[]{:S(2)}, u32[]{:S(2)}) %collective-permute-start.1) | collective-permute-done | bytes 294944 | tf_op jit(solution)/shard_map/ppermute | solution.py:255
  74.9 0.1 shard_map.63
  75.0 22.0 %all_to_all.17.came_ref = bf16[8,16,1152]{2,1,0:T(8,128)(2,1)S(1)} all-to-all(bf16[8,16,1152]{2,1,0:T(8,128)(2,1)S(1)} %shard_map.63), channel_id=1, replica_groups={{0,2,4,6,8,10,12,14},{1,3,5,7,9,11,13,15},{16,18,20,22,24,26,28,30},{17..., dimensions={0} | all-to-all | bytes 589824 | tf_op jit(solution)/shard_map/all_to_all | solution.py:247
  97.0 0.7 shard_map.64
Async XLA Ops:
  0.6 8.7 %copy-start.3 = (bf16[2,1,128,1024]{3,2,1,0:T(8,128)(2,1)S(1)}, bf16[2,1,128,1024]{3,2,1,0:T(8,128)(2,1)}, u32[]{:S(2)}) copy-start(bf16[2,1,128,1024]{3,2,1,0:T(8,128)(2,1)} %param.4) | copy-start | bytes 1572868
  1.7 7.7 %collective-permute-start = (bf16[128,1024]{1,0:T(8,128)(2,1)S(1)}, bf16[128,1024]{1,0:T(8,128)(2,1)S(1)}, u32[]{:S(2)}, u32[]{:S(2)}) collective-permute-start(bf16[128,1024]{1,0:T(8,128)(2,1)S(1)} %slice_bitcast_fusion.guess_ref), channel_id=1, source_target_pairs={{16,0},{32,16},{48,32},{64,48},{80,64},{96,80},{112,96},{128,112},... | collective-permute-start | bytes 786440 | tf_op jit(solution)/shard_map/ppermute | solution.py:249
  3.0 1.1 %copy-start = (bf16[2,128,1152]{2,1,0:T(8,128)(2,1)S(1)}, bf16[2,128,1152]{2,1,0:T(8,128)(2,1)}, u32[]{:S(2)}) copy-start(bf16[2,128,1152]{2,1,0:T(8,128)(2,1)} %filters_hbm.1) | copy-start | bytes 1769476
  4.0 5.3 %copy-start.1 = (bf16[2,128,1152]{2,1,0:T(8,128)(2,1)S(1)}, bf16[2,128,1152]{2,1,0:T(8,128)(2,1)}, u32[]{:S(2)}) copy-start(bf16[2,128,1152]{2,1,0:T(8,128)(2,1)} %filters_hbm.1) | copy-start | bytes 1769476
  9.4 1.0 copy-start.4
  29.2 32.4 %copy-start.2 = (bf16[2,1,128,1024]{3,2,1,0:T(8,128)(2,1)S(1)}, bf16[2,1,128,1024]{3,2,1,0:T(8,128)(2,1)}, u32[]{:S(2)}) copy-start(bf16[2,1,128,1024]{3,2,1,0:T(8,128)(2,1)} %param.6) | copy-start | bytes 1572868
  67.6 7.3 %collective-permute-start.1 = (bf16[8,16,1152]{2,1,0:T(8,128)(2,1)S(1)}, bf16[8,16,1152]{2,1,0:T(8,128)(2,1)S(1)}, u32[]{:S(2)}, u32[]{:S(2)}) collective-permute-start(bf16[8,16,1152]{2,1,0:T(8,128)(2,1)S(1)} %get-tuple-element.11), channel_id=1, source_target_pairs={{1,0},{0,1},{3,2},{2,3},{5,4},{4,5},{7,6},{6,7},{9,8},{8,9},{11,10... | collective-permute-start | bytes 884744 | tf_op jit(solution)/shard_map/ppermute | solution.py:255

commit v3 on v2

--- a/solution.py
+++ b/solution.py
@@ -62,9 +62,22 @@
     return (square == cell).astype(F32).astype(BF)
 
 
-def times(high, low, right):
-    right_high, right_low = split(right)
-    return dot(high, right_high) + dot(high, right_low) + dot(low, right_high)
+def identity():
+    row = lax.broadcasted_iota(jnp.int32, (CH, CH), 0)
+    return jnp.where(row == lax.broadcasted_iota(jnp.int32, (CH, CH), 1), 1.0, 0.0)
+
+
+def rounded(part):
+    row = lax.broadcasted_iota(jnp.int32, (CH, CH), 0).astype(F32)
+    col = lax.broadcasted_iota(jnp.int32, (CH, CH), 1).astype(F32)
+    place = row * 0.7548776662 + col * 0.5698402910
+    offset = place - jnp.floor(place) - 0.5
+    return (part + part * offset * 0.00546875).astype(BF)
+
+
+def times(scale, part, right):
+    high, low = split(right)
+    return scale * right + (dot(part, high) + dot(part, low))
 
 
 def tanh_of(state):
@@ -75,25 +88,26 @@
     return STEP * (1.0 - act * act)
 
 
-def prep_kernel(filters_ref, matrix_ref):
+def prep_kernel(filters_ref, terminal_ref, matrix_ref, ending_ref):
     total = filters_ref[0, :, 0:CH].astype(F32)
     for t in range(1, TAPS):
         total += filters_ref[0, :, t * CH : (t + 1) * CH].astype(F32)
-    row = lax.broadcasted_iota(jnp.int32, (CH, CH), 0)
-    col = lax.broadcasted_iota(jnp.int32, (CH, CH), 1)
-    base = jnp.where(row == col, KEEP, 0.0) + STEP * total
-    high, low = split(dot(base, base, EXACT))
-    matrix_ref[:, :CH] = high
-    matrix_ref[:, CH:] = low
+    total *= STEP
+    matrix_ref[...] = rounded((2.0 * KEEP) * total + dot(total, total, EXACT))
+    ending_ref[...] = terminal_ref[...]
 
 
 def fine_kernel(
-    above_ref, terminal_ref, guess_ref, states_ref, filters_ref, matrix_ref, top_ref, pack_ref, stack_ref
+    above_ref, terminal_ref, guess_ref, states_hbm, filters_ref, matrix_ref,
+    top_ref, pack_ref, states_ref, stack_ref, sem,
 ):
+    fetch = pltpu.make_async_copy(states_hbm, states_ref, sem)
+    fetch.start()
     last = lax.axis_index("layer") == XS * YS - 1
     top = jnp.where(last, terminal_ref[...].astype(F32), above_ref[...].astype(F32))
     top_ref[...] = top.astype(BF)
     write_stack(top.astype(BF), stack_ref)
+    fetch.wait()
     below = KEEP * top + slope_of(tanh_of(states_ref[1])) * dot(filters_ref[1], stack_ref[...])
     below = below.astype(BF)
     write_stack(below, stack_ref)
@@ -109,19 +123,18 @@
 
 
 def group_kernel(packs_ref, pack_ref):
+    parts = [packs_ref[j, :, CELLS:] for j in range(XS)]
     value = packs_ref[XS - 1, :, :CELLS].astype(F32)
-    highs = [packs_ref[j, :, CELLS : CELLS + CH] for j in range(XS)]
-    lows = [packs_ref[j, :, CELLS + CH :] for j in range(XS)]
     for j in range(XS - 2, -1, -1):
-        value = times(highs[j], lows[j], value) + packs_ref[j, :, :CELLS].astype(F32)
-    full = [highs[j].astype(F32) + lows[j].astype(F32) for j in range(XS)]
+        value = times(KEEP**2, parts[j], value) + packs_ref[j, :, :CELLS].astype(F32)
+    one = identity()
+    full = [KEEP**2 * one + part.astype(F32) for part in parts]
     group = dot(dot(full[0], full[1], EXACT), dot(full[2], full[3], EXACT), EXACT)
     value = value.astype(BF)
-    high, low = split(group)
+    part = rounded(group - KEEP**8 * one)
     for j in range(YS):
         pack_ref[j, :, :CELLS] = value
-        pack_ref[j, :, CELLS : CELLS + CH] = high
-        pack_ref[j, :, CELLS + CH :] = low
+        pack_ref[j, :, CELLS:] = part
 
 
 def correct_kernel(
@@ -145,12 +158,12 @@
     x, y = layer % XS, layer // XS
     upper = jnp.zeros((CH, CELLS), F32)
     for j in range(YS - 1, 0, -1):
-        moved = times(groups_ref[j, :, CELLS : CELLS + CH], groups_ref[j, :, CELLS + CH :], upper)
+        moved = times(KEEP**8, groups_ref[j, :, CELLS:], upper)
         upper = jnp.where(j > y, moved + groups_ref[j, :, :CELLS].astype(F32), upper)
     copies[0].wait()
     own = upper
     for j in range(XS - 1, -1, -1):
-        moved = times(packs_ref[j, :, CELLS : CELLS + CH], packs_ref[j, :, CELLS + CH :], upper)
+        moved = times(KEEP**2, packs_ref[j, :, CELLS:], upper)
         moved += packs_ref[j, :, :CELLS].astype(F32)
         own = jnp.where(x == j, moved, own)
         upper = jnp.where(j > x, moved, upper)
@@ -208,13 +221,20 @@
     )
 
 
-WIDTH = CELLS + 2 * CH
+WIDTH = CELLS + CH
 FIELD = (CH, PIX)
 STACK = pltpu.VMEM((TAPS * CH, PIX), BF)
 SHARE = (ZS, 16, TAPS * CH)
 ANY = pl.BlockSpec(memory_space=pl.ANY)
-prep = call(prep_kernel, [((CH, 2 * CH), BF)])
-fine = call(fine_kernel, [(FIELD, BF), ((XS, CH, WIDTH), BF)], [STACK], 10**9, 16)
+prep = call(prep_kernel, [((CH, CH), BF), (FIELD, BF)])
+fine = call(
+    fine_kernel,
+    [(FIELD, BF), ((XS, CH, WIDTH), BF)],
+    [pltpu.VMEM((2,) + FIELD, BF), STACK, pltpu.SemaphoreType.DMA(())],
+    10**9,
+    16,
+    [VMEM] * 3 + [ANY] + [VMEM] * 2,
+)
 group_of = call(group_kernel, [((YS, CH, WIDTH), BF)])
 correct = call(
     correct_kernel,
@@ -247,8 +267,8 @@
         return lax.all_to_all(a, axis, 0, 0, axis_index_groups=groups)
 
     above = lax.ppermute(guess[0], "layer", [(i + 1, i) for i in range(XS * YS - 1)])
-    matrix = prep(filters)
-    top, pack = fine(above, terminal, guess[0], states, filters, matrix)
+    matrix, ending = prep(filters, terminal)
+    top, pack = fine(above, ending, guess[0], states, filters, matrix)
     packs = exchange(pack, "layer", x_groups)
     groups = exchange(group_of(packs), "layer", y_groups)
     adjoint, keep, send = correct(groups, packs, top, guess, states, filters)

time: 98 us -> 90.8 us (0.927)
  blocking collectives: 69.9 us -> 62 us
    all_to_all x3, blocking collectives: 69.9 us -> 62 us  [exchange(): return lax.all_to_all(a, axis, 0, 0, axis_index_groups=groups)]
    unnamed x10 -> x12, local copies, waits for them, and re-layouts: 2.02 us -> 2.12 us
where the time goes in v3:
time: 90.8 us; the launch traced here: 90.4 us
  blocking collectives  62 us (68%)
  Pallas kernels  10.2 us (11%)
  starting transfers between devices  8.16 us (9%)
  waiting for transfers between devices  6.26 us (7%)
  local copies, waits for them, and re-layouts  3.13 us (3%)
    all_to_all x3, blocking collectives, exchange(): return lax.all_to_all(a, axis, 0, 0, axis_index_groups=groups)  62 us
    ppermute x1, starting transfers between devices, per_device(): came = lax.ppermute(send, 'dp', [(i ^ 1, i) for i in range(2 * ZS)])  6.87 us
    pallas_call x1, Pallas kernels, per_device(): adjoint, keep, send = correct(groups, packs, top, guess, states, filters)  5.86 us
    ppermute x1, waiting for transfers between devices, per_device(): lax.ppermute(guess[0], 'layer', [(i + 1, i) for i in range(XS * YS - 1)])  5.07 us
    pallas_call x1, Pallas kernels, per_device(): top, pack = fine(above, ending, guess[0], states, filters, matrix)  2.41 us
    unnamed x12, local copies, waits for them, and re-layouts  2.12 us
  transfers between devices with their start and end apart: 2, of which 2 were waited for; matrix products, arithmetic and copies ran while one was open for 0% of the time, Pallas kernels for 0%

profile of v3, /device:TPU:1, one launch (start us, length us, event | category | flops | bytes accessed | tf_op | source)
XLA Modules:
  0.0 90.4 jit_solution(14798287374954649995)
XLA Ops:
  0.6 0.0 copy-start.2
  0.6 1.0 %slice_bitcast_fusion.guess_ref = bf16[128,1024]{1,0:T(8,128)(2,1)S(1)} fusion(bf16[2,1,128,1024]{3,2,1,0:T(8,128)(2,1)} %param.6), kind=kLoop, calls=%fused_computation | loop fusion | bytes 524288 | tf_op jit(solution)/shard_map/squeeze | solution.py:269
  1.7 1.3 %collective-permute-start = (bf16[128,1024]{1,0:T(8,128)(2,1)S(1)}, bf16[128,1024]{1,0:T(8,128)(2,1)S(1)}, u32[]{:S(2)}, u32[]{:S(2)}) collective-permute-start(bf16[128,1024]{1,0:T(8,128)(2,1)S(1)} %slice_bitcast_fusion.guess_ref), channel_id=1, source_target_pairs={{16,0},{32,16},{48,32},{64,48},{80,64},{96,80},{112,96},{128,112},... | collective-permute-start | bytes 786440 | tf_op jit(solution)/shard_map/ppermute | solution.py:269
  3.0 0.0 copy-done.2
  3.0 0.0 copy-start
  3.0 1.1 %copy-done = bf16[2,128,1152]{2,1,0:T(8,128)(2,1)S(1)} copy-done((bf16[2,128,1152]{2,1,0:T(8,128)(2,1)S(1)}, bf16[2,128,1152]{2,1,0:T(8,128)(2,1)}, u32[]{:S(2)}) %copy-start) | copy-done | bytes 589848
  4.0 0.0 copy-start.1
  4.0 0.2 shard_map.59
  4.3 5.1 %collective-permute-done.above_ref = bf16[128,1024]{1,0:T(8,128)(2,1)S(1)} collective-permute-done((bf16[128,1024]{1,0:T(8,128)(2,1)S(1)}, bf16[128,1024]{1,0:T(8,128)(2,1)S(1)}, u32[]{:S(2)}, u32[]{:S(2)}) %collective-permute-start) | collective-permute-done | bytes 262176 | tf_op jit(solution)/shard_map/ppermute | solution.py:269
  9.3 0.0 copy-done.1
  9.3 0.0 copy-start.4
  9.4 1.0 %copy-done.4 = bf16[2,1,128,1024]{3,2,1,0:T(8,128)(2,1)S(1)} copy-done((bf16[2,1,128,1024]{3,2,1,0:T(8,128)(2,1)S(1)}, bf16[2,1,128,1024]{3,2,1,0:T(8,128)(2,1)}, u32[]{:S(2)}) %copy-start.4) | copy-done | bytes 524312
  10.4 2.4 %shard_map.60 = (bf16[128,1024]{1,0:T(8,128)(2,1)S(1)}, bf16[4,128,384]{2,1,0:T(8,128)(2,1)S(1)}) custom-call(bf16[128,1024]{1,0:T(8,128)(2,1)S(1)} %collective-permute-done.above_ref, bf16[128,1024]{1,0:T(8,128)(2,1)S(1)} %get-tuple-element.9.terminal_ref, bf16[128,1024]{1,0:T(8,128)(2,1)S(1)} %slice_bitcast_fusion.guess_ref, ...), custom_call_target="tpu_custom_call" | custom-call | flops 1000000000 | bytes 1048576 | tf_op jit(solution)/shard_map/pallas_call | solution.py:271
  12.8 14.1 %all_to_all.15.packs_ref.packs_hbm = bf16[4,128,384]{2,1,0:T(8,128)(2,1)S(1)} all-to-all(bf16[4,128,384]{2,1,0:T(8,128)(2,1)S(1)} %get-tuple-element.11), channel_id=1, replica_groups={{0,16,32,48},{64,80,96,112},{128,144,160,176},{192,208,224,240},{256,27..., dimensions={0} | all-to-all | bytes 786432 | tf_op jit(solution)/shard_map/all_to_all | solution.py:267
  26.9 0.9 %shard_map.61 = bf16[8,128,384]{2,1,0:T(8,128)(2,1)S(1)} custom-call(bf16[4,128,384]{2,1,0:T(8,128)(2,1)S(1)} %all_to_all.15.packs_ref.packs_hbm), custom_call_target="tpu_custom_call" | custom-call | flops 1000000 | bytes 1048576 | tf_op jit(solution)/shard_map/pallas_call | solution.py:273
  27.8 0.0 copy-start.3
  27.9 0.0 copy-start.5
  27.9 25.9 %all_to_all.16.groups_ref = bf16[8,128,384]{2,1,0:T(8,128)(2,1)S(1)} all-to-all(bf16[8,128,384]{2,1,0:T(8,128)(2,1)S(1)} %shard_map.61), channel_id=1, replica_groups={{0,64,128,192,256,320,384,448},{16,80,144,208,272,336,400,464},{32,96,1..., dimensions={0} | all-to-all | bytes 1572864 | tf_op jit(solution)/shard_map/all_to_all | solution.py:267
  53.7 0.0 copy-done.3
  53.7 0.0 copy-done.5
  53.7 5.9 %shard_map.62 = (bf16[2,128,1024]{2,1,0:T(8,128)(2,1)}, f32[8,16,1152]{2,1,0:T(8,128)S(1)}, bf16[8,16,1152]{2,1,0:T(8,128)(2,1)S(1)}) custom-call(bf16[8,128,384]{2,1,0:T(8,128)(2,1)S(1)} %all_to_all.16.groups_ref, bf16[4,128,384]{2,1,0:T(8,128)(2,1)S(1)} %all_to_all.15.packs_ref.packs_hbm, bf16[128,1024]{1,0:T(8,128)(2,1)S(1)} %get-tuple-element.12.top_hbm, ...), custom_call_target="tpu_custom_call" | custom-call | flops 2000000000 | bytes 1048576 | tf_op jit(solution)/shard_map/pallas_call | solution.py:274
  59.6 6.9 %collective-permute-start.1 = (bf16[8,16,1152]{2,1,0:T(8,128)(2,1)S(1)}, bf16[8,16,1152]{2,1,0:T(8,128)(2,1)S(1)}, u32[]{:S(2)}, u32[]{:S(2)}) collective-permute-start(bf16[8,16,1152]{2,1,0:T(8,128)(2,1)S(1)} %get-tuple-element.15), channel_id=1, source_target_pairs={{1,0},{0,1},{3,2},{2,3},{5,4},{4,5},{7,6},{6,7},{9,8},{8,9},{11,10... | collective-permute-start | bytes 884744 | tf_op jit(solution)/shard_map/ppermute | solution.py:275
  66.5 1.2 %collective-permute-done.1.came_ref = bf16[8,16,1152]{2,1,0:T(8,128)(2,1)S(1)} collective-permute-done((bf16[8,16,1152]{2,1,0:T(8,128)(2,1)S(1)}, bf16[8,16,1152]{2,1,0:T(8,128)(2,1)S(1)}, u32[]{:S(2)}, u32[]{:S(2)}) %collective-permute-start.1) | collective-permute-done | bytes 294944 | tf_op jit(solution)/shard_map/ppermute | solution.py:275
  67.7 0.1 shard_map.63
  67.7 22.0 %all_to_all.17.came_ref = bf16[8,16,1152]{2,1,0:T(8,128)(2,1)S(1)} all-to-all(bf16[8,16,1152]{2,1,0:T(8,128)(2,1)S(1)} %shard_map.63), channel_id=1, replica_groups={{0,2,4,6,8,10,12,14},{1,3,5,7,9,11,13,15},{16,18,20,22,24,26,28,30},{17..., dimensions={0} | all-to-all | bytes 589824 | tf_op jit(solution)/shard_map/all_to_all | solution.py:267
  89.7 0.7 shard_map.64
Async XLA Ops:
  0.6 2.3 %copy-start.2 = (bf16[1,128,1024]{2,1,0:T(8,128)(2,1)S(1)}, bf16[1,128,1024]{2,1,0:T(8,128)(2,1)}, u32[]{:S(2)}) copy-start(bf16[1,128,1024]{2,1,0:T(8,128)(2,1)} %param.7) | copy-start | bytes 786436
  1.7 7.7 %collective-permute-start = (bf16[128,1024]{1,0:T(8,128)(2,1)S(1)}, bf16[128,1024]{1,0:T(8,128)(2,1)S(1)}, u32[]{:S(2)}, u32[]{:S(2)}) collective-permute-start(bf16[128,1024]{1,0:T(8,128)(2,1)S(1)} %slice_bitcast_fusion.guess_ref), channel_id=1, source_target_pairs={{16,0},{32,16},{48,32},{64,48},{80,64},{96,80},{112,96},{128,112},... | collective-permute-start | bytes 786440 | tf_op jit(solution)/shard_map/ppermute | solution.py:269
  3.0 1.1 %copy-start = (bf16[2,128,1152]{2,1,0:T(8,128)(2,1)S(1)}, bf16[2,128,1152]{2,1,0:T(8,128)(2,1)}, u32[]{:S(2)}) copy-start(bf16[2,128,1152]{2,1,0:T(8,128)(2,1)} %filters_hbm.1) | copy-start | bytes 1769476
  4.0 5.3 %copy-start.1 = (bf16[2,128,1152]{2,1,0:T(8,128)(2,1)S(1)}, bf16[2,128,1152]{2,1,0:T(8,128)(2,1)}, u32[]{:S(2)}) copy-start(bf16[2,128,1152]{2,1,0:T(8,128)(2,1)} %filters_hbm.1) | copy-start | bytes 1769476
  9.3 1.0 %copy-start.4 = (bf16[2,1,128,1024]{3,2,1,0:T(8,128)(2,1)S(1)}, bf16[2,1,128,1024]{3,2,1,0:T(8,128)(2,1)}, u32[]{:S(2)}) copy-start(bf16[2,1,128,1024]{3,2,1,0:T(8,128)(2,1)} %param.4) | copy-start | bytes 1572868
  27.8 25.9 %copy-start.3 = (bf16[2,1,128,1024]{3,2,1,0:T(8,128)(2,1)S(1)}, bf16[2,1,128,1024]{3,2,1,0:T(8,128)(2,1)}, u32[]{:S(2)}) copy-start(bf16[2,1,128,1024]{3,2,1,0:T(8,128)(2,1)} %param.6) | copy-start | bytes 1572868
  27.9 25.9 %copy-start.5 = (bf16[2,1,128,1024]{3,2,1,0:T(8,128)(2,1)S(1)}, bf16[2,1,128,1024]{3,2,1,0:T(8,128)(2,1)}, u32[]{:S(2)}) copy-start(bf16[2,1,128,1024]{3,2,1,0:T(8,128)(2,1)} %param.4) | copy-start | bytes 1572868
  59.6 8.1 %collective-permute-start.1 = (bf16[8,16,1152]{2,1,0:T(8,128)(2,1)S(1)}, bf16[8,16,1152]{2,1,0:T(8,128)(2,1)S(1)}, u32[]{:S(2)}, u32[]{:S(2)}) collective-permute-start(bf16[8,16,1152]{2,1,0:T(8,128)(2,1)S(1)} %get-tuple-element.15), channel_id=1, source_target_pairs={{1,0},{0,1},{3,2},{2,3},{5,4},{4,5},{7,6},{6,7},{9,8},{8,9},{11,10... | collective-permute-start | bytes 884744 | tf_op jit(solution)/shard_map/ppermute | solution.py:275

commit v4 on v3

v4 whole, which is shorter than its diff:
```python
import functools

import jax
import jax.numpy as jnp
from jax import lax
from jax.experimental import pallas as pl
from jax.experimental.pallas import tpu as pltpu
from jax.sharding import PartitionSpec as P

STEP = 0.0625
KEEP = 1.0 - STEP
SIDE, PIX, CH, TAPS = 32, 1024, 128, 9
HALF = SIDE // 2
CELLS = HALF * HALF
XS, YS, ZS = 4, 8, 8
BF, F32 = jnp.bfloat16, jnp.float32
EXACT = lax.Precision.HIGHEST
VMEM = pl.BlockSpec(memory_space=pltpu.VMEM)


def dot(a, b, precision=None):
    return jnp.dot(a, b, preferred_element_type=F32, precision=precision)


def split(a):
    high = a.astype(BF)
    return high, (a - high.astype(F32)).astype(BF)


def write_stack(field, stack_ref):
    lane = lax.broadcasted_iota(jnp.int32, (1, PIX), 1)
    col = lane & (SIDE - 1)
    first, last = (col != 0).astype(BF), (col != SIDE - 1).astype(BF)
    top, bottom = (lane >= SIDE).astype(BF), (lane < PIX - SIDE).astype(BF)
    columns = (
        pltpu.roll(field, PIX - 1, 1) * last,
        field,
        pltpu.roll(field, 1, 1) * first,
    )
    for c, moved in enumerate(columns):
        rows = (
            pltpu.roll(moved, PIX - SIDE, 1) * bottom,
            moved,
            pltpu.roll(moved, SIDE, 1) * top,
        )
        for a, piece in enumerate(rows):
            t = 3 * a + c
            stack_ref[t * CH : (t + 1) * CH, :] = piece


def pool_matrix():
    pixel = lax.broadcasted_iota(jnp.int32, (PIX, CELLS), 0)
    cell = lax.broadcasted_iota(jnp.int32, (PIX, CELLS), 1)
    square = ((pixel >> 6) << 4) + ((pixel & (SIDE - 1)) >> 1)
    return square == cell


def spread_matrix():
    cell = lax.broadcasted_iota(jnp.int32, (CELLS, PIX), 0)
    pixel = lax.broadcasted_iota(jnp.int32, (CELLS, PIX), 1)
    square = ((pixel >> 6) << 4) + ((pixel & (SIDE - 1)) >> 1)
    return (square == cell).astype(F32).astype(BF)


def identity():
    row = lax.broadcasted_iota(jnp.int32, (CH, CH), 0)
    return jnp.where(row == lax.broadcasted_iota(jnp.int32, (CH, CH), 1), 1.0, 0.0)


def rounded(part):
    row = lax.broadcasted_iota(jnp.int32, (CH, CH), 0).astype(F32)
    col = lax.broadcasted_iota(jnp.int32, (CH, CH), 1).astype(F32)
    place = row * 0.7548776662 + col * 0.5698402910
    offset = place - jnp.floor(place) - 0.5
    return (part + part * offset * 0.00546875).astype(BF)


def times(left, right):
    left_high, left_low = split(left)
    right_high, right_low = split(right)
    return dot(left_high, right_high) + dot(left_high, right_low) + dot(left_low, right_high)


def times_part(part, right):
    high, low = split(right)
    return dot(part, high) + dot(part, low)


def tanh_of(state):
    return jnp.tanh(state.astype(F32))


def slope_of(act):
    return STEP * (1.0 - act * act)


def prep_kernel(filters_ref, terminal_ref, states_ref, matrix_ref, ending_ref, kept_ref, lent_ref):
    total = filters_ref[0, :, 0:CH].astype(F32)
    for t in range(1, TAPS):
        total += filters_ref[0, :, t * CH : (t + 1) * CH].astype(F32)
    total *= STEP
    matrix_ref[...] = rounded((2.0 * KEEP) * total + dot(total, total, EXACT))
    ending_ref[...] = terminal_ref[...]
    kept_ref[...] = states_ref[...]
    lent_ref[...] = states_ref[lax.axis_index("dp") % 2]


def fine_kernel(
    above_ref, terminal_ref, guess_ref, states_ref, filters_ref, matrix_ref, top_ref, pack_ref, stack_ref
):
    last = lax.axis_index("layer") == XS * YS - 1
    top = jnp.where(last, terminal_ref[...].astype(F32), above_ref[...].astype(F32))
    top_ref[...] = top.astype(BF)
    write_stack(top.astype(BF), stack_ref)
    below = KEEP * top + slope_of(tanh_of(states_ref[1])) * dot(filters_ref[1], stack_ref[...])
    below = below.astype(BF)
    write_stack(below, stack_ref)
    moved = slope_of(tanh_of(states_ref[0])) * dot(filters_ref[0], stack_ref[...])
    residual = KEEP * below.astype(F32) + moved - guess_ref[...].astype(F32)
    high, low = split(residual)
    pool = jnp.where(pool_matrix(), 0.25, 0.0).astype(BF)
    coarse = (dot(high, pool) + dot(low, pool)).astype(BF)
    matrix = matrix_ref[...]
    for j in range(XS):
        pack_ref[j, :, :CELLS] = coarse
        pack_ref[j, :, CELLS:] = matrix


def group_kernel(packs_ref, pack_ref):
    scale = KEEP**2
    coarse = [packs_ref[j, :, :CELLS] for j in range(XS)]
    part = [packs_ref[j, :, CELLS:] for j in range(XS)]
    near, far = (
        coarse[j].astype(F32) + scale * coarse[j + 1].astype(F32) + dot(part[j], coarse[j + 1]) for j in (0, 2)
    )
    left, right = (
        scale * (part[j].astype(F32) + part[j + 1].astype(F32)) + dot(part[j], part[j + 1]) for j in (0, 2)
    )
    value = (near + scale**2 * far + times(left, far)).astype(BF)
    group = rounded(scale**2 * (left + right) + times(left, right))
    for j in range(YS):
        pack_ref[j, :, :CELLS] = value
        pack_ref[j, :, CELLS:] = group


def upper_error(groups_ref, y):
    scale = KEEP**8
    pairs = []
    for a in range(0, YS, 2):
        on = [(a + i > y).astype(F32) for i in range(2)]
        hold = [jnp.where(a + i > y, scale, 1.0) for i in range(2)]
        values = [groups_ref[a + i, :, :CELLS] for i in range(2)]
        parts = [groups_ref[a + i, :, CELLS:] for i in range(2)]
        mixed = hold[0] * values[1].astype(F32) + on[0] * dot(parts[0], values[1])
        field = on[0] * values[0].astype(F32) + on[1] * mixed
        crossed = (hold[0] * on[1]) * parts[1].astype(F32) + (hold[1] * on[0]) * parts[0].astype(F32)
        crossed += (on[0] * on[1]) * dot(parts[0], parts[1])
        pairs.append((field, hold[0] * hold[1], crossed))

    def joined(low, high):
        return low[0] + low[1] * high[0] + times(low[2], high[0])

    near, far = joined(pairs[0], pairs[1]), joined(pairs[2], pairs[3])
    hold = pairs[0][1] * pairs[1][1]
    crossed = pairs[0][1] * pairs[1][2] + pairs[1][1] * pairs[0][2] + times(pairs[0][2], pairs[1][2])
    return near + hold * far + times(crossed, far)


def local_maps(packs_ref):
    scale = KEEP**2
    coarse = [packs_ref[j, :, :CELLS] for j in range(XS)]
    part = [packs_ref[j, :, CELLS:] for j in range(XS)]
    field, hold, crossed = coarse[3].astype(F32), scale, part[3].astype(F32)
    maps = [(field, hold, crossed)]
    for j in (2, 1, 0):
        field = coarse[j].astype(F32) + scale * field + times_part(part[j], field)
        crossed = scale * crossed + hold * part[j].astype(F32) + times_part(part[j], crossed)
        hold *= scale
        maps.append((field, hold, crossed))
    return maps[::-1]


def correct_kernel(
    groups_ref, packs_hbm, top_hbm, guess_hbm, states_hbm, filters_hbm,
    adjoint_ref, own_ref, lent_ref, act_ref,
    packs_ref, top_ref, guess_ref, states_ref, filters_ref, stack_ref, next_scr, act_scr, sems,
):
    copies = [
        pltpu.make_async_copy(source, target, sems.at[i])
        for i, (source, target) in enumerate((
            (packs_hbm, packs_ref),
            (top_hbm, top_ref),
            (states_hbm, states_ref),
            (guess_hbm.at[0], guess_ref),
            (filters_hbm.at[1], filters_ref),
        ))
    ]
    for copy in copies:
        copy.start()
    layer = lax.axis_index("layer")
    core = lax.axis_index("dp") % 2
    x, y = layer % XS, layer // XS
    copies[0].wait()
    maps = local_maps(packs_ref)
    nil = (jnp.zeros((CH, CELLS), F32), 1.0, jnp.zeros((CH, CH), F32))
    own_map, upper_map = maps[XS - 1], nil
    for j in range(XS - 2, -1, -1):
        own_map = tuple(jnp.where(x == j, a, b) for a, b in zip(maps[j], own_map))
        upper_map = tuple(jnp.where(x == j, a, b) for a, b in zip(maps[j + 1], upper_map))
    far = upper_error(groups_ref, y)
    spread = spread_matrix()

    def widened(local):
        high, low = split(local[0] + local[1] * far + times(local[2], far))
        return dot(high, spread) + dot(low, spread)

    copies[1].wait()
    top = (top_ref[...].astype(F32) + widened(upper_map)).astype(BF)
    write_stack(top, stack_ref)
    copies[2].wait()
    copies[3].wait()
    copies[4].wait()
    act = tanh_of(states_ref[1])
    below = KEEP * top.astype(F32) + slope_of(act) * dot(filters_ref[...], stack_ref[...])
    below = below.astype(BF)
    next_scr[1] = top
    next_scr[0] = below
    act_scr[1] = act.astype(BF)
    act_scr[0] = tanh_of(states_ref[0]).astype(BF)
    adjoint_ref[0] = (guess_ref[...].astype(F32) + widened(own_map)).astype(BF)
    adjoint_ref[1] = below
    lent_ref[...] = next_scr[core]
    own_ref[...] = next_scr[1 - core]
    act_ref[...] = act_scr[1 - core]


def gradient_of(act, field, stack_ref):
    write_stack(field, stack_ref)
    contract = (((1,), (1,)), ((), ()))
    return STEP * lax.dot_general(act, stack_ref[...], contract, preferred_element_type=F32)


def own_kernel(adjoint_ref, own_ref, act_ref, other_ref, out_hbm, grad_ref, other_act_ref, stack_ref, sem):
    copy = pltpu.make_async_copy(adjoint_ref, out_hbm, sem)
    copy.start()
    other_act_ref[...] = tanh_of(other_ref[...]).astype(BF)
    grad_ref[...] = gradient_of(act_ref[...], own_ref[...], stack_ref)
    copy.wait()


def other_kernel(came_ref, other_act_ref, grad_ref, share_ref, stack_ref):
    grad = grad_ref[...] + gradient_of(other_act_ref[...], came_ref[...], stack_ref)
    share_ref[...] = grad.reshape(2 * ZS, 8, TAPS * CH).astype(BF)


def total_kernel(came_ref, grad_ref):
    for l in range(2):
        total = came_ref[1 - l].astype(F32)
        for z in range(1, ZS):
            total += came_ref[2 * z + 1 - l].astype(F32)
        grad_ref[l] = total


def call(body, outs, scratch=(), flops=10**6, vmem=6, in_specs=None, out_specs=None):
    outs = [jax.ShapeDtypeStruct(s, d) for s, d in outs]
    extra = {} if in_specs is None else {"in_specs": in_specs}
    if out_specs is not None:
        extra["out_specs"] = out_specs
    return pl.pallas_call(
        body,
        out_shape=outs[0] if len(outs) == 1 else outs,
        scratch_shapes=list(scratch),
        compiler_params=pltpu.CompilerParams(vmem_limit_bytes=vmem << 20),
        cost_estimate=pl.CostEstimate(flops=flops, bytes_accessed=1 << 20, transcendentals=0),
        **extra,
    )


WIDTH = CELLS + CH
FIELD = (CH, PIX)
STACK = pltpu.VMEM((TAPS * CH, PIX), BF)
ANY = pl.BlockSpec(memory_space=pl.ANY)
prep = call(prep_kernel, [((CH, CH), BF), (FIELD, BF), ((2,) + FIELD, BF), (FIELD, BF)])
fine = call(fine_kernel, [(FIELD, BF), ((XS, CH, WIDTH), BF)], [STACK], 10**9, 16)
group_of = call(group_kernel, [((YS, CH, WIDTH), BF)])
correct = call(
    correct_kernel,
    [((2,) + FIELD, BF), (FIELD, BF), (FIELD, BF), (FIELD, BF)],
    [
        pltpu.VMEM((XS, CH, WIDTH), BF),
        pltpu.VMEM(FIELD, BF),
        pltpu.VMEM(FIELD, BF),
        pltpu.VMEM((2,) + FIELD, BF),
        pltpu.VMEM((CH, TAPS * CH), BF),
        STACK,
        pltpu.VMEM((2,) + FIELD, BF),
        pltpu.VMEM((2,) + FIELD, BF),
        pltpu.SemaphoreType.DMA((5,)),
    ],
    10**9,
    20,
    [VMEM] + [ANY] * 5,
)
own_part = call(
    own_kernel,
    [((2,) + FIELD, BF), ((CH, TAPS * CH), F32), (FIELD, BF)],
    [STACK, pltpu.SemaphoreType.DMA(())],
    10**9,
    12,
    [VMEM] * 4,
    [ANY, VMEM, VMEM],
)
other_part = call(other_kernel, [((2 * ZS, 8, TAPS * CH), BF)], [STACK], 10**9, 12)
total_of = call(total_kernel, [((2, 8, TAPS * CH), F32)])


def per_device(states, filters, guess, terminal):
    states, guess, terminal = states[:, 0], guess[:, 0], terminal[0]
    x_groups = [[y * XS + x for x in range(XS)] for y in range(YS)]
    y_groups = [[y * XS + x for y in range(YS)] for x in range(XS)]

    def exchange(a, axis, groups):
        return lax.all_to_all(a, axis, 0, 0, axis_index_groups=groups)

    above = lax.ppermute(guess[0], "layer", [(i + 1, i) for i in range(XS * YS - 1)])
    matrix, ending, kept, lent = prep(filters, terminal, states)
    swap = [(i ^ 1, i) for i in range(2 * ZS)]
    other = lax.ppermute(lent, "dp", swap)
    above, other = lax.optimization_barrier((above, other))
    top, pack = fine(above, ending, guess[0], kept, filters, matrix)
    packs = exchange(pack, "layer", x_groups)
    groups = exchange(group_of(packs), "layer", y_groups)
    fresh, own, lent, act = correct(groups, packs, top, guess, states, filters)
    came = lax.ppermute(lent, "dp", swap)
    adjoint, grad, other_act = own_part(fresh, own, act, other)
    shares = lax.all_to_all(other_part(came, other_act, grad), "dp", 0, 0)
    return adjoint[:, None], total_of(shares)


def solution(mesh):
    return jax.shard_map(
        per_device,
        mesh=mesh,
        in_specs=(
            P("layer", "dp", None, None),
            P("layer", None, None),
            P("layer", "dp", None, None),
            P("dp", None, None),
        ),
        out_specs=(P("layer", "dp", None, None), P("layer", "dp", None)),
        check_vma=False,
    )
```

time: 90.8 us -> 89.2 us (0.982)
  starting transfers between devices: 8.16 us -> 16.9 us
  blocking collectives: 62 us -> 56.7 us
  waiting for transfers between devices: 6.26 us -> 1.13 us
    all_to_all x3 -> x2, blocking collectives: 62 us -> 34.2 us  [exchange(): return lax.all_to_all(a, axis, 0, 0, axis_index_groups=groups)]
    all_to_all x0 -> x1, blocking collectives: none -> 22.5 us  [per_device(): shares = lax.all_to_all(other_part(came, other_act, grad), 'dp', 0, 0)]
    ppermute x1 -> x2, starting transfers between devices: 6.87 us -> 15.6 us  [the longest x1 8.75 us: per_device(): other = lax.ppermute(lent, 'dp', swap)]
    ppermute x1, waiting for transfers between devices: 5.07 us -> 0.01 us  [per_device(): lax.ppermute(guess[0], 'layer', [(i + 1, i) for i in range(XS * YS - 1)])]
    pallas_call x4 -> x5, Pallas kernels: 8.55 us -> 9.11 us  [the longest x1 3.88 us: per_device(): fresh, own, lent, act = correct(groups, packs, top, guess, states, filters)]
    unnamed x12 -> x10, local copies, waits for them, and re-layouts: 2.12 us -> 2.02 us
  transfers between devices with their start and end apart: 2 -> 3, of which waited for: 2 -> 1; matrix products, arithmetic and copies ran while one was open for 0% -> 0% of each run, Pallas kernels for 0% -> 2%
where the time goes in v4:
time: 89.2 us; the launch traced here: 88.8 us
  blocking collectives  56.7 us (64%)
  starting transfers between devices  16.9 us (19%)
  Pallas kernels  10.2 us (11%)
  local copies, waits for them, and re-layouts  3.05 us (3%)
  waiting for transfers between devices  1.13 us (1%)
    all_to_all x2, blocking collectives, exchange(): return lax.all_to_all(a, axis, 0, 0, axis_index_groups=groups)  34.2 us
    all_to_all x1, blocking collectives, per_device(): shares = lax.all_to_all(other_part(came, other_act, grad), 'dp', 0, 0)  22.5 us
    ppermute x1, starting transfers between devices, per_device(): other = lax.ppermute(lent, 'dp', swap)  8.75 us
    ppermute x1, starting transfers between devices, per_device(): came = lax.ppermute(lent, 'dp', swap)  6.86 us
    pallas_call x1, Pallas kernels, per_device(): fresh, own, lent, act = correct(groups, packs, top, guess, states, filters)  3.88 us
    pallas_call x1, Pallas kernels, per_device(): top, pack = fine(above, ending, guess[0], kept, filters, matrix)  2.32 us
    unnamed x10, local copies, waits for them, and re-layouts  2.02 us
  transfers between devices with their start and end apart: 3, of which 1 were waited for; matrix products, arithmetic and copies ran while one was open for 0% of the time, Pallas kernels for 2%

profile of v4, /device:TPU:1, one launch (start us, length us, event | category | flops | bytes accessed | tf_op | source)
XLA Modules:
  0.0 88.8 jit_solution(373749462651291039)
XLA Ops:
  0.6 0.0 copy-start.2
  0.6 1.0 %slice_bitcast_fusion.guess_ref = bf16[128,1024]{1,0:T(8,128)(2,1)S(1)} fusion(bf16[2,1,128,1024]{3,2,1,0:T(8,128)(2,1)} %param.6), kind=kLoop, calls=%fused_computation | loop fusion | bytes 524288 | tf_op jit(solution)/shard_map/squeeze | solution.py:325
  1.7 1.3 %collective-permute-start = (bf16[128,1024]{1,0:T(8,128)(2,1)S(1)}, bf16[128,1024]{1,0:T(8,128)(2,1)S(1)}, u32[]{:S(2)}, u32[]{:S(2)}) collective-permute-start(bf16[128,1024]{1,0:T(8,128)(2,1)S(1)} %slice_bitcast_fusion.guess_ref), channel_id=1, source_target_pairs={{16,0},{32,16},{48,32},{64,48},{80,64},{96,80},{112,96},{128,112},... | collective-permute-start | bytes 786440 | tf_op jit(solution)/shard_map/ppermute | solution.py:325
  3.0 0.0 copy-done.2
  3.0 0.0 copy-start
  3.0 1.1 %copy-done = bf16[2,128,1152]{2,1,0:T(8,128)(2,1)S(1)} copy-done((bf16[2,128,1152]{2,1,0:T(8,128)(2,1)S(1)}, bf16[2,128,1152]{2,1,0:T(8,128)(2,1)}, u32[]{:S(2)}) %copy-start) | copy-done | bytes 589848
  4.0 0.0 copy-start.3
  4.0 0.9 %copy-done.3 = bf16[1,128,1024]{2,1,0:T(8,128)(2,1)S(1)} copy-done((bf16[1,128,1024]{2,1,0:T(8,128)(2,1)S(1)}, bf16[1,128,1024]{2,1,0:T(8,128)(2,1)}, u32[]{:S(2)}) %copy-start.3) | copy-done | bytes 262168
  5.0 0.0 copy-start.1
  5.0 0.2 shard_map.59
  5.2 8.7 %collective-permute-start.1 = (bf16[128,1024]{1,0:T(8,128)(2,1)S(1)}, bf16[128,1024]{1,0:T(8,128)(2,1)S(1)}, u32[]{:S(2)}, u32[]{:S(2)}) collective-permute-start(bf16[128,1024]{1,0:T(8,128)(2,1)S(1)} %get-tuple-element.17), channel_id=1, source_target_pairs={{1,0},{0,1},{3,2},{2,3},{5,4},{4,5},{7,6},{6,7},{9,8},{8,9},{11,10... | collective-permute-start | bytes 786440 | tf_op jit(solution)/shard_map/ppermute | solution.py:328
  14.0 0.0 collective-permute-done.above_ref
  14.0 1.1 %collective-permute-done.1.other_ref = bf16[128,1024]{1,0:T(8,128)(2,1)S(1)} collective-permute-done((bf16[128,1024]{1,0:T(8,128)(2,1)S(1)}, bf16[128,1024]{1,0:T(8,128)(2,1)S(1)}, u32[]{:S(2)}, u32[]{:S(2)}) %collective-permute-start.1) | collective-permute-done | bytes 262176 | tf_op jit(solution)/shard_map/ppermute | solution.py:328
  15.1 0.0 copy-done.1
  15.1 2.3 %shard_map.60 = (bf16[128,1024]{1,0:T(8,128)(2,1)S(1)}, bf16[4,128,384]{2,1,0:T(8,128)(2,1)S(1)}) custom-call(bf16[128,1024]{1,0:T(8,128)(2,1)S(1)} %collective-permute-done.above_ref, bf16[128,1024]{1,0:T(8,128)(2,1)S(1)} %get-tuple-element.19.terminal_ref, bf16[128,1024]{1,0:T(8,128)(2,1)S(1)} %slice_bitcast_fusion.guess_ref, ...), custom_call_target="tpu_custom_call" | custom-call | flops 1000000000 | bytes 1048576 | tf_op jit(solution)/shard_map/pallas_call | solution.py:330
  17.5 10.7 %all_to_all.15.packs_ref.packs_hbm = bf16[4,128,384]{2,1,0:T(8,128)(2,1)S(1)} all-to-all(bf16[4,128,384]{2,1,0:T(8,128)(2,1)S(1)} %get-tuple-element.22), channel_id=1, replica_groups={{0,16,32,48},{64,80,96,112},{128,144,160,176},{192,208,224,240},{256,27..., dimensions={0} | all-to-all | bytes 786432 | tf_op jit(solution)/shard_map/all_to_all | solution.py:323
  28.1 0.5 shard_map.61
  28.6 0.0 copy-start.4
  28.6 23.5 %all_to_all.16.groups_ref = bf16[8,128,384]{2,1,0:T(8,128)(2,1)S(1)} all-to-all(bf16[8,128,384]{2,1,0:T(8,128)(2,1)S(1)} %shard_map.61), channel_id=1, replica_groups={{0,64,128,192,256,320,384,448},{16,80,144,208,272,336,400,464},{32,96,1..., dimensions={0} | all-to-all | bytes 1572864 | tf_op jit(solution)/shard_map/all_to_all | solution.py:323
  52.1 0.0 copy-done.4
  52.1 3.9 %shard_map.62 = (bf16[2,128,1024]{2,1,0:T(8,128)(2,1)S(1)}, bf16[128,1024]{1,0:T(8,128)(2,1)S(1)}, bf16[128,1024]{1,0:T(8,128)(2,1)S(1)}, bf16[128,1024]{1,0:T(8,128)(2,1)S(1)}) custom-call(bf16[8,128,384]{2,1,0:T(8,128)(2,1)S(1)} %all_to_all.16.groups_ref, bf16[4,128,384]{2,1,0:T(8,128)(2,1)S(1)} %all_to_all.15.packs_ref.packs_hbm, ...), custom_call_target="tpu_custom_call" | custom-call | flops 1000000000 | bytes 1048576 | tf_op jit(solution)/shard_map/pallas_call | solution.py:333
  56.0 6.9 %collective-permute-start.2 = (bf16[128,1024]{1,0:T(8,128)(2,1)S(1)}, bf16[128,1024]{1,0:T(8,128)(2,1)S(1)}, u32[]{:S(2)}, u32[]{:S(2)}) collective-permute-start(bf16[128,1024]{1,0:T(8,128)(2,1)S(1)} %get-tuple-element.29), channel_id=1, source_target_pairs={{1,0},{0,1},{3,2},{2,3},{5,4},{4,5},{7,6},{6,7},{9,8},{8,9},{11,10... | collective-permute-start | bytes 786440 | tf_op jit(solution)/shard_map/ppermute | solution.py:334
  62.9 1.5 %shard_map.63 = (bf16[2,128,1024]{2,1,0:T(8,128)(2,1)}, f32[128,1152]{1,0:T(8,128)S(1)}, bf16[128,1024]{1,0:T(8,128)(2,1)S(1)}) custom-call(bf16[2,128,1024]{2,1,0:T(8,128)(2,1)S(1)} %get-tuple-element.24.adjoint_ref, bf16[128,1024]{1,0:T(8,128)(2,1)S(1)} %get-tuple-element.25.own_ref, bf16[128,1024]{1,0:T(8,128)(2,1)S(1)} %get-tuple-element.26.act_ref, ...), custom_call_target="tpu_custom_call" | custom-call | flops 1000000000 | bytes 1048576 | tf_op jit(solution)/shard_map/pallas_call | solution.py:335
  64.4 0.0 collective-permute-done.2.came_ref
  64.4 1.1 %shard_map.64 = bf16[16,8,1152]{2,1,0:T(8,128)(2,1)S(1)} custom-call(bf16[128,1024]{1,0:T(8,128)(2,1)S(1)} %collective-permute-done.2.came_ref, bf16[128,1024]{1,0:T(8,128)(2,1)S(1)} %get-tuple-element.30.other_act_ref, f32[128,1152]{1,0:T(8,128)S(1)} %get-tuple-element.31.grad_ref), custom_call_target="tpu_custom_call" | custom-call | flops 1000000000 | bytes 1048576 | tf_op jit(solution)/shard_map/pallas_call | solution.py:336
  65.6 22.5 %all_to_all.17.came_ref = bf16[16,8,1152]{2,1,0:T(8,128)(2,1)S(1)} all-to-all(bf16[16,8,1152]{2,1,0:T(8,128)(2,1)S(1)} %shard_map.64), channel_id=1, replica_groups=mesh['layer'=32,'dp'=16] {'dp'}, dimensions={0} | all-to-all | bytes 589824 | tf_op jit(solution)/shard_map/all_to_all | solution.py:336
  88.1 0.7 shard_map.65
Async XLA Ops:
  0.6 2.3 %copy-start.2 = (bf16[2,1,128,1024]{3,2,1,0:T(8,128)(2,1)S(1)}, bf16[2,1,128,1024]{3,2,1,0:T(8,128)(2,1)}, u32[]{:S(2)}) copy-start(bf16[2,1,128,1024]{3,2,1,0:T(8,128)(2,1)} %param.4) | copy-start | bytes 1572868
  1.7 12.3 %collective-permute-start = (bf16[128,1024]{1,0:T(8,128)(2,1)S(1)}, bf16[128,1024]{1,0:T(8,128)(2,1)S(1)}, u32[]{:S(2)}, u32[]{:S(2)}) collective-permute-start(bf16[128,1024]{1,0:T(8,128)(2,1)S(1)} %slice_bitcast_fusion.guess_ref), channel_id=1, source_target_pairs={{16,0},{32,16},{48,32},{64,48},{80,64},{96,80},{112,96},{128,112},... | collective-permute-start | bytes 786440 | tf_op jit(solution)/shard_map/ppermute | solution.py:325
  3.0 1.1 %copy-start = (bf16[2,128,1152]{2,1,0:T(8,128)(2,1)S(1)}, bf16[2,128,1152]{2,1,0:T(8,128)(2,1)}, u32[]{:S(2)}) copy-start(bf16[2,128,1152]{2,1,0:T(8,128)(2,1)} %filters_hbm.1) | copy-start | bytes 1769476
  4.0 0.9 %copy-start.3 = (bf16[1,128,1024]{2,1,0:T(8,128)(2,1)S(1)}, bf16[1,128,1024]{2,1,0:T(8,128)(2,1)}, u32[]{:S(2)}) copy-start(bf16[1,128,1024]{2,1,0:T(8,128)(2,1)} %param.7) | copy-start | bytes 786436
  5.0 10.1 %copy-start.1 = (bf16[2,128,1152]{2,1,0:T(8,128)(2,1)S(1)}, bf16[2,128,1152]{2,1,0:T(8,128)(2,1)}, u32[]{:S(2)}) copy-start(bf16[2,128,1152]{2,1,0:T(8,128)(2,1)} %filters_hbm.1) | copy-start | bytes 1769476
  5.2 9.9 %collective-permute-start.1 = (bf16[128,1024]{1,0:T(8,128)(2,1)S(1)}, bf16[128,1024]{1,0:T(8,128)(2,1)S(1)}, u32[]{:S(2)}, u32[]{:S(2)}) collective-permute-start(bf16[128,1024]{1,0:T(8,128)(2,1)S(1)} %get-tuple-element.17), channel_id=1, source_target_pairs={{1,0},{0,1},{3,2},{2,3},{5,4},{4,5},{7,6},{6,7},{9,8},{8,9},{11,10... | collective-permute-start | bytes 786440 | tf_op jit(solution)/shard_map/ppermute | solution.py:328
  28.6 23.5 %copy-start.4 = (bf16[2,1,128,1024]{3,2,1,0:T(8,128)(2,1)S(1)}, bf16[2,1,128,1024]{3,2,1,0:T(8,128)(2,1)}, u32[]{:S(2)}) copy-start(bf16[2,1,128,1024]{3,2,1,0:T(8,128)(2,1)} %param.6) | copy-start | bytes 1572868
  56.0 8.4 %collective-permute-start.2 = (bf16[128,1024]{1,0:T(8,128)(2,1)S(1)}, bf16[128,1024]{1,0:T(8,128)(2,1)S(1)}, u32[]{:S(2)}, u32[]{:S(2)}) collective-permute-start(bf16[128,1024]{1,0:T(8,128)(2,1)S(1)} %get-tuple-element.29), channel_id=1, source_target_pairs={{1,0},{0,1},{3,2},{2,3},{5,4},{4,5},{7,6},{6,7},{9,8},{8,9},{11,10... | collective-permute-start | bytes 786440 | tf_op jit(solution)/shard_map/ppermute | solution.py:334

commit v5 on v4

--- a/solution.py
+++ b/solution.py
@@ -12,7 +12,7 @@
 SIDE, PIX, CH, TAPS = 32, 1024, 128, 9
 HALF = SIDE // 2
 CELLS = HALF * HALF
-XS, YS, ZS = 4, 8, 8
+GROUP, GROUPS, ZS = 8, 4, 8
 BF, F32 = jnp.bfloat16, jnp.float32
 EXACT = lax.Precision.HIGHEST
 VMEM = pl.BlockSpec(memory_space=pltpu.VMEM)
@@ -108,7 +108,7 @@
 def fine_kernel(
     above_ref, terminal_ref, guess_ref, states_ref, filters_ref, matrix_ref, top_ref, pack_ref, stack_ref
 ):
-    last = lax.axis_index("layer") == XS * YS - 1
+    last = lax.axis_index("layer") == GROUP * GROUPS - 1
     top = jnp.where(last, terminal_ref[...].astype(F32), above_ref[...].astype(F32))
     top_ref[...] = top.astype(BF)
     write_stack(top.astype(BF), stack_ref)
@@ -121,34 +121,45 @@
     pool = jnp.where(pool_matrix(), 0.25, 0.0).astype(BF)
     coarse = (dot(high, pool) + dot(low, pool)).astype(BF)
     matrix = matrix_ref[...]
-    for j in range(XS):
+    for j in range(GROUP):
         pack_ref[j, :, :CELLS] = coarse
         pack_ref[j, :, CELLS:] = matrix
 
 
+def paired(scale, fields, parts):
+    near, far, left, right = fields[::2], fields[1::2], parts[::2], parts[1::2]
+    joint = [a + scale * b + times(part, b) for a, b, part in zip(near, far, left)]
+    mixed = [scale * (a + b) + times(a, b) for a, b in zip(left, right)]
+    return scale * scale, joint, mixed
+
+
 def group_kernel(packs_ref, pack_ref):
     scale = KEEP**2
-    coarse = [packs_ref[j, :, :CELLS] for j in range(XS)]
-    part = [packs_ref[j, :, CELLS:] for j in range(XS)]
-    near, far = (
-        coarse[j].astype(F32) + scale * coarse[j + 1].astype(F32) + dot(part[j], coarse[j + 1]) for j in (0, 2)
-    )
-    left, right = (
-        scale * (part[j].astype(F32) + part[j + 1].astype(F32)) + dot(part[j], part[j + 1]) for j in (0, 2)
-    )
-    value = (near + scale**2 * far + times(left, far)).astype(BF)
-    group = rounded(scale**2 * (left + right) + times(left, right))
-    for j in range(YS):
+    coarse = [packs_ref[j, :, :CELLS] for j in range(GROUP)]
+    part = [packs_ref[j, :, CELLS:] for j in range(GROUP)]
+    fields, parts = [], []
+    for j in range(0, GROUP, 2):
+        fields.append(coarse[j].astype(F32) + scale * coarse[j + 1].astype(F32) + dot(part[j], coarse[j + 1]))
+        parts.append(scale * (part[j].astype(F32) + part[j + 1].astype(F32)) + dot(part[j], part[j + 1]))
+    scale *= scale
+    while len(fields) > 1:
+        scale, fields, parts = paired(scale, fields, parts)
+    value, group = fields[0].astype(BF), rounded(parts[0])
+    for j in range(GROUPS):
         pack_ref[j, :, :CELLS] = value
         pack_ref[j, :, CELLS:] = group
 
 
-def upper_error(groups_ref, y):
-    scale = KEEP**8
+def applied(local, error):
+    return local[0] + local[1] * error + times(local[2], error)
+
+
+def upper_error(groups_ref, at):
+    scale = KEEP ** (2 * GROUP)
     pairs = []
-    for a in range(0, YS, 2):
-        on = [(a + i > y).astype(F32) for i in range(2)]
-        hold = [jnp.where(a + i > y, scale, 1.0) for i in range(2)]
+    for a in range(0, GROUPS, 2):
+        on = [(a + i > at).astype(F32) for i in range(2)]
+        hold = [jnp.where(a + i > at, scale, 1.0) for i in range(2)]
         values = [groups_ref[a + i, :, :CELLS] for i in range(2)]
         parts = [groups_ref[a + i, :, CELLS:] for i in range(2)]
         mixed = hold[0] * values[1].astype(F32) + on[0] * dot(parts[0], values[1])
@@ -156,28 +167,27 @@
         crossed = (hold[0] * on[1]) * parts[1].astype(F32) + (hold[1] * on[0]) * parts[0].astype(F32)
         crossed += (on[0] * on[1]) * dot(parts[0], parts[1])
         pairs.append((field, hold[0] * hold[1], crossed))
-
-    def joined(low, high):
-        return low[0] + low[1] * high[0] + times(low[2], high[0])
-
-    near, far = joined(pairs[0], pairs[1]), joined(pairs[2], pairs[3])
-    hold = pairs[0][1] * pairs[1][1]
-    crossed = pairs[0][1] * pairs[1][2] + pairs[1][1] * pairs[0][2] + times(pairs[0][2], pairs[1][2])
-    return near + hold * far + times(crossed, far)
-
-
-def local_maps(packs_ref):
+    return applied(pairs[0], pairs[1][0])
+
+
+def suffix_maps(packs_ref, first, last):
     scale = KEEP**2
-    coarse = [packs_ref[j, :, :CELLS] for j in range(XS)]
-    part = [packs_ref[j, :, CELLS:] for j in range(XS)]
-    field, hold, crossed = coarse[3].astype(F32), scale, part[3].astype(F32)
-    maps = [(field, hold, crossed)]
-    for j in (2, 1, 0):
+    coarse = {j: packs_ref[j, :, :CELLS] for j in range(first, last + 1)}
+    part = {j: packs_ref[j, :, CELLS:] for j in range(first, last + 1)}
+    field, hold, crossed = coarse[last].astype(F32), scale, part[last].astype(F32)
+    maps = {last: (field, hold, crossed)}
+    for j in range(last - 1, first - 1, -1):
         field = coarse[j].astype(F32) + scale * field + times_part(part[j], field)
         crossed = scale * crossed + hold * part[j].astype(F32) + times_part(part[j], crossed)
         hold *= scale
-        maps.append((field, hold, crossed))
-    return maps[::-1]
+        maps[j] = (field, hold, crossed)
+    return maps
+
+
+def picked(maps, default, at):
+    for j, local in maps.items():
+        default = tuple(jnp.where(at == j, a, b) for a, b in zip(local, default))
+    return default
 
 
 def correct_kernel(
@@ -199,23 +209,25 @@
         copy.start()
     layer = lax.axis_index("layer")
     core = lax.axis_index("dp") % 2
-    x, y = layer % XS, layer // XS
+    place, at = layer % GROUP, layer // GROUP
     copies[0].wait()
-    maps = local_maps(packs_ref)
+    half = GROUP // 2
+    low, high = suffix_maps(packs_ref, 0, half - 1), suffix_maps(packs_ref, half, GROUP - 1)
     nil = (jnp.zeros((CH, CELLS), F32), 1.0, jnp.zeros((CH, CH), F32))
-    own_map, upper_map = maps[XS - 1], nil
-    for j in range(XS - 2, -1, -1):
-        own_map = tuple(jnp.where(x == j, a, b) for a, b in zip(maps[j], own_map))
-        upper_map = tuple(jnp.where(x == j, a, b) for a, b in zip(maps[j + 1], upper_map))
-    far = upper_error(groups_ref, y)
+    low_own = picked(low, nil, place)
+    low_upper = picked({j - 1: low[j] for j in range(1, half)}, nil, place)
+    high_own = picked({j: high[j] for j in range(half + 1, GROUP)}, high[half], place)
+    high_upper = picked({j - 1: high[j] for j in range(half + 1, GROUP)}, high[half], place)
+    high_upper = picked({GROUP - 1: nil}, high_upper, place)
+    far = upper_error(groups_ref, at)
     spread = spread_matrix()
 
-    def widened(local):
-        high, low = split(local[0] + local[1] * far + times(local[2], far))
-        return dot(high, spread) + dot(low, spread)
+    def widened(near, beyond):
+        high_part, low_part = split(applied(near, applied(beyond, far)))
+        return dot(high_part, spread) + dot(low_part, spread)
 
     copies[1].wait()
-    top = (top_ref[...].astype(F32) + widened(upper_map)).astype(BF)
+    top = (top_ref[...].astype(F32) + widened(low_upper, high_upper)).astype(BF)
     write_stack(top, stack_ref)
     copies[2].wait()
     copies[3].wait()
@@ -227,7 +239,7 @@
     next_scr[0] = below
     act_scr[1] = act.astype(BF)
     act_scr[0] = tanh_of(states_ref[0]).astype(BF)
-    adjoint_ref[0] = (guess_ref[...].astype(F32) + widened(own_map)).astype(BF)
+    adjoint_ref[0] = (guess_ref[...].astype(F32) + widened(low_own, high_own)).astype(BF)
     adjoint_ref[1] = below
     lent_ref[...] = next_scr[core]
     own_ref[...] = next_scr[1 - core]
@@ -281,13 +293,13 @@
 STACK = pltpu.VMEM((TAPS * CH, PIX), BF)
 ANY = pl.BlockSpec(memory_space=pl.ANY)
 prep = call(prep_kernel, [((CH, CH), BF), (FIELD, BF), ((2,) + FIELD, BF), (FIELD, BF)])
-fine = call(fine_kernel, [(FIELD, BF), ((XS, CH, WIDTH), BF)], [STACK], 10**9, 16)
-group_of = call(group_kernel, [((YS, CH, WIDTH), BF)])
+fine = call(fine_kernel, [(FIELD, BF), ((GROUP, CH, WIDTH), BF)], [STACK], 10**9, 16)
+group_of = call(group_kernel, [((GROUPS, CH, WIDTH), BF)])
 correct = call(
     correct_kernel,
     [((2,) + FIELD, BF), (FIELD, BF), (FIELD, BF), (FIELD, BF)],
     [
-        pltpu.VMEM((XS, CH, WIDTH), BF),
+        pltpu.VMEM((GROUP, CH, WIDTH), BF),
         pltpu.VMEM(FIELD, BF),
         pltpu.VMEM(FIELD, BF),
         pltpu.VMEM((2,) + FIELD, BF),
@@ -316,20 +328,20 @@
 
 def per_device(states, filters, guess, terminal):
     states, guess, terminal = states[:, 0], guess[:, 0], terminal[0]
-    x_groups = [[y * XS + x for x in range(XS)] for y in range(YS)]
-    y_groups = [[y * XS + x for y in range(YS)] for x in range(XS)]
+    near_groups = [[k * GROUP + j for j in range(GROUP)] for k in range(GROUPS)]
+    far_groups = [[k * GROUP + j for k in range(GROUPS)] for j in range(GROUP)]
 
     def exchange(a, axis, groups):
         return lax.all_to_all(a, axis, 0, 0, axis_index_groups=groups)
 
-    above = lax.ppermute(guess[0], "layer", [(i + 1, i) for i in range(XS * YS - 1)])
+    above = lax.ppermute(guess[0], "layer", [(i + 1, i) for i in range(GROUP * GROUPS - 1)])
     matrix, ending, kept, lent = prep(filters, terminal, states)
     swap = [(i ^ 1, i) for i in range(2 * ZS)]
     other = lax.ppermute(lent, "dp", swap)
     above, other = lax.optimization_barrier((above, other))
     top, pack = fine(above, ending, guess[0], kept, filters, matrix)
-    packs = exchange(pack, "layer", x_groups)
-    groups = exchange(group_of(packs), "layer", y_groups)
+    packs = exchange(pack, "layer", near_groups)
+    groups = exchange(group_of(packs), "layer", far_groups)
     fresh, own, lent, act = correct(groups, packs, top, guess, states, filters)
     came = lax.ppermute(lent, "dp", swap)
     adjoint, grad, other_act = own_part(fresh, own, act, other)

time: 89.2 us -> 85.2 us (0.955)
  blocking collectives: 56.7 us -> 51.7 us
    all_to_all x2, blocking collectives: 34.2 us -> 29.2 us  [exchange(): return lax.all_to_all(a, axis, 0, 0, axis_index_groups=groups)]
where the time goes in v5:
time: 85.2 us; the launch traced here: 84.8 us
  blocking collectives  51.7 us (61%)
  starting transfers between devices  17.3 us (20%)
  Pallas kernels  10.9 us (13%)
  local copies, waits for them, and re-layouts  3.05 us (4%)
  waiting for transfers between devices  1.13 us (1%)
    all_to_all x2, blocking collectives, exchange(): return lax.all_to_all(a, axis, 0, 0, axis_index_groups=groups)  29.2 us
    all_to_all x1, blocking collectives, per_device(): shares = lax.all_to_all(other_part(came, other_act, grad), 'dp', 0, 0)  22.5 us
    ppermute x1, starting transfers between devices, per_device(): other = lax.ppermute(lent, 'dp', swap)  8.75 us
    ppermute x1, starting transfers between devices, per_device(): came = lax.ppermute(lent, 'dp', swap)  7.24 us
    pallas_call x1, Pallas kernels, per_device(): fresh, own, lent, act = correct(groups, packs, top, guess, states, filters)  4.17 us
    pallas_call x1, Pallas kernels, per_device(): top, pack = fine(above, ending, guess[0], kept, filters, matrix)  2.32 us
    unnamed x10, local copies, waits for them, and re-layouts  2.02 us
  transfers between devices with their start and end apart: 3, of which 1 were waited for; matrix products, arithmetic and copies ran while one was open for 0% of the time, Pallas kernels for 2%

profile of v5, /device:TPU:1, one launch (start us, length us, event | category | flops | bytes accessed | tf_op | source)
XLA Modules:
  0.0 84.8 jit_solution(5309983496910460478)
XLA Ops:
  0.6 0.0 copy-start.2
  0.6 1.0 %slice_bitcast_fusion.guess_ref = bf16[128,1024]{1,0:T(8,128)(2,1)S(1)} fusion(bf16[2,1,128,1024]{3,2,1,0:T(8,128)(2,1)} %param.6), kind=kLoop, calls=%fused_computation | loop fusion | bytes 524288 | tf_op jit(solution)/shard_map/squeeze | solution.py:337
  1.7 1.3 %collective-permute-start = (bf16[128,1024]{1,0:T(8,128)(2,1)S(1)}, bf16[128,1024]{1,0:T(8,128)(2,1)S(1)}, u32[]{:S(2)}, u32[]{:S(2)}) collective-permute-start(bf16[128,1024]{1,0:T(8,128)(2,1)S(1)} %slice_bitcast_fusion.guess_ref), channel_id=1, source_target_pairs={{16,0},{32,16},{48,32},{64,48},{80,64},{96,80},{112,96},{128,112},... | collective-permute-start | bytes 786440 | tf_op jit(solution)/shard_map/ppermute | solution.py:337
  3.0 0.0 copy-done.2
  3.0 0.0 copy-start
  3.0 1.1 %copy-done = bf16[2,128,1152]{2,1,0:T(8,128)(2,1)S(1)} copy-done((bf16[2,128,1152]{2,1,0:T(8,128)(2,1)S(1)}, bf16[2,128,1152]{2,1,0:T(8,128)(2,1)}, u32[]{:S(2)}) %copy-start) | copy-done | bytes 589848
  4.0 0.0 copy-start.3
  4.0 0.9 %copy-done.3 = bf16[1,128,1024]{2,1,0:T(8,128)(2,1)S(1)} copy-done((bf16[1,128,1024]{2,1,0:T(8,128)(2,1)S(1)}, bf16[1,128,1024]{2,1,0:T(8,128)(2,1)}, u32[]{:S(2)}) %copy-start.3) | copy-done | bytes 262168
  5.0 0.0 copy-start.1
  5.0 0.2 shard_map.59
  5.2 8.7 %collective-permute-start.1 = (bf16[128,1024]{1,0:T(8,128)(2,1)S(1)}, bf16[128,1024]{1,0:T(8,128)(2,1)S(1)}, u32[]{:S(2)}, u32[]{:S(2)}) collective-permute-start(bf16[128,1024]{1,0:T(8,128)(2,1)S(1)} %get-tuple-element.17), channel_id=1, source_target_pairs={{1,0},{0,1},{3,2},{2,3},{5,4},{4,5},{7,6},{6,7},{9,8},{8,9},{11,10... | collective-permute-start | bytes 786440 | tf_op jit(solution)/shard_map/ppermute | solution.py:340
  14.0 0.0 collective-permute-done.above_ref
  14.0 1.1 %collective-permute-done.1.other_ref = bf16[128,1024]{1,0:T(8,128)(2,1)S(1)} collective-permute-done((bf16[128,1024]{1,0:T(8,128)(2,1)S(1)}, bf16[128,1024]{1,0:T(8,128)(2,1)S(1)}, u32[]{:S(2)}, u32[]{:S(2)}) %collective-permute-start.1) | collective-permute-done | bytes 262176 | tf_op jit(solution)/shard_map/ppermute | solution.py:340
  15.1 0.0 copy-done.1
  15.1 2.3 %shard_map.60 = (bf16[128,1024]{1,0:T(8,128)(2,1)S(1)}, bf16[8,128,384]{2,1,0:T(8,128)(2,1)S(1)}) custom-call(bf16[128,1024]{1,0:T(8,128)(2,1)S(1)} %collective-permute-done.above_ref, bf16[128,1024]{1,0:T(8,128)(2,1)S(1)} %get-tuple-element.19.terminal_ref, bf16[128,1024]{1,0:T(8,128)(2,1)S(1)} %slice_bitcast_fusion.guess_ref, ...), custom_call_target="tpu_custom_call" | custom-call | flops 1000000000 | bytes 1048576 | tf_op jit(solution)/shard_map/pallas_call | solution.py:342
  17.5 14.2 %all_to_all.15.packs_ref.packs_hbm = bf16[8,128,384]{2,1,0:T(8,128)(2,1)S(1)} all-to-all(bf16[8,128,384]{2,1,0:T(8,128)(2,1)S(1)} %get-tuple-element.22), channel_id=1, replica_groups={{0,16,32,48,64,80,96,112},{128,144,160,176,192,208,224,240},{256,272,28..., dimensions={0} | all-to-all | bytes 1572864 | tf_op jit(solution)/shard_map/all_to_all | solution.py:335
  31.7 0.8 shard_map.61
  32.5 0.0 copy-start.4
  32.5 15.0 %all_to_all.16.groups_ref = bf16[4,128,384]{2,1,0:T(8,128)(2,1)S(1)} all-to-all(bf16[4,128,384]{2,1,0:T(8,128)(2,1)S(1)} %shard_map.61), channel_id=1, replica_groups={{0,128,256,384},{16,144,272,400},{32,160,288,416},{48,176,304,432},{64,..., dimensions={0} | all-to-all | bytes 786432 | tf_op jit(solution)/shard_map/all_to_all | solution.py:335
  47.5 0.0 copy-done.4
  47.5 4.2 %shard_map.62 = (bf16[2,128,1024]{2,1,0:T(8,128)(2,1)S(1)}, bf16[128,1024]{1,0:T(8,128)(2,1)S(1)}, bf16[128,1024]{1,0:T(8,128)(2,1)S(1)}, bf16[128,1024]{1,0:T(8,128)(2,1)S(1)}) custom-call(bf16[4,128,384]{2,1,0:T(8,128)(2,1)S(1)} %all_to_all.16.groups_ref, bf16[8,128,384]{2,1,0:T(8,128)(2,1)S(1)} %all_to_all.15.packs_ref.packs_hbm, ...), custom_call_target="tpu_custom_call" | custom-call | flops 1000000000 | bytes 1048576 | tf_op jit(solution)/shard_map/pallas_call | solution.py:345
  51.7 7.2 %collective-permute-start.2 = (bf16[128,1024]{1,0:T(8,128)(2,1)S(1)}, bf16[128,1024]{1,0:T(8,128)(2,1)S(1)}, u32[]{:S(2)}, u32[]{:S(2)}) collective-permute-start(bf16[128,1024]{1,0:T(8,128)(2,1)S(1)} %get-tuple-element.29), channel_id=1, source_target_pairs={{1,0},{0,1},{3,2},{2,3},{5,4},{4,5},{7,6},{6,7},{9,8},{8,9},{11,10... | collective-permute-start | bytes 786440 | tf_op jit(solution)/shard_map/ppermute | solution.py:346
  58.9 1.5 %shard_map.63 = (bf16[2,128,1024]{2,1,0:T(8,128)(2,1)}, f32[128,1152]{1,0:T(8,128)S(1)}, bf16[128,1024]{1,0:T(8,128)(2,1)S(1)}) custom-call(bf16[2,128,1024]{2,1,0:T(8,128)(2,1)S(1)} %get-tuple-element.24.adjoint_ref, bf16[128,1024]{1,0:T(8,128)(2,1)S(1)} %get-tuple-element.25.own_ref, bf16[128,1024]{1,0:T(8,128)(2,1)S(1)} %get-tuple-element.26.act_ref, ...), custom_call_target="tpu_custom_call" | custom-call | flops 1000000000 | bytes 1048576 | tf_op jit(solution)/shard_map/pallas_call | solution.py:347
  60.5 0.0 collective-permute-done.2.came_ref
  60.5 1.1 %shard_map.64 = bf16[16,8,1152]{2,1,0:T(8,128)(2,1)S(1)} custom-call(bf16[128,1024]{1,0:T(8,128)(2,1)S(1)} %collective-permute-done.2.came_ref, bf16[128,1024]{1,0:T(8,128)(2,1)S(1)} %get-tuple-element.30.other_act_ref, f32[128,1152]{1,0:T(8,128)S(1)} %get-tuple-element.31.grad_ref), custom_call_target="tpu_custom_call" | custom-call | flops 1000000000 | bytes 1048576 | tf_op jit(solution)/shard_map/pallas_call | solution.py:348
  61.6 22.5 %all_to_all.17.came_ref = bf16[16,8,1152]{2,1,0:T(8,128)(2,1)S(1)} all-to-all(bf16[16,8,1152]{2,1,0:T(8,128)(2,1)S(1)} %shard_map.64), channel_id=1, replica_groups=mesh['layer'=32,'dp'=16] {'dp'}, dimensions={0} | all-to-all | bytes 589824 | tf_op jit(solution)/shard_map/all_to_all | solution.py:348
  84.2 0.7 shard_map.65
Async XLA Ops:
  0.6 2.3 %copy-start.2 = (bf16[2,1,128,1024]{3,2,1,0:T(8,128)(2,1)S(1)}, bf16[2,1,128,1024]{3,2,1,0:T(8,128)(2,1)}, u32[]{:S(2)}) copy-start(bf16[2,1,128,1024]{3,2,1,0:T(8,128)(2,1)} %param.4) | copy-start | bytes 1572868
  1.7 12.3 %collective-permute-start = (bf16[128,1024]{1,0:T(8,128)(2,1)S(1)}, bf16[128,1024]{1,0:T(8,128)(2,1)S(1)}, u32[]{:S(2)}, u32[]{:S(2)}) collective-permute-start(bf16[128,1024]{1,0:T(8,128)(2,1)S(1)} %slice_bitcast_fusion.guess_ref), channel_id=1, source_target_pairs={{16,0},{32,16},{48,32},{64,48},{80,64},{96,80},{112,96},{128,112},... | collective-permute-start | bytes 786440 | tf_op jit(solution)/shard_map/ppermute | solution.py:337
  3.0 1.1 %copy-start = (bf16[2,128,1152]{2,1,0:T(8,128)(2,1)S(1)}, bf16[2,128,1152]{2,1,0:T(8,128)(2,1)}, u32[]{:S(2)}) copy-start(bf16[2,128,1152]{2,1,0:T(8,128)(2,1)} %filters_hbm.1) | copy-start | bytes 1769476
  4.0 0.9 %copy-start.3 = (bf16[1,128,1024]{2,1,0:T(8,128)(2,1)S(1)}, bf16[1,128,1024]{2,1,0:T(8,128)(2,1)}, u32[]{:S(2)}) copy-start(bf16[1,128,1024]{2,1,0:T(8,128)(2,1)} %param.7) | copy-start | bytes 786436
  5.0 10.1 %copy-start.1 = (bf16[2,128,1152]{2,1,0:T(8,128)(2,1)S(1)}, bf16[2,128,1152]{2,1,0:T(8,128)(2,1)}, u32[]{:S(2)}) copy-start(bf16[2,128,1152]{2,1,0:T(8,128)(2,1)} %filters_hbm.1) | copy-start | bytes 1769476
  5.2 9.9 %collective-permute-start.1 = (bf16[128,1024]{1,0:T(8,128)(2,1)S(1)}, bf16[128,1024]{1,0:T(8,128)(2,1)S(1)}, u32[]{:S(2)}, u32[]{:S(2)}) collective-permute-start(bf16[128,1024]{1,0:T(8,128)(2,1)S(1)} %get-tuple-element.17), channel_id=1, source_target_pairs={{1,0},{0,1},{3,2},{2,3},{5,4},{4,5},{7,6},{6,7},{9,8},{8,9},{11,10... | collective-permute-start | bytes 786440 | tf_op jit(solution)/shard_map/ppermute | solution.py:340
  32.5 15.0 %copy-start.4 = (bf16[2,1,128,1024]{3,2,1,0:T(8,128)(2,1)S(1)}, bf16[2,1,128,1024]{3,2,1,0:T(8,128)(2,1)}, u32[]{:S(2)}) copy-start(bf16[2,1,128,1024]{3,2,1,0:T(8,128)(2,1)} %param.6) | copy-start | bytes 1572868
  51.7 8.8 %collective-permute-start.2 = (bf16[128,1024]{1,0:T(8,128)(2,1)S(1)}, bf16[128,1024]{1,0:T(8,128)(2,1)S(1)}, u32[]{:S(2)}, u32[]{:S(2)}) collective-permute-start(bf16[128,1024]{1,0:T(8,128)(2,1)S(1)} %get-tuple-element.29), channel_id=1, source_target_pairs={{1,0},{0,1},{3,2},{2,3},{5,4},{4,5},{7,6},{6,7},{9,8},{8,9},{11,10... | collective-permute-start | bytes 786440 | tf_op jit(solution)/shard_map/ppermute | solution.py:346

commit v6 on v5

--- a/solution.py
+++ b/solution.py
@@ -1,11 +1,10 @@
-import functools
-
 import jax
 import jax.numpy as jnp
 from jax import lax
 from jax.experimental import pallas as pl
 from jax.experimental.pallas import tpu as pltpu
 from jax.sharding import PartitionSpec as P
+
 
 STEP = 0.0625
 KEEP = 1.0 - STEP
@@ -62,11 +61,6 @@
     return (square == cell).astype(F32).astype(BF)
 
 
-def identity():
-    row = lax.broadcasted_iota(jnp.int32, (CH, CH), 0)
-    return jnp.where(row == lax.broadcasted_iota(jnp.int32, (CH, CH), 1), 1.0, 0.0)
-
-
 def rounded(part):
     row = lax.broadcasted_iota(jnp.int32, (CH, CH), 0).astype(F32)
     col = lax.broadcasted_iota(jnp.int32, (CH, CH), 1).astype(F32)
@@ -94,19 +88,23 @@
     return STEP * (1.0 - act * act)
 
 
-def prep_kernel(filters_ref, terminal_ref, states_ref, matrix_ref, ending_ref, kept_ref, lent_ref):
+def matrix_kernel(filters_ref, matrix_ref):
     total = filters_ref[0, :, 0:CH].astype(F32)
     for t in range(1, TAPS):
         total += filters_ref[0, :, t * CH : (t + 1) * CH].astype(F32)
     total *= STEP
-    matrix_ref[...] = rounded((2.0 * KEEP) * total + dot(total, total, EXACT))
+    part = rounded((2.0 * KEEP) * total + dot(total, total, EXACT))
+    for j in range(GROUP):
+        matrix_ref[j] = part
+
+
+def prep_kernel(terminal_ref, states_ref, ending_ref, kept_ref):
     ending_ref[...] = terminal_ref[...]
     kept_ref[...] = states_ref[...]
-    lent_ref[...] = states_ref[lax.axis_index("dp") % 2]
 
 
 def fine_kernel(
-    above_ref, terminal_ref, guess_ref, states_ref, filters_ref, matrix_ref, top_ref, pack_ref, stack_ref
+    above_ref, terminal_ref, guess_ref, states_ref, filters_ref, top_ref, pack_ref, stack_ref
 ):
     last = lax.axis_index("layer") == GROUP * GROUPS - 1
     top = jnp.where(last, terminal_ref[...].astype(F32), above_ref[...].astype(F32))
@@ -120,10 +118,8 @@
     high, low = split(residual)
     pool = jnp.where(pool_matrix(), 0.25, 0.0).astype(BF)
     coarse = (dot(high, pool) + dot(low, pool)).astype(BF)
-    matrix = matrix_ref[...]
     for j in range(GROUP):
-        pack_ref[j, :, :CELLS] = coarse
-        pack_ref[j, :, CELLS:] = matrix
+        pack_ref[j] = coarse
 
 
 def paired(scale, fields, parts):
@@ -133,10 +129,10 @@
     return scale * scale, joint, mixed
 
 
-def group_kernel(packs_ref, pack_ref):
+def group_kernel(coarse_ref, part_ref, pack_ref):
     scale = KEEP**2
-    coarse = [packs_ref[j, :, :CELLS] for j in range(GROUP)]
-    part = [packs_ref[j, :, CELLS:] for j in range(GROUP)]
+    coarse = [coarse_ref[j] for j in range(GROUP)]
+    part = [part_ref[j] for j in range(GROUP)]
     fields, parts = [], []
     for j in range(0, GROUP, 2):
         fields.append(coarse[j].astype(F32) + scale * coarse[j + 1].astype(F32) + dot(part[j], coarse[j + 1]))
@@ -170,10 +166,10 @@
     return applied(pairs[0], pairs[1][0])
 
 
-def suffix_maps(packs_ref, first, last):
+def suffix_maps(coarse_ref, part_ref, first, last):
     scale = KEEP**2
-    coarse = {j: packs_ref[j, :, :CELLS] for j in range(first, last + 1)}
-    part = {j: packs_ref[j, :, CELLS:] for j in range(first, last + 1)}
+    coarse = {j: coarse_ref[j] for j in range(first, last + 1)}
+    part = {j: part_ref[j] for j in range(first, last + 1)}
     field, hold, crossed = coarse[last].astype(F32), scale, part[last].astype(F32)
     maps = {last: (field, hold, crossed)}
     for j in range(last - 1, first - 1, -1):
@@ -191,28 +187,15 @@
 
 
 def correct_kernel(
-    groups_ref, packs_hbm, top_hbm, guess_hbm, states_hbm, filters_hbm,
+    groups_ref, coarse_ref, part_ref, top_ref, guess_ref, states_ref, filters_ref,
     adjoint_ref, own_ref, lent_ref, act_ref,
-    packs_ref, top_ref, guess_ref, states_ref, filters_ref, stack_ref, next_scr, act_scr, sems,
+    stack_ref, next_scr, act_scr,
 ):
-    copies = [
-        pltpu.make_async_copy(source, target, sems.at[i])
-        for i, (source, target) in enumerate((
-            (packs_hbm, packs_ref),
-            (top_hbm, top_ref),
-            (states_hbm, states_ref),
-            (guess_hbm.at[0], guess_ref),
-            (filters_hbm.at[1], filters_ref),
-        ))
-    ]
-    for copy in copies:
-        copy.start()
     layer = lax.axis_index("layer")
     core = lax.axis_index("dp") % 2
     place, at = layer % GROUP, layer // GROUP
-    copies[0].wait()
     half = GROUP // 2
-    low, high = suffix_maps(packs_ref, 0, half - 1), suffix_maps(packs_ref, half, GROUP - 1)
+    low, high = suffix_maps(coarse_ref, part_ref, 0, half - 1), suffix_maps(coarse_ref, part_ref, half, GROUP - 1)
     nil = (jnp.zeros((CH, CELLS), F32), 1.0, jnp.zeros((CH, CH), F32))
     low_own = picked(low, nil, place)
     low_upper = picked({j - 1: low[j] for j in range(1, half)}, nil, place)
@@ -226,22 +209,19 @@
         high_part, low_part = split(applied(near, applied(beyond, far)))
         return dot(high_part, spread) + dot(low_part, spread)
 
-    copies[1].wait()
     top = (top_ref[...].astype(F32) + widened(low_upper, high_upper)).astype(BF)
     write_stack(top, stack_ref)
-    copies[2].wait()
-    copies[3].wait()
-    copies[4].wait()
     act = tanh_of(states_ref[1])
-    below = KEEP * top.astype(F32) + slope_of(act) * dot(filters_ref[...], stack_ref[...])
+    below = KEEP * top.astype(F32) + slope_of(act) * dot(filters_ref[1], stack_ref[...])
     below = below.astype(BF)
     next_scr[1] = top
     next_scr[0] = below
     act_scr[1] = act.astype(BF)
     act_scr[0] = tanh_of(states_ref[0]).astype(BF)
-    adjoint_ref[0] = (guess_ref[...].astype(F32) + widened(low_own, high_own)).astype(BF)
+    adjoint_ref[0] = (guess_ref[0].astype(F32) + widened(low_own, high_own)).astype(BF)
     adjoint_ref[1] = below
-    lent_ref[...] = next_scr[core]
+    lent_ref[0] = next_scr[core]
+    lent_ref[1] = act_scr[core]
     own_ref[...] = next_scr[1 - core]
     act_ref[...] = act_scr[1 - core]
 
@@ -252,16 +232,15 @@
     return STEP * lax.dot_general(act, stack_ref[...], contract, preferred_element_type=F32)
 
 
-def own_kernel(adjoint_ref, own_ref, act_ref, other_ref, out_hbm, grad_ref, other_act_ref, stack_ref, sem):
+def own_kernel(adjoint_ref, own_ref, act_ref, out_hbm, grad_ref, stack_ref, sem):
     copy = pltpu.make_async_copy(adjoint_ref, out_hbm, sem)
     copy.start()
-    other_act_ref[...] = tanh_of(other_ref[...]).astype(BF)
     grad_ref[...] = gradient_of(act_ref[...], own_ref[...], stack_ref)
     copy.wait()
 
 
-def other_kernel(came_ref, other_act_ref, grad_ref, share_ref, stack_ref):
-    grad = grad_ref[...] + gradient_of(other_act_ref[...], came_ref[...], stack_ref)
+def other_kernel(came_ref, grad_ref, share_ref, stack_ref):
+    grad = grad_ref[...] + gradient_of(came_ref[1], came_ref[0], stack_ref)
     share_ref[...] = grad.reshape(2 * ZS, 8, TAPS * CH).astype(BF)
 
 
@@ -292,41 +271,35 @@
 FIELD = (CH, PIX)
 STACK = pltpu.VMEM((TAPS * CH, PIX), BF)
 ANY = pl.BlockSpec(memory_space=pl.ANY)
-prep = call(prep_kernel, [((CH, CH), BF), (FIELD, BF), ((2,) + FIELD, BF), (FIELD, BF)])
-fine = call(fine_kernel, [(FIELD, BF), ((GROUP, CH, WIDTH), BF)], [STACK], 10**9, 16)
+matrix_of = call(matrix_kernel, [((GROUP, CH, CH), BF)])
+prep = call(prep_kernel, [(FIELD, BF), ((2,) + FIELD, BF)])
+fine = call(fine_kernel, [(FIELD, BF), ((GROUP, CH, CELLS), BF)], [STACK], 10**9, 16)
 group_of = call(group_kernel, [((GROUPS, CH, WIDTH), BF)])
 correct = call(
     correct_kernel,
-    [((2,) + FIELD, BF), (FIELD, BF), (FIELD, BF), (FIELD, BF)],
+    [((2,) + FIELD, BF), (FIELD, BF), ((2,) + FIELD, BF), (FIELD, BF)],
     [
-        pltpu.VMEM((GROUP, CH, WIDTH), BF),
-        pltpu.VMEM(FIELD, BF),
-        pltpu.VMEM(FIELD, BF),
-        pltpu.VMEM((2,) + FIELD, BF),
-        pltpu.VMEM((CH, TAPS * CH), BF),
         STACK,
         pltpu.VMEM((2,) + FIELD, BF),
         pltpu.VMEM((2,) + FIELD, BF),
-        pltpu.SemaphoreType.DMA((5,)),
     ],
     10**9,
-    20,
-    [VMEM] + [ANY] * 5,
+    16,
 )
 own_part = call(
     own_kernel,
-    [((2,) + FIELD, BF), ((CH, TAPS * CH), F32), (FIELD, BF)],
+    [((2,) + FIELD, BF), ((CH, TAPS * CH), F32)],
     [STACK, pltpu.SemaphoreType.DMA(())],
     10**9,
     12,
-    [VMEM] * 4,
-    [ANY, VMEM, VMEM],
+    [VMEM] * 3,
+    [ANY, VMEM],
 )
 other_part = call(other_kernel, [((2 * ZS, 8, TAPS * CH), BF)], [STACK], 10**9, 12)
 total_of = call(total_kernel, [((2, 8, TAPS * CH), F32)])
 
 
-def per_device(states, filters, guess, terminal):
+def iterate(states, filters, guess, terminal):
     states, guess, terminal = states[:, 0], guess[:, 0], terminal[0]
     near_groups = [[k * GROUP + j for j in range(GROUP)] for k in range(GROUPS)]
     far_groups = [[k * GROUP + j for k in range(GROUPS)] for j in range(GROUP)]
@@ -335,23 +308,23 @@
         return lax.all_to_all(a, axis, 0, 0, axis_index_groups=groups)
 
     above = lax.ppermute(guess[0], "layer", [(i + 1, i) for i in range(GROUP * GROUPS - 1)])
-    matrix, ending, kept, lent = prep(filters, terminal, states)
+    matrix = matrix_of(filters)
+    parts = exchange(matrix, "layer", near_groups)
+    ending, kept = prep(terminal, states)
     swap = [(i ^ 1, i) for i in range(2 * ZS)]
-    other = lax.ppermute(lent, "dp", swap)
-    above, other = lax.optimization_barrier((above, other))
-    top, pack = fine(above, ending, guess[0], kept, filters, matrix)
-    packs = exchange(pack, "layer", near_groups)
-    groups = exchange(group_of(packs), "layer", far_groups)
-    fresh, own, lent, act = correct(groups, packs, top, guess, states, filters)
+    top, pack = fine(above, ending, guess[0], kept, filters)
+    coarses = exchange(pack, "layer", near_groups)
+    groups = exchange(group_of(coarses, parts), "layer", far_groups)
+    fresh, own, lent, act = correct(groups, coarses, parts, top, guess, states, filters)
     came = lax.ppermute(lent, "dp", swap)
-    adjoint, grad, other_act = own_part(fresh, own, act, other)
-    shares = lax.all_to_all(other_part(came, other_act, grad), "dp", 0, 0)
+    adjoint, grad = own_part(fresh, own, act)
+    shares = lax.all_to_all(other_part(came, grad), "dp", 0, 0)
     return adjoint[:, None], total_of(shares)
 
 
 def solution(mesh):
     return jax.shard_map(
-        per_device,
+        iterate,
         mesh=mesh,
         in_specs=(
             P("layer", "dp", None, None),

time: 85.2 us -> 87 us (1.021)
  waiting for transfers between devices: 1.13 us -> 5.89 us
  starting transfers between devices: 17.3 us -> 14.3 us
  blocking collectives: 51.7 us -> 53.7 us
  local copies, waits for them, and re-layouts: 3.05 us -> 1.1 us
    ppermute x3 -> x2, starting transfers between devices: 17.3 us -> 8.35 us  [the longest x1 6.92 us: iterate(): came = lax.ppermute(lent, 'dp', swap)]
    all_to_all x0 -> x1, starting transfers between devices: none -> 5.98 us  [exchange(): return lax.all_to_all(a, axis, 0, 0, axis_index_groups=groups)]
    ppermute x3 -> x2, waiting for transfers between devices: 1.13 us -> 5.89 us  [the longest x1 5.74 us: iterate(): lax.ppermute(guess[0], 'layer', [(i + 1, i) for i in range(GROUP * GROUPS...]
    all_to_all x2, blocking collectives: 29.2 us -> 31 us  [exchange(): return lax.all_to_all(a, axis, 0, 0, axis_index_groups=groups)]
    squeeze x1, local copies, waits for them, and re-layouts: 1.03 us -> 0.02 us  [iterate(): guess[0]]
    unnamed x10, local copies, waits for them, and re-layouts: 2.02 us -> 1.08 us
    pallas_call x7 -> x8, Pallas kernels: 10.9 us -> 10.8 us  [the longest x1 3.51 us: iterate(): correct(groups, coarses, parts, top, guess, states, filters)]
  transfers between devices with their start and end apart: 3 -> 3, of which waited for: 1 -> 2; matrix products, arithmetic and copies ran while one was open for 0% -> 0% of each run, Pallas kernels for 2% -> 4%
where the time goes in v6:
time: 87 us; the launch traced here: 86.6 us
  blocking collectives  53.7 us (62%)
  starting transfers between devices  14.3 us (16%)
  Pallas kernels  10.8 us (12%)
  waiting for transfers between devices  5.89 us (7%)
  local copies, waits for them, and re-layouts  1.1 us (1%)
    all_to_all x2, blocking collectives, exchange(): return lax.all_to_all(a, axis, 0, 0, axis_index_groups=groups)  31 us
    all_to_all x1, blocking collectives, iterate(): shares = lax.all_to_all(other_part(came, grad), 'dp', 0, 0)  22.8 us
    ppermute x1, starting transfers between devices, iterate(): came = lax.ppermute(lent, 'dp', swap)  6.92 us
    all_to_all x1, starting transfers between devices, exchange(): return lax.all_to_all(a, axis, 0, 0, axis_index_groups=groups)  5.98 us
    ppermute x1, waiting for transfers between devices, iterate(): lax.ppermute(guess[0], 'layer', [(i + 1, i) for i in range(GROUP * GROUPS...  5.74 us
    pallas_call x1, Pallas kernels, iterate(): correct(groups, coarses, parts, top, guess, states, filters)  3.51 us
    pallas_call x1, Pallas kernels, iterate(): top, pack = fine(above, ending, guess[0], kept, filters)  2.32 us
  transfers between devices with their start and end apart: 3, of which 2 were waited for; matrix products, arithmetic and copies ran while one was open for 0% of the time, Pallas kernels for 4%

profile of v6, /device:TPU:1, one launch (start us, length us, event | category | flops | bytes accessed | tf_op | source)
XLA Modules:
  0.0 86.6 jit_solution(15016310292233250464)
XLA Ops:
  0.6 0.0 copy-start
  0.6 1.1 %copy-done = bf16[2,128,1152]{2,1,0:T(8,128)(2,1)S(1)} copy-done((bf16[2,128,1152]{2,1,0:T(8,128)(2,1)S(1)}, bf16[2,128,1152]{2,1,0:T(8,128)(2,1)}, u32[]{:S(2)}) %copy-start) | copy-done | bytes 589848
  1.7 0.0 copy-start.4
  1.7 0.9 %shard_map.61 = bf16[8,128,128]{2,1,0:T(8,128)(2,1)} custom-call(bf16[2,128,1152]{2,1,0:T(8,128)(2,1)S(1)} %copy-done), custom_call_target="tpu_custom_call" | custom-call | flops 1000000 | bytes 1048576 | tf_op jit(solution)/shard_map/pallas_call | solution.py:311
  2.6 0.0 copy-start.2
  2.6 0.0 copy-start.3
  2.6 6.0 %all-to-all-start.1 = ((bf16[8,128,128]{2,1,0:T(8,128)(2,1)}), bf16[8,128,128]{2,1,0:T(8,128)(2,1)S(1)}, u32[]{:S(2)}, u32[]{:S(2)}) async-start(bf16[8,128,128]{2,1,0:T(8,128)(2,1)} %shard_map.61), calls=%async_computation.1 | async-start | bytes 524288 | tf_op jit(solution)/shard_map/all_to_all | solution.py:308
  8.6 0.0 copy-done.4
  8.6 0.0 copy-start.1
  8.7 1.4 %collective-permute-start = (bf16[128,1024]{1,0:T(8,128)(2,1)S(1)}, bf16[128,1024]{1,0:T(8,128)(2,1)S(1)}, u32[]{:S(2)}, u32[]{:S(2)}) collective-permute-start(bf16[128,1024]{1,0:T(8,128)(2,1)S(1)} %slice_bitcast_fusion.guess_ref), channel_id=1, source_target_pairs={{16,0},{32,16},{48,32},{64,48},{80,64},{96,80},{112,96},{128,112},... | collective-permute-start | bytes 786440 | tf_op jit(solution)/shard_map/ppermute | solution.py:310
  10.1 0.0 copy-done.2
  10.1 0.0 copy-done.3
  10.1 0.1 shard_map.59
  10.2 5.7 %collective-permute-done.above_ref = bf16[128,1024]{1,0:T(8,128)(2,1)S(1)} collective-permute-done((bf16[128,1024]{1,0:T(8,128)(2,1)S(1)}, bf16[128,1024]{1,0:T(8,128)(2,1)S(1)}, u32[]{:S(2)}, u32[]{:S(2)}) %collective-permute-start) | collective-permute-done | bytes 262176 | tf_op jit(solution)/shard_map/ppermute | solution.py:310
  15.9 0.0 copy-done.1
  15.9 2.3 %shard_map.60 = (bf16[128,1024]{1,0:T(8,128)(2,1)S(1)}, bf16[8,128,256]{2,1,0:T(8,128)(2,1)S(1)}) custom-call(bf16[128,1024]{1,0:T(8,128)(2,1)S(1)} %collective-permute-done.above_ref, bf16[128,1024]{1,0:T(8,128)(2,1)S(1)} %get-tuple-element.12.terminal_ref, bf16[128,1024]{1,0:T(8,128)(2,1)S(1)} %slice_bitcast_fusion.guess_ref, ...), custom_call_target="tpu_custom_call" | custom-call | flops 1000000000 | bytes 1048576 | tf_op jit(solution)/shard_map/pallas_call | solution.py:315
  18.2 0.0 all-to-all-done.1.part_ref
  18.3 14.9 %all_to_all.20.coarse_ref = bf16[8,128,256]{2,1,0:T(8,128)(2,1)S(1)} all-to-all(bf16[8,128,256]{2,1,0:T(8,128)(2,1)S(1)} %get-tuple-element.14), channel_id=1, replica_groups={{0,16,32,48,64,80,96,112},{128,144,160,176,192,208,224,240},{256,272,28..., dimensions={0} | all-to-all | bytes 1048576 | tf_op jit(solution)/shard_map/all_to_all | solution.py:308
  33.2 0.8 shard_map.62
  34.0 16.0 %all_to_all.21.groups_ref = bf16[4,128,384]{2,1,0:T(8,128)(2,1)S(1)} all-to-all(bf16[4,128,384]{2,1,0:T(8,128)(2,1)S(1)} %shard_map.62), channel_id=1, replica_groups={{0,128,256,384},{16,144,272,400},{32,160,288,416},{48,176,304,432},{64,..., dimensions={0} | all-to-all | bytes 786432 | tf_op jit(solution)/shard_map/all_to_all | solution.py:308
  50.0 3.5 %shard_map.63 = (bf16[2,128,1024]{2,1,0:T(8,128)(2,1)S(1)}, bf16[128,1024]{1,0:T(8,128)(2,1)S(1)}, bf16[2,128,1024]{2,1,0:T(8,128)(2,1)S(1)}, bf16[128,1024]{1,0:T(8,128)(2,1)S(1)}) custom-call(bf16[4,128,384]{2,1,0:T(8,128)(2,1)S(1)} %all_to_all.21.groups_ref, bf16[8,128,256]{2,1,0:T(8,128)(2,1)S(1)} %all_to_all.20.coarse_ref, ...), custom_call_target="tpu_custom_call" | custom-call | flops 1000000000 | bytes 1048576 | tf_op jit(solution)/shard_map/pallas_call | solution.py:318
  53.5 6.9 %collective-permute-start.1 = (bf16[2,128,1024]{2,1,0:T(8,128)(2,1)S(1)}, bf16[2,128,1024]{2,1,0:T(8,128)(2,1)S(1)}, u32[]{:S(2)}, u32[]{:S(2)}) collective-permute-start(bf16[2,128,1024]{2,1,0:T(8,128)(2,1)S(1)} %get-tuple-element.20), channel_id=1, source_target_pairs={{1,0},{0,1},{3,2},{2,3},{5,4},{4,5},{7,6},{6,7},{9,8},{8,9},{11,10... | collective-permute-start | bytes 1572872 | tf_op jit(solution)/shard_map/ppermute | solution.py:319
  60.5 1.4 %shard_map.64 = (bf16[2,128,1024]{2,1,0:T(8,128)(2,1)}, f32[128,1152]{1,0:T(8,128)S(1)}) custom-call(bf16[2,128,1024]{2,1,0:T(8,128)(2,1)S(1)} %get-tuple-element.16.adjoint_ref, bf16[128,1024]{1,0:T(8,128)(2,1)S(1)} %get-tuple-element.17.own_ref, bf16[128,1024]{1,0:T(8,128)(2,1)S(1)} %get-tuple-element.18.act_ref), custom_call_target="tpu_custom_call" | custom-call | flops 1000000000 | bytes 1048576 | tf_op jit(solution)/shard_map/pallas_call | solution.py:320
  61.8 0.1 collective-permute-done.1.came_ref
  62.0 1.1 %shard_map.65 = bf16[16,8,1152]{2,1,0:T(8,128)(2,1)S(1)} custom-call(bf16[2,128,1024]{2,1,0:T(8,128)(2,1)S(1)} %collective-permute-done.1.came_ref, f32[128,1152]{1,0:T(8,128)S(1)} %get-tuple-element.21.grad_ref), custom_call_target="tpu_custom_call" | custom-call | flops 1000000000 | bytes 1048576 | tf_op jit(solution)/shard_map/pallas_call | solution.py:321
  63.1 22.8 %all_to_all.22.came_ref = bf16[16,8,1152]{2,1,0:T(8,128)(2,1)S(1)} all-to-all(bf16[16,8,1152]{2,1,0:T(8,128)(2,1)S(1)} %shard_map.65), channel_id=1, replica_groups=mesh['layer'=32,'dp'=16] {'dp'}, dimensions={0} | all-to-all | bytes 589824 | tf_op jit(solution)/shard_map/all_to_all | solution.py:321
  85.9 0.7 shard_map.66
  (1 shorter events, 0.0 us)
Async XLA Ops:
  0.6 1.1 %copy-start = (bf16[2,128,1152]{2,1,0:T(8,128)(2,1)S(1)}, bf16[2,128,1152]{2,1,0:T(8,128)(2,1)}, u32[]{:S(2)}) copy-start(bf16[2,128,1152]{2,1,0:T(8,128)(2,1)} %filters_ref.5) | copy-start | bytes 1769476
  1.7 6.9 %copy-start.4 = (bf16[2,1,128,1024]{3,2,1,0:T(8,128)(2,1)S(1)}, bf16[2,1,128,1024]{3,2,1,0:T(8,128)(2,1)}, u32[]{:S(2)}) copy-start(bf16[2,1,128,1024]{3,2,1,0:T(8,128)(2,1)} %param.6) | copy-start | bytes 1572868
  2.6 7.5 %copy-start.2 = (bf16[2,1,128,1024]{3,2,1,0:T(8,128)(2,1)S(1)}, bf16[2,1,128,1024]{3,2,1,0:T(8,128)(2,1)}, u32[]{:S(2)}) copy-start(bf16[2,1,128,1024]{3,2,1,0:T(8,128)(2,1)} %param.4) | copy-start | bytes 1572868
  2.6 7.5 %copy-start.3 = (bf16[1,128,1024]{2,1,0:T(8,128)(2,1)S(1)}, bf16[1,128,1024]{2,1,0:T(8,128)(2,1)}, u32[]{:S(2)}) copy-start(bf16[1,128,1024]{2,1,0:T(8,128)(2,1)} %param.7) | copy-start | bytes 786436
  2.6 15.6 %all-to-all-start.1 = ((bf16[8,128,128]{2,1,0:T(8,128)(2,1)}), bf16[8,128,128]{2,1,0:T(8,128)(2,1)S(1)}, u32[]{:S(2)}, u32[]{:S(2)}) async-start(bf16[8,128,128]{2,1,0:T(8,128)(2,1)} %shard_map.61), calls=%async_computation.1 | async-start | bytes 524288 | tf_op jit(solution)/shard_map/all_to_all | solution.py:308
  8.6 7.3 %copy-start.1 = (bf16[2,128,1152]{2,1,0:T(8,128)(2,1)S(1)}, bf16[2,128,1152]{2,1,0:T(8,128)(2,1)}, u32[]{:S(2)}) copy-start(bf16[2,128,1152]{2,1,0:T(8,128)(2,1)} %filters_ref.5) | copy-start | bytes 1769476
  8.7 7.2 %collective-permute-start = (bf16[128,1024]{1,0:T(8,128)(2,1)S(1)}, bf16[128,1024]{1,0:T(8,128)(2,1)S(1)}, u32[]{:S(2)}, u32[]{:S(2)}) collective-permute-start(bf16[128,1024]{1,0:T(8,128)(2,1)S(1)} %slice_bitcast_fusion.guess_ref), channel_id=1, source_target_pairs={{16,0},{32,16},{48,32},{64,48},{80,64},{96,80},{112,96},{128,112},... | collective-permute-start | bytes 786440 | tf_op jit(solution)/shard_map/ppermute | solution.py:310
  53.5 8.4 %collective-permute-start.1 = (bf16[2,128,1024]{2,1,0:T(8,128)(2,1)S(1)}, bf16[2,128,1024]{2,1,0:T(8,128)(2,1)S(1)}, u32[]{:S(2)}, u32[]{:S(2)}) collective-permute-start(bf16[2,128,1024]{2,1,0:T(8,128)(2,1)S(1)} %get-tuple-element.20), channel_id=1, source_target_pairs={{1,0},{0,1},{3,2},{2,3},{5,4},{4,5},{7,6},{6,7},{9,8},{8,9},{11,10... | collective-permute-start | bytes 1572872 | tf_op jit(solution)/shard_map/ppermute | solution.py:319
